TPU v7x, 256 devices: a whole 4x4x8 slice. The times are simulated.
256 devices in a mesh: ctx: 16 (over y, x), exp: 8 (over z), dp: 2 (over core).
Axes of the slice: x: 4, y: 4, z: 8, core: 2. Of those that a mesh axis runs over, the one named last changes fastest.
Arguments:
- residual: bfloat16 [2048, 4096], P('ctx', ('exp', 'dp')), may hold values from -6 to 6
- ssm_values: bfloat16 [2048, 4096], P('ctx', ('exp', 'dp')), may hold values from -6 to 6
- ssm_keys: bfloat16 [2048, 64], P('ctx'), may hold values from -6 to 6
- ssm_queries: bfloat16 [2048, 64], P('ctx'), may hold values from -0.015625 to 0.015625
- log_decay: float32 [2048, 64], P('ctx', ('exp', 'dp')), may hold values from -1 to 0, as said below
- expert_ids: int32 [2048, 2], P('ctx'), may hold values from 0 to 7, all different within a row; in each aligned block of 128 rows (0 to 127, 128 to 255, ...) at most 40 rows name the same one
- gate_probs: float32 [2048, 2], P('ctx'), may hold values from 0.2 to 1
- norm_gain: float32 [4096], P(('exp', 'dp')), may hold values from 0.5 to 1.5
- w_gate: bfloat16 [8, 4096, 8192], P('exp', None, ('ctx', 'dp')), may hold values from -0.09375 to 0.09375
- w_up: bfloat16 [8, 4096, 8192], P('exp', None, ('ctx', 'dp')), may hold values from -0.09375 to 0.09375
- w_down: bfloat16 [8, 4096, 8192], P('exp', None, ('ctx', 'dp')), may hold values from -0.0625 to 0.0625
- out_grad: bfloat16 [2048, 4096], P('ctx', ('exp', 'dp')), may hold values from -6 to 6
Outputs:
- grad_residual: bfloat16 [2048, 4096], P('ctx', ('exp', 'dp'))
- grad_values: bfloat16 [2048, 4096], P('ctx', ('exp', 'dp'))
- grad_keys: float32 [2048, 64], P('ctx')
- grad_queries: float32 [2048, 64], P('ctx')
- grad_decay: float32 [2048, 64], P('ctx', ('exp', 'dp'))
- grad_probs: float32 [2048, 2], P('ctx')
- grad_gain: float32 [4096], P(('exp', 'dp'))
- w_gate_grad: bfloat16 [8, 4096, 8192], P('exp', None, ('ctx', 'dp'))
- w_up_grad: bfloat16 [8, 4096, 8192], P('exp', None, ('ctx', 'dp'))
- w_down_grad: bfloat16 [8, 4096, 8192], P('exp', None, ('ctx', 'dp'))
Inputs may be any that keep to these rules, and one draw needn't show every extreme that they name: `expert_ids`: each token names two different experts; among the 128 tokens of one index of ctx (aligned blocks) no expert is named more than 40 times, a bound that some block reaches. `log_decay`: negative everywhere.
All inputs are finite; a program needn't handle non-finite values.
Results may differ from a plain program's by a relative error of at most 0.028.
Values may be sent and summed in bfloat16 or wider, within the bound.
No kernel may reach another device: no remote copies, remote signals or barrier semaphores. Data moves between devices by JAX's collectives and lax.ppermute only.
A program may use at most 128 MiB of HBM per device.

v0:
```python
import jax
import jax.numpy as jnp
from jax import lax
from jax.sharding import PartitionSpec as P

HIGH = lax.Precision.HIGHEST
EPS = 1e-05


def entering(x, axis, join, neutral):
    place = lax.axis_index(axis)
    gathered = jax.tree.map(
        lambda a, kind: lax.all_gather(a.astype(kind), axis), x, (jnp.bfloat16, jnp.bfloat16)
    )
    state = jax.tree.map(lambda a, e: jnp.zeros_like(a) + jnp.asarray(e, a.dtype), x, neutral)

    def entering_one(step, state):
        return join(
            state,
            jax.tree.map(
                lambda a, own: lax.dynamic_index_in_dim(a, step, 0, False).astype(own.dtype),
                gathered,
                x,
            ),
        )

    return lax.fori_loop(0, place, entering_one, state)


def carried_in(x, axis, join, neutral):
    count = lax.axis_size(axis)
    place = lax.axis_index(axis)
    ahead = count - 1 - place
    gathered = jax.tree.map(
        lambda a, kind: lax.all_gather(a.astype(kind), axis),
        x,
        jax.tree.map(lambda a: jnp.bfloat16 if a.dtype == jnp.float32 else a.dtype, x),
    )
    state = jax.tree.map(lambda a, e: jnp.zeros_like(a) + jnp.asarray(e, a.dtype), x, neutral)

    def carried_one(step, state):
        source = count - 1 - step
        return join(
            state,
            jax.tree.map(
                lambda a, own: lax.dynamic_index_in_dim(a, source, 0, False).astype(own.dtype),
                gathered,
                x,
            ),
        )

    return lax.fori_loop(0, ahead, carried_one, state)


def block_state(values, key_rows, log_decay):
    cumulative = jnp.cumsum(log_decay, axis=0)
    total_log = cumulative[-1]
    tail_decay = jnp.exp(total_log[None, :] - cumulative)
    weighted = tail_decay[:, :, None] * values
    state_local = jnp.einsum("shp,sn->hpn", weighted, key_rows, precision=HIGH)
    return (jnp.exp(total_log), state_local)


def block_output(values, key_rows, queries, log_decay, state_in):
    cumulative = jnp.cumsum(log_decay, axis=0)
    length = values.shape[0]
    row_index = lax.broadcasted_iota(jnp.int32, (length, length), 0)
    col_index = lax.broadcasted_iota(jnp.int32, (length, length), 1)
    causal = (row_index >= col_index)[None]
    cum_heads = cumulative.T
    log_gap = jnp.where(causal, cum_heads[:, :, None] - cum_heads[:, None, :], 0.0)
    decay_mat = jnp.where(causal, jnp.exp(log_gap), 0.0)
    scores = jnp.dot(queries, key_rows.T, precision=HIGH)
    inner_part = jnp.einsum("hts,shp->thp", decay_mat * scores[None], values, precision=HIGH)
    carried = jnp.einsum("tn,hpn->thp", queries, state_in, precision=HIGH)
    return inner_part + jnp.exp(cumulative)[:, :, None] * carried


def silu_parts(gate_act):
    sigmoid_val = jax.nn.sigmoid(gate_act)
    return (gate_act * sigmoid_val, sigmoid_val * (1.0 + gate_act * (1.0 - sigmoid_val)))


def route_slots(token_ids, expert_count):
    owners = token_ids.reshape(-1)
    onehot = (owners[:, None] == jnp.arange(expert_count, dtype=jnp.int32)[None, :]).astype(
        jnp.int32
    )
    rank_before = jnp.cumsum(onehot, axis=0) - onehot
    return (owners, jnp.sum(rank_before * onehot, axis=1))


def combine_states(earlier_part, later_part):
    return (
        earlier_part[0] * later_part[0],
        later_part[0][:, None, None] * earlier_part[1] + later_part[1],
    )


def arrange_rows(gathered, ctx_count, dp_count):
    capacity = gathered.shape[1]
    exp_count = gathered.shape[2]
    feat = gathered.shape[3]
    shaped = gathered.reshape(ctx_count, dp_count, capacity, exp_count, feat)
    return shaped.transpose(0, 2, 3, 1, 4).reshape(
        ctx_count * capacity, exp_count * dp_count * feat
    )


def arrange_sums(full_term, ctx_count, dp_count, exp_count, capacity):
    feat = full_term.shape[1] // (exp_count * dp_count)
    shaped = full_term.reshape(ctx_count, capacity, exp_count, dp_count, feat)
    return shaped.transpose(0, 3, 1, 2, 4).reshape(
        ctx_count * dp_count * capacity, exp_count * feat
    )


def per_device(
    residual,
    ssm_values,
    ssm_keys,
    ssm_queries,
    log_decay,
    expert_ids,
    gate_probs,
    norm_gain,
    w_gate,
    w_up,
    w_down,
    out_grad,
):
    tokens = residual.shape[0]
    feat = residual.shape[1]
    heads_here = log_decay.shape[1]
    head_size = feat // heads_here
    model_width = w_gate.shape[1]
    ctx_count = lax.axis_size("ctx")
    exp_count = lax.axis_size("exp")
    dp_count = lax.axis_size("dp")
    expert_count = w_gate.shape[0] * exp_count
    capacity = 5 * tokens // (2 * expert_count)
    block_vals = ssm_values.astype(jnp.float32).reshape(tokens, heads_here, head_size)
    block_keys = ssm_keys.astype(jnp.float32)
    block_queries = ssm_queries.astype(jnp.float32)
    (decay_total, state_local), state_pull = jax.vjp(block_state, block_vals, block_keys, log_decay)
    neutral = (jnp.ones_like(decay_total), jnp.zeros_like(state_local))
    state_in = entering((decay_total, state_local), "ctx", combine_states, neutral)[1]
    mixer_out, output_pull = jax.vjp(
        block_output, block_vals, block_keys, block_queries, log_decay, state_in
    )
    hidden = (residual.astype(jnp.float32) + mixer_out.reshape(tokens, feat)).astype(jnp.bfloat16)
    hidden_f = hidden.astype(jnp.float32)
    square_sum = lax.psum(jnp.sum(hidden_f * hidden_f, axis=1), ("exp", "dp"))
    inv_rms = lax.rsqrt(square_sum / model_width + EPS)[:, None]
    normed = (hidden_f * inv_rms * norm_gain[None, :]).astype(jnp.bfloat16)
    owners, slot_index = route_slots(expert_ids, expert_count)
    pair_rows = jnp.repeat(normed, 2, axis=0)
    dout_rows = jnp.repeat(out_grad, 2, axis=0)
    pair_prob = gate_probs.reshape(-1)
    pair_cot = (pair_prob[:, None] * dout_rows.astype(jnp.float32)).astype(jnp.bfloat16)
    empty = jnp.zeros((expert_count, capacity, feat), jnp.bfloat16)
    send_rows = empty.at[owners, slot_index].set(pair_rows).reshape(expert_count, capacity, 1, feat)
    got_rows = lax.all_to_all(send_rows, "exp", split_axis=0, concat_axis=2, tiled=True)
    all_rows = lax.all_gather(got_rows, ("ctx", "dp"), axis=0, tiled=True)
    rows_flat = arrange_rows(all_rows, ctx_count, dp_count)
    act_gate = jnp.dot(rows_flat, w_gate[0], preferred_element_type=jnp.float32)
    act_up = jnp.dot(rows_flat, w_up[0], preferred_element_type=jnp.float32)
    swish_val, swish_slope = silu_parts(act_gate)
    hidden_act = (swish_val * act_up).astype(jnp.bfloat16)
    full_out = lax.dot_general(
        hidden_act, w_down[0], (((1,), (1,)), ((), ())), preferred_element_type=jnp.float32
    )
    out_total = lax.psum_scatter(
        arrange_sums(full_out, ctx_count, dp_count, exp_count, capacity).astype(jnp.bfloat16),
        ("ctx", "dp"),
        scatter_dimension=0,
        tiled=True,
    )
    expert_out = out_total.reshape(1, capacity, exp_count, feat)
    back_out = lax.all_to_all(expert_out, "exp", split_axis=2, concat_axis=0, tiled=True).reshape(
        expert_count, capacity, feat
    )
    out_pairs = back_out[owners, slot_index]
    probs_part = jnp.einsum(
        "kd,kd->k", out_pairs, dout_rows, preferred_element_type=jnp.float32
    ).reshape(tokens, 2)
    grad_probs = lax.psum(probs_part, ("exp", "dp"))
    send_cot = empty.at[owners, slot_index].set(pair_cot).reshape(expert_count, capacity, 1, feat)
    got_cot = lax.all_to_all(send_cot, "exp", split_axis=0, concat_axis=2, tiled=True)
    all_cot = lax.all_gather(got_cot, ("ctx", "dp"), axis=0, tiled=True)
    cot_flat = arrange_rows(all_cot, ctx_count, dp_count)
    grad_act = jnp.dot(cot_flat, w_down[0], preferred_element_type=jnp.float32)
    grad_gate = (grad_act * act_up * swish_slope).astype(jnp.bfloat16)
    grad_up = (grad_act * swish_val).astype(jnp.bfloat16)
    full_back = lax.dot_general(
        grad_gate, w_gate[0], (((1,), (1,)), ((), ())), preferred_element_type=jnp.float32
    ) + lax.dot_general(
        grad_up, w_up[0], (((1,), (1,)), ((), ())), preferred_element_type=jnp.float32
    )
    back_total = lax.psum_scatter(
        arrange_sums(full_back, ctx_count, dp_count, exp_count, capacity).astype(jnp.bfloat16),
        ("ctx", "dp"),
        scatter_dimension=0,
        tiled=True,
    )
    pair_back = back_total.reshape(1, capacity, exp_count, feat)
    back_in = lax.all_to_all(pair_back, "exp", split_axis=2, concat_axis=0, tiled=True).reshape(
        expert_count, capacity, feat
    )
    grad_normed = (
        back_in[owners, slot_index].astype(jnp.float32).reshape(tokens, 2, feat).sum(axis=1)
    )
    w_gate_grad = jnp.dot(rows_flat.T, grad_gate, preferred_element_type=jnp.float32).astype(
        jnp.bfloat16
    )[None]
    w_up_grad = jnp.dot(rows_flat.T, grad_up, preferred_element_type=jnp.float32).astype(
        jnp.bfloat16
    )[None]
    w_down_grad = jnp.dot(cot_flat.T, hidden_act, preferred_element_type=jnp.float32).astype(
        jnp.bfloat16
    )[None]
    scaled = grad_normed * norm_gain[None, :]
    inner_sum = lax.psum(jnp.sum(hidden_f * scaled, axis=1), ("exp", "dp"))
    projection = (inner_sum / model_width)[:, None]
    grad_hidden = (
        out_grad.astype(jnp.float32) + inv_rms * scaled - hidden_f * inv_rms**3 * projection
    )
    gain_part = jnp.sum(grad_normed * hidden_f * inv_rms, axis=0)
    grad_gain = lax.psum(gain_part, "ctx")
    grad_mixer = grad_hidden.reshape(tokens, heads_here, head_size)
    vals_first, keys_first, queries_part, decay_first, carry_cot = output_pull(grad_mixer)
    grad_state = carried_in((decay_total, carry_cot), "ctx", combine_states, neutral)[1]
    grad_total = jnp.sum(grad_state * state_in, axis=(1, 2))
    vals_second, keys_second, decay_second = state_pull((grad_total, grad_state))
    grad_keys, grad_queries = (
        lax.psum((keys_first + keys_second).astype(jnp.bfloat16), ("exp", "dp")).astype(
            jnp.float32
        ),
        lax.psum(queries_part.astype(jnp.bfloat16), ("exp", "dp")).astype(jnp.float32),
    )
    grad_residual = grad_hidden.astype(jnp.bfloat16)
    grad_values = (vals_first + vals_second).reshape(tokens, feat).astype(jnp.bfloat16)
    grad_decay = decay_first + decay_second
    return (
        grad_residual,
        grad_values,
        grad_keys,
        grad_queries,
        grad_decay,
        grad_probs,
        grad_gain,
        w_gate_grad,
        w_up_grad,
        w_down_grad,
    )


def solution(mesh):
    return jax.shard_map(
        per_device,
        mesh=mesh,
        in_specs=(
            P("ctx", ("exp", "dp")),
            P("ctx", ("exp", "dp")),
            P("ctx", None),
            P("ctx", None),
            P("ctx", ("exp", "dp")),
            P("ctx", None),
            P("ctx", None),
            P(("exp", "dp")),
            P("exp", None, ("ctx", "dp")),
            P("exp", None, ("ctx", "dp")),
            P("exp", None, ("ctx", "dp")),
            P("ctx", ("exp", "dp")),
        ),
        out_specs=(
            P("ctx", ("exp", "dp")),
            P("ctx", ("exp", "dp")),
            P("ctx", None),
            P("ctx", None),
            P("ctx", ("exp", "dp")),
            P("ctx", None),
            P(("exp", "dp")),
            P("exp", None, ("ctx", "dp")),
            P("exp", None, ("ctx", "dp")),
            P("exp", None, ("ctx", "dp")),
        ),
        check_vma=False,
    )
```

profile of v0, /device:TPU:2, one launch (start us, length us, event | category | flops | bytes accessed | tf_op | source)
XLA Modules:
  0.0 650.8 jit_solution(5369685150378966095)
XLA Ops:
  11.6 13.2 %scatter_fusion = bf16[8,40,256]{2,1,0:T(8,128)(2,1)S(1)} fusion(bf16[8,40,256]{2,1,0:T(8,128)(2,1)S(1)} %broadcast_in_dim.73.clone.1, s32[256]{0:T(256)S(1)} %bitcast.193, bf16[256,256]{1,0:T(8,128)(2,1)S(1)} %fusion.19), kind=kCustom, calls=%fused_computation.2 | custom fusion | bytes 395264 | tf_op jit(solution)/shard_map/scatter | solution.py:188
  24.9 18.0 %all_to_all.66 = bf16[8,40,1,256]{3,1,2,0:T(8,128)(2,1)S(1)} all-to-all(bf16[8,40,1,256]{3,1,2,0:T(8,128)(2,1)S(1)} %bitcast.200), channel_id=1, replica_groups=mesh['ctx'=16,'exp'=8,'dp'=2] {'exp'}, dimensions={0} | all-to-all | bytes 327680 | tf_op jit(solution)/shard_map/all_to_all | solution.py:189
  44.6 20.7 %all-gather.4 = bf16[16,1,4]{2,1,0:T(2,128)(2,1)S(1)} all-gather(bf16[1,1,4]{2,1,0:T(2,128)(2,1)S(1)} %get-tuple-element.299), channel_id=1, replica_groups=mesh['ctx'=16,'exp'=8,'dp'=2] {'ctx'}, dimensions={0}, use_global_device_ids=true | all-gather | bytes 136 | tf_op jit(solution)/shard_map/all_gather | solution.py:13
  67.0 27.6 %all-gather = bf16[64,64,64]{2,1,0:T(8,128)(2,1)} all-gather(bf16[4,64,64]{2,1,0:T(8,128)(2,1)S(1)} %convolution_convert_fusion.4), channel_id=2, replica_groups=mesh['ctx'=16,'exp'=8,'dp'=2] {'ctx'}, dimensions={0}, use_global_device_ids=true | all-gather | bytes 557056 | tf_op jit(solution)/shard_map/all_gather | solution.py:13
  96.7 23.5 %psum.42 = f32[128]{0:T(128)S(1)} all-reduce(f32[128]{0:T(128)S(1)} %get-tuple-element.291), channel_id=1, replica_groups=mesh['ctx'=16,'exp'=8,'dp'=2] {'exp','dp'}, use_global_device_ids=true, to_apply=%region_4.5 | all-reduce | flops 128 | bytes 1024 | tf_op jit(solution)/shard_map/psum | solution.py:153
  121.1 13.2 %scatter_fusion.1 = bf16[8,40,256]{2,1,0:T(8,128)(2,1)S(1)} fusion(bf16[8,40,256]{2,1,0:T(8,128)(2,1)S(1)} %broadcast_in_dim.73.clone, s32[256]{0:T(256)S(1)} %bitcast.194, bf16[256,256]{1,0:T(8,128)(2,1)S(1)} %reshape.273), kind=kCustom, calls=%fused_computation.3 | custom fusion | bytes 395264 | tf_op jit(solution)/shard_map/scatter | solution.py:162
  134.3 12.5 %all_to_all.67 = bf16[8,40,1,256]{3,1,2,0:T(8,128)(2,1)S(1)} all-to-all(bf16[8,40,1,256]{3,1,2,0:T(8,128)(2,1)S(1)} %bitcast.199), channel_id=1, replica_groups=mesh['ctx'=16,'exp'=8,'dp'=2] {'exp'}, dimensions={0} | all-to-all | bytes 327680 | tf_op jit(solution)/shard_map/all_to_all | solution.py:163
  147.9 13.0 %copy.164 = bf16[16,40,8,2,256]{4,3,2,1,0:T(2,128)(2,1)} copy(bf16[16,40,8,2,256]{4,2,1,3,0:T(8,128)(2,1)} %bitcast.203) | data formatting | bytes 10485760 | tf_op jit(solution)/shard_map/transpose | solution.py:105
  160.9 10.0 %reshape.236 = bf16[640,4096]{1,0:T(8,128)(2,1)} reshape(bf16[16,40,8,2,256]{4,3,2,1,0:T(2,128)(2,1)} %copy.164) | data formatting | bytes 10485760 | tf_op jit(solution)/shard_map/reshape | solution.py:105
  170.9 35.7 %all-gather.10.cloned.1.call-done = bf16[32,40,8,1,256]{4,2,3,1,0:T(8,128)(2,1)} async-done(((bf16[1,40,8,1,256]{4,2,3,1,0:T(8,128)(2,1)}), bf16[32,40,8,1,256]{4,2,3,1,0:T(8,128)(2,1)}) %all-gather.10.cloned.1.call-update) | async-done | bytes 5242896 | tf_op jit(solution)/shard_map/all_gather | solution.py:164
  206.6 13.0 %copy.167 = bf16[16,40,8,2,256]{4,3,2,1,0:T(2,128)(2,1)} copy(bf16[16,40,8,2,256]{4,2,1,3,0:T(8,128)(2,1)} %bitcast.204) | data formatting | bytes 10485760 | tf_op jit(solution)/shard_map/transpose | solution.py:105
  219.6 9.6 %reshape.240 = bf16[640,4096]{1,0:T(8,128)(2,1)} reshape(bf16[16,40,8,2,256]{4,3,2,1,0:T(2,128)(2,1)} %copy.167) | data formatting | bytes 10485760 | tf_op jit(solution)/shard_map/reshape | solution.py:105
  253.6 9.6 %convert_element_type.165 = bf16[16,40,8,2,256]{4,3,2,1,0:T(2,128)(2,1)} reshape(bf16[640,4096]{1,0:T(8,128)(2,1)} %add_convert_fusion) | data formatting | bytes 10485760 | tf_op jit(solution)/shard_map/convert_element_type | solution.py:201
  272.3 5.9 fusion.2
  278.2 60.4 %reduce-scatter.5.cloned.1.call-done = bf16[40,2048]{1,0:T(8,128)(2,1)} async-done(((bf16[1280,2048]{1,0:T(8,128)(2,1)}), bf16[40,2048]{1,0:T(8,128)(2,1)}) %reduce-scatter.5.cloned.1.call-update) | async-done | bytes 163856 | tf_op jit(solution)/shard_map/reduce_scatter | solution.py:173
  340.2 7.0 %all-to-all-start.3 = ((bf16[1,40,8,256]{3,1,0,2:T(8,128)(2,1)}), bf16[1,40,8,256]{3,1,0,2:T(8,128)(2,1)S(1)}, u32[]{:S(2)}, u32[]{:S(2)}) async-start(bf16[1,40,8,256]{3,1,0,2:T(8,128)(2,1)} %copy.177), calls=%async_computation.5 | async-start | bytes 327680 | tf_op jit(solution)/shard_map/all_to_all | solution.py:180
  347.2 5.7 fusion
  352.9 81.3 %reduce-scatter.3.cloned.1.call-done = bf16[40,2048]{1,0:T(8,128)(2,1)} async-done(((bf16[1280,2048]{1,0:T(8,128)(2,1)}), bf16[40,2048]{1,0:T(8,128)(2,1)}) %reduce-scatter.3.cloned.1.call-update) | async-done | bytes 163856 | tf_op jit(solution)/shard_map/reduce_scatter | solution.py:200
  435.8 7.3 %all-to-all-start.2 = ((bf16[1,40,8,256]{3,1,0,2:T(8,128)(2,1)}), bf16[1,40,8,256]{3,1,0,2:T(8,128)(2,1)S(1)}, u32[]{:S(2)}, u32[]{:S(2)}) async-start(bf16[1,40,8,256]{3,1,0,2:T(8,128)(2,1)} %copy.169), calls=%async_computation.3 | async-start | bytes 327680 | tf_op jit(solution)/shard_map/all_to_all | solution.py:207
  454.8 46.5 %all-reduce.1 = (f32[128]{0:T(128)S(1)}, f32[128,2]{1,0:T(8,128)S(1)}) all-reduce(f32[128]{0:T(128)S(1)} %get-tuple-element.264, f32[128,2]{1,0:T(8,128)S(1)} %reshape.247), channel_id=1, replica_groups=mesh['ctx'=16,'exp'=8,'dp'=2] {'exp','dp'}, use_global_device_ids=true, to_apply=%region_13.14 | all-reduce | flops 384 | bytes 3072 | tf_op jit(solution)/shard_map/psum | solution.py:223
  502.7 25.0 %all-gather.3 = bf16[64,64,64]{2,1,0:T(8,128)(2,1)} all-gather(bf16[4,64,64]{2,1,0:T(8,128)(2,1)S(1)} %convolution_convert_fusion.3), channel_id=5, replica_groups=mesh['ctx'=16,'exp'=8,'dp'=2] {'ctx'}, dimensions={0}, use_global_device_ids=true | all-gather | bytes 557056 | tf_op jit(solution)/shard_map/all_gather | solution.py:35
  527.8 22.9 %while.27 = (s32[]{:T(128)}, f32[4,64,64]{2,1,0:T(8,128)S(1)}, s32[]{:T(128)}, bf16[16,4]{1,0:T(8,128)(2,1)}, bf16[16,4,64,64]{3,2,1,0:T(8,128)(2,1)}, /*index=5*/s32[]{:T(128)}, s32[]{:T(128)}, s32[]{:T(128)}, s32[]{:T(128)}) while((s32[]{:T(128)}, f32[4,64,64]{2,1,0:T(8,128)S(1)}, s32[]{:T(128)}, bf16[16,4]{1,0:T(8,128)(2,1)}, ...), condition=%wide.region_15.16_spmd, body=%wide.region_14.15_spmd.sunk | while | flops 49162 | bytes 164035 | solution.py:52
  551.1 39.5 %psum.47 = f32[256]{0:T(256)} all-reduce(f32[256]{0:T(256)S(1)} %get-tuple-element.263), channel_id=1, replica_groups=mesh['ctx'=16,'exp'=8,'dp'=2] {'ctx'}, use_global_device_ids=true, to_apply=%region_30.31 | all-reduce | flops 256 | bytes 2048 | tf_op jit(solution)/shard_map/psum | solution.py:229
  593.8 45.7 %all-reduce.2 = (bf16[128,64]{0,1:T(8,128)(2,1)S(1)}, bf16[128,64]{0,1:T(8,128)(2,1)S(1)}) all-reduce(bf16[128,64]{0,1:T(8,128)(2,1)S(1)} %fusion.16, bf16[128,64]{0,1:T(8,128)(2,1)S(1)} %fusion.17), channel_id=1, replica_groups=mesh['ctx'=16,'exp'=8,'dp'=2] {'exp','dp'}, use_global_device_ids=true, to_apply=%region_17.18 | all-reduce | flops 16384 | bytes 65536 | tf_op jit(solution)/shard_map/psum | solution.py:236
  (179 shorter events, 92.8 us)
Async XLA Ops:
  7.2 222.0 %copy-start = (bf16[1,4096,256]{2,1,0:T(8,128)(2,1)S(1)}, bf16[1,4096,256]{2,1,0:T(8,128)(2,1)}, u32[]{:S(2)}) copy-start(bf16[1,4096,256]{2,1,0:T(8,128)(2,1)} %param.26) | copy-start | bytes 6291460
  7.2 59.6 %copy-start.13 = (bf16[128,64]{0,1:T(8,128)(2,1)S(1)}, bf16[128,64]{0,1:T(8,128)(2,1)}, u32[]{:S(2)}) copy-start(bf16[128,64]{0,1:T(8,128)(2,1)} %param.18) | copy-start | bytes 49156
  7.2 87.4 %copy-start.12 = (bf16[128,64]{0,1:T(8,128)(2,1)S(1)}, bf16[128,64]{0,1:T(8,128)(2,1)}, u32[]{:S(2)}) copy-start(bf16[128,64]{0,1:T(8,128)(2,1)} %param.19) | copy-start | bytes 49156
  7.2 89.4 %copy-start.16 = (bf16[128,256]{1,0:T(8,128)(2,1)S(1)}, bf16[128,256]{1,0:T(8,128)(2,1)}, u32[]{:S(2)}) copy-start(bf16[128,256]{1,0:T(8,128)(2,1)} %param.16) | copy-start | bytes 196612
  7.2 113.6 %copy-start.17 = (f32[256]{0:T(256)S(1)}, f32[256]{0:T(256)}, u32[]{:S(2)}) copy-start(f32[256]{0:T(256)} %param.23) | copy-start | bytes 3076
  7.2 140.6 %all-gather.8.cloned.1.call-start = ((), (), s32[]{:S(2)}) async-start(), calls=%async_computation.8 | async-start | bytes 5406720 | tf_op jit(solution)/shard_map/all_gather | solution.py:190
  43.6 163.0 %all-gather.10.cloned.1.call-start = ((), (), s32[]{:S(2)}) async-start(), calls=%async_computation.9 | async-start | bytes 5406720 | tf_op jit(solution)/shard_map/all_gather | solution.py:164
  66.4 67.9 %copy-start.19 = (f32[4,128]{1,0:T(4,128)}, f32[4,128]{1,0:T(4,128)S(1)}, u32[]{:S(2)}) copy-start(f32[4,128]{1,0:T(4,128)S(1)} %copy.150) | copy-start | bytes 6148
  94.8 39.5 %copy-start.14 = (f32[128,128]{1,0:T(8,128)}, f32[128,128]{1,0:T(8,128)S(1)}, u32[]{:S(2)}) copy-start(f32[128,128]{1,0:T(8,128)S(1)} %fusion.65) | copy-start | bytes 196612
  95.8 38.5 %copy-start.18 = (bf16[16,4]{1,0:T(8,128)(2,1)}, bf16[16,4]{1,0:T(8,128)(2,1)S(1)}, u32[]{:S(2)}) copy-start(bf16[16,4]{1,0:T(8,128)(2,1)S(1)} %get-tuple-element.437) | copy-start | bytes 388
  147.5 191.0 %reduce-scatter.5.cloned.1.call-start = ((), (), s32[]{:S(2)}) async-start(), calls=%async_computation.7 | async-start | bytes 5406720 | tf_op jit(solution)/shard_map/reduce_scatter | solution.py:173
  229.2 4.2 copy-start.2
  229.2 4.7 copy-start.3
  238.0 3.9 copy-start.9
  246.6 187.6 %reduce-scatter.3.cloned.1.call-start = ((), (), s32[]{:S(2)}) async-start(), calls=%async_computation.6 | async-start | bytes 5406720 | tf_op jit(solution)/shard_map/reduce_scatter | solution.py:200
  248.2 1.6 copy-start.7
  340.2 95.7 %all-to-all-start.3 = ((bf16[1,40,8,256]{3,1,0,2:T(8,128)(2,1)}), bf16[1,40,8,256]{3,1,0,2:T(8,128)(2,1)S(1)}, u32[]{:S(2)}, u32[]{:S(2)}) async-start(bf16[1,40,8,256]{3,1,0,2:T(8,128)(2,1)} %copy.177), calls=%async_computation.5 | async-start | bytes 327680 | tf_op jit(solution)/shard_map/all_to_all | solution.py:180
  347.2 95.9 %copy-start.8 = (bf16[640,256]{1,0:T(8,128)(2,1)S(1)}, bf16[640,256]{1,0:T(8,128)(2,1)}, u32[]{:S(2)}) copy-start(bf16[640,256]{1,0:T(8,128)(2,1)} %get-tuple-element.297) | copy-start | bytes 983044
  435.8 16.7 %all-to-all-start.2 = ((bf16[1,40,8,256]{3,1,0,2:T(8,128)(2,1)}), bf16[1,40,8,256]{3,1,0,2:T(8,128)(2,1)S(1)}, u32[]{:S(2)}, u32[]{:S(2)}) async-start(bf16[1,40,8,256]{3,1,0,2:T(8,128)(2,1)} %copy.169), calls=%async_computation.3 | async-start | bytes 327680 | tf_op jit(solution)/shard_map/all_to_all | solution.py:207
  443.1 58.1 %copy-start.11 = (bf16[128,256]{1,0:T(8,128)(2,1)S(1)}, bf16[128,256]{1,0:T(8,128)(2,1)}, u32[]{:S(2)}) copy-start(bf16[128,256]{1,0:T(8,128)(2,1)} %param.27) | copy-start | bytes 196612
  443.2 58.1 %copy-start.21 = (f32[128]{0:T(128)S(1)}, f32[128]{0:T(128)}, u32[]{:S(2)}) copy-start(f32[128]{0:T(128)} %get-tuple-element.300) | copy-start | bytes 1540
  448.9 142.3 %copy-start.15 = (f32[128,128]{1,0:T(8,128)S(1)}, f32[128,128]{1,0:T(8,128)}, u32[]{:S(2)}) copy-start(f32[128,128]{1,0:T(8,128)} %copy-done.14) | copy-start | bytes 196612
  448.9 142.3 %copy-start.20 = (f32[4,128]{1,0:T(4,128)S(1)}, f32[4,128]{1,0:T(4,128)}, u32[]{:S(2)}) copy-start(f32[4,128]{1,0:T(4,128)} %copy-done.19) | copy-start | bytes 6148
  452.5 191.4 %copy-start.1 = (bf16[1,4096,256]{2,1,0:T(8,128)(2,1)S(1)}, bf16[1,4096,256]{2,1,0:T(8,128)(2,1)}, u32[]{:S(2)}) copy-start(bf16[1,4096,256]{2,1,0:T(8,128)(2,1)} %param.26) | copy-start | bytes 6291460
  (4 other events, 5.8 us)
Sparse Core Ops, SparseCore 0:
  43.7 49.1 all-gather.7
  147.6 58.9 all-gather.9
  246.7 91.7 reduce-scatter.4
  342.4 91.7 reduce-scatter.2
where the time goes:
time: 657 us; the launch traced here: 651 us
  blocking collectives  259 us (39%)
  waiting for transfers between devices  179 us (27%)
  local copies, waits for them, and re-layouts  116 us (18%)
  matrix products  35.9 us (5%)
  other arithmetic  30.4 us (5%)
  starting transfers between devices  15 us (2%)
  between operations  14.8 us (2%)
    reduce_scatter x1, waiting for transfers between devices, per_device(): lax.psum_scatter(arrange_sums(full_back, ctx_count, dp_count, exp_count,...  81.3 us
    reduce_scatter x1, waiting for transfers between devices, per_device(): lax.psum_scatter(arrange_sums(full_out, ctx_count, dp_count, exp_count, c...  60.4 us
    all_gather x2, blocking collectives, entering(): lax.all_gather(a.astype(kind), axis)  48.3 us
    psum x1, blocking collectives, per_device(): inner_sum = lax.psum(jnp.sum(hidden_f * scaled, axis=1), ('exp', 'dp'))  46.5 us
    psum x1, blocking collectives, per_device(): lax.psum((keys_first + keys_second).astype(jnp.bfloat16), ('exp', 'dp'))  45.7 us
    psum x1, blocking collectives, per_device(): grad_gain = lax.psum(gain_part, 'ctx')  39.5 us
    all_gather x1, waiting for transfers between devices, per_device(): all_rows = lax.all_gather(got_rows, ('ctx', 'dp'), axis=0, tiled=True)  35.7 us
    transpose x2, local copies, waits for them, and re-layouts, arrange_rows(): shaped.transpose(0, 2, 3, 1, 4)  26 us
  transfers between devices with their start and end apart: 6, of which 4 were waited for; matrix products, arithmetic and copies ran while one was open for 13% of the time, Pallas kernels for 0%

commit v1 on v0

v1 whole, which is shorter than its diff:
```python
import jax
import jax.numpy as jnp
from jax import lax
from jax.experimental import pallas as pl
from jax.experimental.pallas import tpu as pltpu
from jax.sharding import PartitionSpec as P

HIGH = lax.Precision.HIGHEST
EPS = 1e-05
F32 = jnp.float32
BF16 = jnp.bfloat16


def dot(a, b, dims=((1,), (0,)), precision=None):
    return lax.dot_general(a, b, (dims, ((), ())), precision=precision, preferred_element_type=F32)


def head_map(heads, width):
    size = width // heads
    return (
        lax.broadcasted_iota(jnp.int32, (heads, width), 1) // size
        == lax.broadcasted_iota(jnp.int32, (heads, width), 0)
    ).astype(F32)


def lower_mask(n):
    return lax.broadcasted_iota(jnp.int32, (n, n), 0) >= lax.broadcasted_iota(jnp.int32, (n, n), 1)


def block_state(values, key_rows, log_decay):
    tri = lower_mask(values.shape[0]).astype(F32)
    spread = head_map(log_decay.shape[1], values.shape[1])
    cumulative = dot(tri, log_decay, precision=HIGH)
    total_log = cumulative[-1:]
    tail = dot(jnp.exp(total_log - cumulative), spread, precision=HIGH)
    return total_log, dot(key_rows, tail * values, ((0,), (0,)), HIGH)


def block_output(values, key_rows, queries, log_decay, state_in):
    length, width = values.shape
    heads = log_decay.shape[1]
    size = width // heads
    causal = lower_mask(length)
    tri = causal.astype(F32)
    cumulative = dot(tri, log_decay, precision=HIGH)
    cum_heads = dot(log_decay, tri, ((0,), (1,)), HIGH)
    scores = dot(queries, key_rows, ((1,), (1,)), HIGH)
    parts = []
    for h in range(heads):
        log_gap = jnp.where(causal, cumulative[:, h : h + 1] - cum_heads[h : h + 1, :], 0.0)
        decay_mat = jnp.where(causal, jnp.exp(log_gap), 0.0)
        parts.append(dot(decay_mat * scores, values[:, h * size : (h + 1) * size], precision=HIGH))
    carried = dot(queries, state_in, precision=HIGH)
    growth = dot(jnp.exp(cumulative), head_map(heads, width), precision=HIGH)
    return jnp.concatenate(parts, axis=1) + growth * carried


def split_rows(x, parts):
    rows = []
    for _ in range(parts):
        head = lax.reduce_precision(x, 8, 7)
        rows.append(head.astype(BF16))
        x = x - head
    return rows


def pad_rows(rows, count, width):
    block = jnp.concatenate(rows, axis=0)
    return jnp.pad(block, ((0, count - block.shape[0]), (0, width - block.shape[1])))


def swap(x, axis):
    return lax.all_to_all(x, axis, 0, 0, tiled=True)


def to_all(x, axis):
    return swap(jnp.broadcast_to(x[None], (lax.axis_size(axis),) + x.shape), axis)


def flat_rows(block):
    shape = block.shape
    return block.astype(F32).reshape(shape[0] * shape[1], shape[2])


def open_kernel(core, rows_ref, gain_ref, wg_ref, wu_ref, ag_ref, au_ref, ss_ref):
    rows = flat_rows(rows_ref[...])
    scaled = (rows * gain_ref[...]).astype(BF16)

    @pl.when(pl.program_id(0) == 0)
    def _():
        ag_ref[...] = jnp.zeros_like(ag_ref)
        au_ref[...] = jnp.zeros_like(au_ref)
        ss_ref[...] = jnp.zeros_like(ss_ref)

    ag_ref[...] += dot(scaled, wg_ref[...])
    au_ref[...] += dot(scaled, wu_ref[...])
    ss_ref[...] += jnp.broadcast_to(jnp.sum(rows * rows, axis=1, keepdims=True), ss_ref.shape)


def close_kernel(
    core, rows_ref, gain_ref, wg_ref, wu_ref, ag_in, au_in, ss_in, ga_ref,
    hact_ref, dg_ref, du_ref, dgi_ref, dui_ref, sc_ref, ag_ref, au_ref, ss_ref,
):
    rows = flat_rows(rows_ref[...])
    scaled = (rows * gain_ref[...]).astype(BF16)

    @pl.when(pl.program_id(0) == 0)
    def _():
        ag_ref[...] = ag_in[...]
        au_ref[...] = au_in[...]
        ss_ref[...] = ss_in[...]

    ag_ref[...] += dot(scaled, wg_ref[...])
    au_ref[...] += dot(scaled, wu_ref[...])
    ss_ref[...] += jnp.broadcast_to(jnp.sum(rows * rows, axis=1, keepdims=True), ss_ref.shape)

    @pl.when(pl.program_id(0) == pl.num_programs(0) - 1)
    def _():
        width = 2 * pl.num_programs(0) * rows.shape[1]
        inv = lax.rsqrt(ss_ref[:, :1] / width + EPS)
        act_gate = inv * ag_ref[...]
        act_up = inv * au_ref[...]
        grad_act = ga_ref[...]
        sig = jax.nn.sigmoid(act_gate)
        swish = act_gate * sig
        slope = sig * (1.0 + act_gate * (1.0 - sig))
        hact = (swish * act_up).astype(BF16)
        dg32 = grad_act * act_up * slope
        du32 = grad_act * swish
        dg = dg32.astype(BF16)
        du = du32.astype(BF16)
        hact_ref[...] = hact
        dg_ref[...] = dg
        du_ref[...] = du
        dgi_ref[...] = (inv * dg32).astype(BF16)
        dui_ref[...] = (inv * du32).astype(BF16)
        probs = jnp.sum(hact.astype(F32) * grad_act, axis=1, keepdims=True)
        inner = jnp.sum(
            dg.astype(F32) * act_gate + du.astype(F32) * act_up, axis=1, keepdims=True
        )
        lane = lax.broadcasted_iota(jnp.int32, sc_ref.shape, 1)
        sc_ref[...] = jnp.where(
            lane == 0, probs, jnp.where(lane == 1, inner, jnp.where(lane == 2, inv, 0.0))
        )


def cot_kernel(cot_ref, wd_ref, ga_ref):
    total = dot(flat_rows(cot_ref[:, 0]).astype(BF16), wd_ref[0])
    total += dot(flat_rows(cot_ref[:, 1]).astype(BF16), wd_ref[1])

    @pl.when(pl.program_id(0) == 0)
    def _():
        ga_ref[...] = total

    @pl.when(pl.program_id(0) > 0)
    def _():
        ga_ref[...] += total


def back_term(dg_ref, du_ref, wg_ref, wu_ref):
    return dot(dg_ref[...], wg_ref[...], ((1,), (1,))) + dot(
        du_ref[...], wu_ref[...], ((1,), (1,))
    )


def back_kernel(core, dg_ref, du_ref, wg_ref, wu_ref, out_ref):
    term = back_term(dg_ref, du_ref, wg_ref, wu_ref)
    out_ref[...] = term.reshape(out_ref.shape).astype(BF16)


def back_add_kernel(core, dg_ref, du_ref, wg_ref, wu_ref, other_ref, sc_ref, out_ref):
    slots = other_ref.shape[1]
    step = pl.program_id(0)
    term = back_term(dg_ref, du_ref, wg_ref, wu_ref).astype(BF16).astype(F32)
    both = term.reshape(other_ref.shape) + other_ref[...].astype(F32)
    out_ref[:, pl.ds(pl.multiple_of(step * slots, 8), slots), :] = both.astype(BF16)

    @pl.when(step == 0)
    def _():
        out_ref[:, pl.num_programs(0) * slots :, :] = sc_ref[...]


def grads_kernel(
    core, own_ref, oth_ref, cot_ref, gown_ref, goth_ref, dgi_ref, dui_ref, hact_ref,
    gate_ref, up_ref, down_ref,
):
    here = core[0]
    first = ((0,), (0,))
    for rows_ref, gain_ref, place in ((own_ref, gown_ref, here), (oth_ref, goth_ref, 1 - here)):
        scaled = (flat_rows(rows_ref[...]) * gain_ref[...]).astype(BF16)
        gate_ref[place] = dot(scaled, dgi_ref[...], first).astype(BF16)
        up_ref[place] = dot(scaled, dui_ref[...], first).astype(BF16)
    for place in range(2):
        cot = flat_rows(cot_ref[:, place]).astype(BF16)
        down_ref[place] = dot(cot, hact_ref[...], first).astype(BF16)


def whole(shape):
    return pl.BlockSpec(shape, lambda e, *_: (0,) * len(shape))


def per_device(
    residual,
    ssm_values,
    ssm_keys,
    ssm_queries,
    log_decay,
    expert_ids,
    gate_probs,
    norm_gain,
    w_gate,
    w_up,
    w_down,
    out_grad,
):
    tokens, feat = residual.shape
    heads = log_decay.shape[1]
    model_width, units = w_gate.shape[1:]
    ctx_count = lax.axis_size("ctx")
    exp_count = lax.axis_size("exp")
    capacity = 5 * tokens // (2 * exp_count)
    rows_all = ctx_count * capacity
    ctx_here = lax.axis_index("ctx")
    core = lax.axis_index("dp").astype(jnp.int32).reshape(1)
    other_core = [(0, 1), (1, 0)]

    values = ssm_values.astype(F32)
    key_rows = ssm_keys.astype(F32)
    queries = ssm_queries.astype(F32)
    (total_log, state_local), state_pull = jax.vjp(block_state, values, key_rows, log_decay)
    state_rows = state_local.shape[0]
    payload = jnp.concatenate(
        [state_local.astype(BF16), pad_rows(split_rows(total_log, 3), 8, feat)], axis=0
    )
    got = to_all(payload, "ctx")
    logs = jnp.sum(got[:, state_rows : state_rows + 3, :heads].astype(F32), axis=1)
    source = lax.broadcasted_iota(jnp.int32, (ctx_count, ctx_count), 0)
    between = lax.broadcasted_iota(jnp.int32, (ctx_count, ctx_count), 1)
    spread = head_map(heads, feat)
    rank = jnp.arange(ctx_count, dtype=jnp.int32)[:, None]
    before = ((between > source) & (between < ctx_here)).astype(F32)
    after = ((between < source) & (between > ctx_here)).astype(F32)
    gap_before = jnp.sum(before[:, :, None] * logs[None], axis=1)
    gap_after = jnp.sum(after[:, :, None] * logs[None], axis=1)
    weight_before = dot(
        jnp.where(rank < ctx_here, jnp.exp(gap_before), 0.0), spread, precision=HIGH
    )
    weight_after = dot(jnp.where(rank > ctx_here, jnp.exp(gap_after), 0.0), spread, precision=HIGH)
    state_in = jnp.sum(weight_before[:, None, :] * got[:, :state_rows].astype(F32), axis=0)

    ids = expert_ids.T
    probs = gate_probs.T
    experts = jnp.arange(exp_count, dtype=jnp.int32)[:, None]
    named = [ids[k][None, :] == experts for k in range(2)]
    member = named[0] | named[1]
    strict = (~lower_mask(tokens)).astype(BF16)
    order = dot(member.astype(BF16), strict).astype(jnp.int32)
    slot = lax.broadcasted_iota(jnp.int32, (exp_count, capacity, tokens), 1)
    chosen = (order[:, None, :] == slot) & member[:, None, :]
    select = chosen.astype(BF16).reshape(exp_count * capacity, tokens)
    prob_of = jnp.where(named[0], probs[0][None, :], jnp.where(named[1], probs[1][None, :], 0.0))
    prob_rows = jnp.sum(jnp.where(chosen, prob_of[:, None, :], 0.0), axis=2)

    cot = (dot(select, out_grad).reshape(exp_count, capacity, feat) * prob_rows[:, :, None]).astype(
        BF16
    )
    gain_rows = pad_rows(split_rows(norm_gain[None, :], 3), 8, feat)
    got_cot = swap(
        jnp.concatenate(
            [cot, jnp.broadcast_to(gain_rows[None], (exp_count,) + gain_rows.shape)], axis=1
        ),
        "exp",
    )
    gain_own = jnp.sum(got_cot[:, capacity : capacity + 3].astype(F32), axis=1)[:, None, :]
    gain_oth = lax.ppermute(gain_own, "dp", other_core)
    all_cot = lax.all_gather(
        got_cot[:, :capacity].reshape(exp_count * capacity, feat), ("ctx", "dp"), axis=0
    ).reshape(ctx_count, 2, exp_count, capacity, feat)

    mixer_out, output_pull = jax.vjp(
        block_output, values, key_rows, queries, log_decay, state_in
    )
    hidden = (residual.astype(F32) + mixer_out).astype(BF16)
    hidden_f = hidden.astype(F32)
    got_rows = swap(
        dot(select, hidden).astype(BF16).reshape(exp_count, capacity, feat), "exp"
    )
    own = to_all(got_rows, "ctx")
    oth = lax.ppermute(own, "dp", other_core)

    gate4 = w_gate.reshape(exp_count, 2, feat, units)
    up4 = w_up.reshape(exp_count, 2, feat, units)
    down4 = w_down.reshape(exp_count, 2, feat, units)
    rows_spec = pl.BlockSpec((ctx_count, None, capacity, feat), lambda e, *_: (0, e, 0, 0))
    cot_spec = pl.BlockSpec((ctx_count, 2, None, capacity, feat), lambda e, *_: (0, 0, e, 0, 0))
    gain_spec = pl.BlockSpec((None, 1, feat), lambda e, *_: (e, 0, 0))
    w_own = pl.BlockSpec((None, None, feat, units), lambda e, s: (e, s[0], 0, 0))
    w_oth = pl.BlockSpec((None, None, feat, units), lambda e, s: (e, 1 - s[0], 0, 0))
    w_pair = pl.BlockSpec((None, 2, feat, units), lambda e, *_: (e, 0, 0, 0))
    acts = whole((rows_all, units))
    sums = whole((rows_all, 128))
    acts_f = jax.ShapeDtypeStruct((rows_all, units), F32)
    acts_b = jax.ShapeDtypeStruct((rows_all, units), BF16)
    sums_f = jax.ShapeDtypeStruct((rows_all, 128), F32)

    def grid_of(n_scalars, in_specs, out_specs, scratch=()):
        return pltpu.PrefetchScalarGridSpec(
            num_scalar_prefetch=n_scalars,
            grid=(exp_count,),
            in_specs=in_specs,
            out_specs=out_specs,
            scratch_shapes=list(scratch),
        )

    grad_act = pl.pallas_call(
        cot_kernel, grid_spec=grid_of(0, [cot_spec, w_pair], acts), out_shape=acts_f, name="cot"
    )(all_cot, down4)
    ag, au, ss = pl.pallas_call(
        open_kernel,
        grid_spec=grid_of(1, [rows_spec, gain_spec, w_own, w_own], [acts, acts, sums]),
        out_shape=[acts_f, acts_f, sums_f],
        name="open",
    )(core, own, gain_own, gate4, up4)
    hact, dg, du, dgi, dui, scal = pl.pallas_call(
        close_kernel,
        grid_spec=grid_of(
            1,
            [rows_spec, gain_spec, w_oth, w_oth, acts, acts, sums, acts],
            [acts] * 5 + [sums],
            [
                pltpu.VMEM((rows_all, units), F32),
                pltpu.VMEM((rows_all, units), F32),
                pltpu.VMEM((rows_all, 128), F32),
            ],
        ),
        out_shape=[acts_b] * 5 + [sums_f],
        name="close",
    )(core, oth, gain_oth, gate4, up4, ag, au, ss, grad_act)
    small = scal[:, :8]
    small = small + lax.ppermute(small, "dp", other_core)
    small = small.reshape(ctx_count, capacity, 8).transpose(0, 2, 1)[:, :3]
    small = jnp.concatenate(
        [small[:, :2], small[:, 2:] * (0.5 / ctx_count)], axis=1
    )
    small_rows = jnp.pad(
        jnp.concatenate(split_rows(small, 2), axis=1), ((0, 0), (0, 2), (0, feat - capacity))
    )
    back_oth = pl.pallas_call(
        back_kernel,
        grid_spec=grid_of(1, [acts, acts, w_oth, w_oth], rows_spec),
        out_shape=jax.ShapeDtypeStruct((ctx_count, exp_count, capacity, feat), BF16),
        name="back_oth",
    )(core, dg, du, gate4, up4)
    back_got = lax.ppermute(back_oth, "dp", other_core)
    back_rows = exp_count * capacity
    back = pl.pallas_call(
        back_add_kernel,
        grid_spec=grid_of(
            1,
            [acts, acts, w_own, w_own, rows_spec, whole((ctx_count, 8, feat))],
            whole((ctx_count, back_rows + 8, feat)),
        ),
        out_shape=jax.ShapeDtypeStruct((ctx_count, back_rows + 8, feat), BF16),
        name="back_own",
    )(core, dg, du, gate4, up4, back_got, small_rows)
    gate_grad, up_grad, down_grad = pl.pallas_call(
        grads_kernel,
        grid_spec=grid_of(
            1,
            [rows_spec, rows_spec, cot_spec, gain_spec, gain_spec, acts, acts, acts],
            [w_pair] * 3,
        ),
        out_shape=[jax.ShapeDtypeStruct(gate4.shape, BF16)] * 3,
        name="grads",
    )(core, own, oth, all_cot, gain_own, gain_oth, dgi, dui, hact)

    summed = jnp.sum(swap(back, "ctx").astype(F32), axis=0)
    small = summed[back_rows : back_rows + 3] + summed[back_rows + 3 : back_rows + 6]
    small_rows = pad_rows(split_rows(small, 2), 8, feat)
    got_back = swap(
        jnp.concatenate(
            [
                summed[:back_rows].astype(BF16).reshape(exp_count, capacity, feat),
                jnp.broadcast_to(small_rows[None], (exp_count,) + small_rows.shape),
            ],
            axis=1,
        ),
        "exp",
    )
    grad_normed = dot(select, got_back[:, :capacity].reshape(back_rows, feat), ((0,), (0,)))
    small = got_back[:, capacity:, :capacity].astype(F32)
    small = small[:, :3] + small[:, 3:6]
    per_expert = lax.dot_general(
        small,
        chosen.astype(F32),
        (((2,), (1,)), ((0,), (0,))),
        precision=HIGH,
        preferred_element_type=F32,
    )
    grad_probs = jnp.stack(
        [
            jnp.sum(jnp.where(named[k], per_expert[:, 0], 0.0), axis=0) / probs[k]
            for k in range(2)
        ],
        axis=1,
    )
    inner = jnp.sum(per_expert[:, 1], axis=0)[:, None]
    inv_rms = (jnp.sum(per_expert[:, 2], axis=0) * 0.5)[:, None]
    scaled = grad_normed * norm_gain[None, :]
    grad_hidden = (
        out_grad.astype(F32)
        + inv_rms * scaled
        - hidden_f * (inv_rms * inv_rms * inner / model_width)
    )
    gain_part = jnp.sum(grad_normed * hidden_f * inv_rms, axis=0, keepdims=True)

    vals_first, keys_first, queries_part, decay_first, carry_cot = output_pull(grad_hidden)
    got_carry = to_all(
        jnp.concatenate(
            [carry_cot.astype(BF16), pad_rows(split_rows(gain_part, 3), 8, feat)], axis=0
        ),
        "ctx",
    )
    grad_state = jnp.sum(weight_after[:, None, :] * got_carry[:, :state_rows].astype(F32), axis=0)
    grad_gain = jnp.sum(got_carry[:, state_rows : state_rows + 3].astype(F32), axis=(0, 1))
    grad_total = dot(
        jnp.sum(grad_state * state_in, axis=0, keepdims=True), spread, ((1,), (1,)), HIGH
    ) * jnp.exp(total_log)
    vals_second, keys_second, decay_second = state_pull((grad_total, grad_state))
    both = jnp.concatenate([keys_first + keys_second, queries_part], axis=1).astype(BF16)
    both = (both.astype(F32) + lax.ppermute(both, "dp", other_core).astype(F32)).astype(BF16)
    both = jnp.sum(to_all(both, "exp").astype(F32), axis=0)
    return (
        grad_hidden.astype(BF16),
        (vals_first + vals_second).astype(BF16),
        both[:, :state_rows],
        both[:, state_rows:],
        decay_first + decay_second,
        grad_probs,
        grad_gain,
        gate_grad.reshape(w_gate.shape),
        up_grad.reshape(w_up.shape),
        down_grad.reshape(w_down.shape),
    )


def solution(mesh):
    rows = P("ctx", ("exp", "dp"))
    weights = P("exp", None, ("ctx", "dp"))
    ctx = P("ctx", None)
    gain = P(("exp", "dp"))
    return jax.shard_map(
        per_device,
        mesh=mesh,
        in_specs=(
            rows, rows, ctx, ctx, rows, ctx, ctx, gain, weights, weights, weights, rows,
        ),
        out_specs=(rows, rows, ctx, ctx, rows, ctx, gain, weights, weights, weights),
        check_vma=False,
    )
```

time: 657 us -> 273 us (0.42)
  blocking collectives: 259 us -> 111 us
  waiting for transfers between devices: 179 us -> 32.6 us
  local copies, waits for them, and re-layouts: 116 us -> 12.7 us
  Pallas kernels: 0 us -> 51.8 us
  matrix products: 35.9 us -> 12.8 us
  other arithmetic: 30.4 us -> 7.33 us
  starting transfers between devices: 15 us -> 26.2 us
    psum x4 -> x0, blocking collectives: 155 us -> none  [the longest x1 46.5 us: per_device(): inner_sum = lax.psum(jnp.sum(hidden_f * scaled, axis=1), ('exp', 'dp'))]
    reduce_scatter x2 -> x0, waiting for transfers between devices: 142 us -> none  [the longest x1 81.3 us: per_device(): lax.psum_scatter(arrange_sums(full_back, ctx_count, dp_count, exp_count,...]
    all_to_all x2 -> x4, blocking collectives: 30.5 us -> 111 us  [swap(): return lax.all_to_all(x, axis, 0, 0, tiled=True)]
    all_gather x3 -> x0, blocking collectives: 73.3 us -> none  [the longest x2 48.3 us: entering(): lax.all_gather(a.astype(kind), axis)]
    pallas_call x0 -> x6, Pallas kernels: none -> 51.8 us  [the longest x1 10.9 us: per_device(): pl.pallas_call(grads_kernel, grid_spec=grid_of(1, [rows_spec, rows_spec,...]
    all_gather x2 -> x1, waiting for transfers between devices: 35.8 us -> 0.01 us  [per_device(): lax.all_gather(got_cot[:, :capacity].reshape(exp_count * capacity, feat),...]
    scatter x2 -> x0, local copies, waits for them, and re-layouts: 26.5 us -> none  [the longest x1 13.2 us: per_device(): empty.at[owners, slot_index].set(pair_cot)]
    transpose x3 -> x0, local copies, waits for them, and re-layouts: 26.1 us -> none  [the longest x2 26 us: arrange_rows(): shaped.transpose(0, 2, 3, 1, 4)]
  transfers between devices with their start and end apart: 6 -> 10, of which waited for: 4 -> 4; matrix products, arithmetic and copies ran while one was open for 13% -> 6% of each run, Pallas kernels for 0% -> 10%
where the time goes in v1:
time: 273 us; the launch traced here: 269 us
  blocking collectives  111 us (41%)
  Pallas kernels  51.8 us (19%)
  waiting for transfers between devices  32.6 us (12%)
  starting transfers between devices  26.2 us (10%)
  between operations  15.1 us (6%)
  matrix products  12.8 us (5%)
  local copies, waits for them, and re-layouts  12.7 us (5%)
  other arithmetic  7.33 us (3%)
    all_to_all x4, blocking collectives, swap(): return lax.all_to_all(x, axis, 0, 0, tiled=True)  111 us
    all_to_all x4, waiting for transfers between devices, swap(): return lax.all_to_all(x, axis, 0, 0, tiled=True)  27.5 us
    all_to_all x4, starting transfers between devices, swap(): return lax.all_to_all(x, axis, 0, 0, tiled=True)  24.9 us
    dot_general x36, matrix products, dot(): lax.dot_general(a, b, (dims, ((), ())), precision=precision, preferred_el...  12.5 us
    pallas_call x1, Pallas kernels, per_device(): pl.pallas_call(grads_kernel, grid_spec=grid_of(1, [rows_spec, rows_spec,...  10.9 us
    pallas_call x1, Pallas kernels, per_device(): pl.pallas_call(close_kernel, grid_spec=grid_of(1, [rows_spec, gain_spec,...  9.67 us
    pallas_call x1, Pallas kernels, per_device(): pl.pallas_call(back_add_kernel, grid_spec=grid_of(1, [acts, acts, w_own,...  8.15 us
    pallas_call x1, Pallas kernels, per_device(): pl.pallas_call(open_kernel, grid_spec=grid_of(1, [rows_spec, gain_spec, w...  7.93 us
  transfers between devices with their start and end apart: 10, of which 4 were waited for; matrix products, arithmetic and copies ran while one was open for 6% of the time, Pallas kernels for 10%

profile of v1, /device:TPU:2, one launch (start us, length us, event | category | flops | bytes accessed | tf_op | source)
XLA Modules:
  0.0 269.3 jit_solution(17431522771850737840)
XLA Ops:
  9.8 1.0 fusion
  10.9 18.7 %all_to_all.40 = bf16[8,48,256]{2,1,0:T(8,128)(2,1)S(1)} all-to-all(bf16[8,48,256]{2,1,0:T(8,128)(2,1)S(1)} %pad_maximum_fusion), channel_id=1, replica_groups=mesh['ctx'=16,'exp'=8,'dp'=2] {'exp'}, dimensions={0} | all-to-all | bytes 393216 | tf_op jit(solution)/shard_map/all_to_all | solution.py:73
  32.0 1.0 fusion.1
  33.9 7.5 %all-to-all-start = ((bf16[16,72,256]{2,1,0:T(8,128)(2,1)}), bf16[16,72,256]{2,1,0:T(8,128)(2,1)S(1)}, u32[]{:S(2)}, u32[]{:S(2)}) async-start(bf16[16,72,256]{2,1,0:T(8,128)(2,1)} %broadcast_in_dim.136), calls=%async_computation | async-start | bytes 1179648 | tf_op jit(solution)/shard_map/all_to_all | solution.py:73
  43.3 8.9 %all-to-all-done = bf16[16,72,256]{2,1,0:T(8,128)(2,1)S(1)} async-done(((bf16[16,72,256]{2,1,0:T(8,128)(2,1)}), bf16[16,72,256]{2,1,0:T(8,128)(2,1)S(1)}, u32[]{:S(2)}, u32[]{:S(2)}) %all-to-all-start) | async-done | bytes 589856 | tf_op jit(solution)/shard_map/all_to_all | solution.py:73
  54.3 11.8 %all_to_all.41 = bf16[8,40,256]{2,1,0:T(8,128)(2,1)S(1)} all-to-all(bf16[8,40,256]{2,1,0:T(8,128)(2,1)S(1)} %bitcast.127), channel_id=1, replica_groups=mesh['ctx'=16,'exp'=8,'dp'=2] {'exp'}, dimensions={0} | all-to-all | bytes 327680 | tf_op jit(solution)/shard_map/all_to_all | solution.py:73
  66.4 41.1 %all_to_all.42.rows_ref.own_ref = bf16[16,8,40,256]{3,2,1,0:T(8,128)(2,1)S(1)} all-to-all(bf16[16,8,40,256]{3,2,1,0:T(8,128)(2,1)S(1)} %broadcast_in_dim.138), channel_id=1, replica_groups=mesh['ctx'=16,'exp'=8,'dp'=2] {'ctx'}, dimensions={0} | all-to-all | bytes 5242880 | tf_op jit(solution)/shard_map/all_to_all | solution.py:73
  108.2 0.9 copy-done.1
  109.1 7.9 %open.1 = (f32[640,256]{1,0:T(8,128)}, f32[640,256]{1,0:T(8,128)}, f32[640,128]{1,0:T(8,128)}) custom-call(s32[1]{0:T(128)} %bitcast.core, bf16[16,8,40,256]{3,2,1,0:T(8,128)(2,1)} %copy-done.1, f32[8,1,256]{2,1,0:T(1,128)} %copy-done.11, bf16[8,2,256,256]{3,2,1,0:T(8,128)(2,1)} %bitcast.113, bf16[8,2,256,256]{3,2,1,0:T(8,128)(2,1)} %bitcast.117), custom_call_target="tpu_custom_call" | custom-call | tf_op jit(solution)/shard_map/open/pallas_call | solution.py:318
  117.0 7.6 %cot.1.ga_ref = f32[640,256]{1,0:T(8,128)} custom-call(bf16[16,2,8,40,256]{4,3,2,1,0:T(8,128)(2,1)} %bitcast.121, bf16[8,2,256,256]{3,2,1,0:T(8,128)(2,1)} %bitcast.123), custom_call_target="tpu_custom_call" | custom-call | tf_op jit(solution)/shard_map/cot/pallas_call | solution.py:315
  125.2 9.7 %close.1 = (bf16[640,256]{1,0:T(8,128)(2,1)}, bf16[640,256]{1,0:T(8,128)(2,1)}, bf16[640,256]{1,0:T(8,128)(2,1)}, bf16[640,256]{1,0:T(8,128)(2,1)}, bf16[640,256]{1,0:T(8,128)(2,1)}, /*index=5*/f32[640,128]{1,0:T(8,128)}) custom-call(s32[1]{0:T(128)} %bitcast.core, bf16[16,8,40,256]{3,2,1,0:T(8,128)(2,1)} %collective-permute-done.rows_ref.oth_ref, ...), custom_call_target="tpu_custom_call" | custom-call | tf_op jit(solution)/shard_map/close/pallas_call | solution.py:324
  134.9 7.5 %back_oth.1 = bf16[16,8,40,256]{3,2,1,0:T(8,128)(2,1)} custom-call(s32[1]{0:T(128)} %bitcast.core, bf16[640,256]{1,0:T(8,128)(2,1)} %get-tuple-element.25.dg_ref, bf16[640,256]{1,0:T(8,128)(2,1)} %get-tuple-element.26.du_ref, bf16[8,2,256,256]{3,2,1,0:T(8,128)(2,1)} %bitcast.115, bf16[8,2,256,256]{3,2,1,0:T(8,128)(2,1)} %bitcast.119), custom_call_target="tpu_custom_call" | custom-call | tf_op jit(solution)/shard_map/back_oth/pallas_call | solution.py:348
  143.0 5.1 %collective-permute-done.3 = f32[640,8]{1,0:T(8,128)S(1)} collective-permute-done((f32[640,8]{1,0:T(8,128)S(1)}, f32[640,8]{1,0:T(8,128)S(1)}, u32[]{:S(2)}, u32[]{:S(2)}) %collective-permute-start.3) | collective-permute-done | bytes 20512 | tf_op jit(solution)/shard_map/ppermute | solution.py:340
  148.0 1.0 slice_add_fusion.3
  152.2 1.5 copy-done.2
  153.7 8.1 %back_own.1 = bf16[16,328,256]{2,1,0:T(8,128)(2,1)} custom-call(s32[1]{0:T(128)} %bitcast.core, bf16[640,256]{1,0:T(8,128)(2,1)} %get-tuple-element.25.dg_ref, bf16[640,256]{1,0:T(8,128)(2,1)} %get-tuple-element.26.du_ref, bf16[8,2,256,256]{3,2,1,0:T(8,128)(2,1)} %bitcast.116, bf16[8,2,256,256]{3,2,1,0:T(8,128)(2,1)} %bitcast.120, ...), custom_call_target="tpu_custom_call" | custom-call | tf_op jit(solution)/shard_map/back_own/pallas_call | solution.py:356
  161.9 39.1 %all_to_all.43 = bf16[16,328,256]{2,1,0:T(8,128)(2,1)S(1)} all-to-all(bf16[16,328,256]{2,1,0:T(8,128)(2,1)} %back_own.1), channel_id=1, replica_groups=mesh['ctx'=16,'exp'=8,'dp'=2] {'ctx'}, dimensions={0} | all-to-all | bytes 5373952 | tf_op jit(solution)/shard_map/all_to_all | solution.py:73
  202.2 5.7 %all-to-all-start.5 = ((bf16[8,48,256]{2,1,0:T(8,128)(2,1)}), bf16[8,48,256]{2,1,0:T(8,128)(2,1)S(1)}, u32[]{:S(2)}, u32[]{:S(2)}) async-start(bf16[8,48,256]{2,1,0:T(8,128)(2,1)} %pad_maximum_fusion.1), calls=%async_computation.5 | async-start | bytes 393216 | tf_op jit(solution)/shard_map/all_to_all | solution.py:73
  208.3 10.9 %grads.1 = (bf16[8,2,256,256]{3,2,1,0:T(8,128)(2,1)}, bf16[8,2,256,256]{3,2,1,0:T(8,128)(2,1)}, bf16[8,2,256,256]{3,2,1,0:T(8,128)(2,1)}) custom-call(s32[1]{0:T(128)} %bitcast.core, bf16[16,8,40,256]{3,2,1,0:T(8,128)(2,1)} %copy-done.1, bf16[16,8,40,256]{3,2,1,0:T(8,128)(2,1)} %collective-permute-done.rows_ref.oth_ref, ...), custom_call_target="tpu_custom_call" | custom-call | tf_op jit(solution)/shard_map/grads/pallas_call | solution.py:366
  223.6 4.8 %all-to-all-start.6 = ((bf16[16,72,256]{2,1,0:T(8,128)(2,1)}), bf16[16,72,256]{2,1,0:T(8,128)(2,1)S(1)}, u32[]{:S(2)}, u32[]{:S(2)}) async-start(bf16[16,72,256]{2,1,0:T(8,128)(2,1)} %broadcast_in_dim.150), calls=%async_computation.6 | async-start | bytes 1179648 | tf_op jit(solution)/shard_map/all_to_all | solution.py:73
  231.2 7.6 %all-to-all-done.6 = bf16[16,72,256]{2,1,0:T(8,128)(2,1)S(1)} async-done(((bf16[16,72,256]{2,1,0:T(8,128)(2,1)}), bf16[16,72,256]{2,1,0:T(8,128)(2,1)S(1)}, u32[]{:S(2)}, u32[]{:S(2)}) %all-to-all-start.6) | async-done | bytes 589856 | tf_op jit(solution)/shard_map/all_to_all | solution.py:73
  239.3 0.9 add_convert_fusion
  241.4 7.0 %all-to-all-start.7 = ((bf16[8,128,128]{2,1,0:T(8,128)(2,1)}), bf16[8,128,128]{2,1,0:T(8,128)(2,1)S(1)}, u32[]{:S(2)}, u32[]{:S(2)}) async-start(bf16[8,128,128]{2,1,0:T(8,128)(2,1)} %broadcast_in_dim.151), calls=%async_computation.7 | async-start | bytes 524288 | tf_op jit(solution)/shard_map/all_to_all | solution.py:73
  250.0 10.9 %all-to-all-done.7 = bf16[8,128,128]{2,1,0:T(8,128)(2,1)S(1)} async-done(((bf16[8,128,128]{2,1,0:T(8,128)(2,1)}), bf16[8,128,128]{2,1,0:T(8,128)(2,1)S(1)}, u32[]{:S(2)}, u32[]{:S(2)}) %all-to-all-start.7) | async-done | bytes 262176 | tf_op jit(solution)/shard_map/all_to_all | solution.py:73
  (219 shorter events, 27.7 us)
Async XLA Ops:
  7.2 24.8 %copy-start = (bf16[128,64]{0,1:T(8,128)(2,1)S(1)}, bf16[128,64]{0,1:T(8,128)(2,1)}, u32[]{:S(2)}) copy-start(bf16[128,64]{0,1:T(8,128)(2,1)} %param.14) | copy-start | bytes 49156
  7.2 34.5 %copy-start.3 = (bf16[128,256]{1,0:T(8,128)(2,1)S(1)}, bf16[128,256]{1,0:T(8,128)(2,1)}, u32[]{:S(2)}) copy-start(bf16[128,256]{1,0:T(8,128)(2,1)} %param.13) | copy-start | bytes 196612
  7.2 34.3 %copy-start.5 = (bf16[128,64]{0,1:T(8,128)(2,1)S(1)}, bf16[128,64]{0,1:T(8,128)(2,1)}, u32[]{:S(2)}) copy-start(bf16[128,64]{0,1:T(8,128)(2,1)} %param.15) | copy-start | bytes 49156
  7.2 35.3 %copy-start.12 = (bf16[128,256]{1,0:T(8,128)(2,1)S(1)}, bf16[128,256]{1,0:T(8,128)(2,1)}, u32[]{:S(2)}) copy-start(bf16[128,256]{1,0:T(8,128)(2,1)} %param.12) | copy-start | bytes 196612
  7.2 109.8 %all-gather.2.cloned.1.call-start = ((), (), s32[]{:S(2)}) async-start(), calls=%async_computation.8 | async-start | bytes 5406720 | tf_op jit(solution)/shard_map/all_gather | solution.py:276
  8.0 23.9 %copy-start.21 = (s32[128]{0:T(128)}, s32[128]{0:T(128)S(1)}, u32[]{:S(2)}) copy-start(s32[128]{0:T(128)S(1)} %get-tuple-element.157) | copy-start | bytes 1540
  8.0 23.9 %copy-start.23 = (s32[128]{0:T(128)}, s32[128]{0:T(128)S(1)}, u32[]{:S(2)}) copy-start(s32[128]{0:T(128)S(1)} %get-tuple-element.158) | copy-start | bytes 1540
  8.2 45.2 %copy-start.17 = (s32[8,128]{1,0:T(8,128)}, s32[8,128]{1,0:T(8,128)S(1)}, u32[]{:S(2)}) copy-start(s32[8,128]{1,0:T(8,128)S(1)} %convolution_convert_fusion.3) | copy-start | bytes 12292
  8.2 45.2 %copy-start.19 = (pred[8,128]{1,0:T(8,128)(4,1)}, pred[8,128]{1,0:T(8,128)(4,1)S(1)}, u32[]{:S(2)}) copy-start(pred[8,128]{1,0:T(8,128)(4,1)S(1)} %fusion.135) | copy-start | bytes 3076
  31.1 35.0 %copy-start.9 = (f32[128,4]{0,1:T(4,128)}, f32[128,4]{0,1:T(4,128)S(1)}, u32[]{:S(2)}) copy-start(f32[128,4]{0,1:T(4,128)S(1)} %fusion.46) | copy-start | bytes 6148
  31.6 34.5 %copy-start.14 = (pred[4,256]{1,0:T(4,128)(4,1)}, pred[4,256]{1,0:T(4,128)(4,1)S(1)}, u32[]{:S(2)}) copy-start(pred[4,256]{1,0:T(4,128)(4,1)S(1)} %iota_compare_fusion.13) | copy-start | bytes 3076
  33.9 18.3 %all-to-all-start = ((bf16[16,72,256]{2,1,0:T(8,128)(2,1)}), bf16[16,72,256]{2,1,0:T(8,128)(2,1)S(1)}, u32[]{:S(2)}, u32[]{:S(2)}) async-start(bf16[16,72,256]{2,1,0:T(8,128)(2,1)} %broadcast_in_dim.136), calls=%async_computation | async-start | bytes 1179648 | tf_op jit(solution)/shard_map/all_to_all | solution.py:73
  107.5 17.1 %collective-permute-start = (bf16[16,8,40,256]{3,2,1,0:T(8,128)(2,1)S(1)}, bf16[16,8,40,256]{3,2,1,0:T(8,128)(2,1)}, u32[]{:S(2)}, u32[]{:S(2)}) collective-permute-start(bf16[16,8,40,256]{3,2,1,0:T(8,128)(2,1)S(1)} %all_to_all.42.rows_ref.own_ref), channel_id=1, source_target_pairs={{0,1},{1,0},{2,3},{3,2},{4,5},{5,4},{6,7},{7,6},{8,9},{9,8},{10,11... | collective-permute-start | bytes 7864328 | tf_op jit(solution)/shard_map/ppermute | solution.py:289
  107.6 17.1 %collective-permute-start.1 = (f32[8,1,256]{2,1,0:T(1,128)S(1)}, f32[8,1,256]{2,1,0:T(1,128)S(1)}, u32[]{:S(2)}, u32[]{:S(2)}) collective-permute-start(f32[8,1,256]{2,1,0:T(1,128)S(1)} %broadcast_in_dim.147.gain_ref.gown_ref), channel_id=1, source_target_pairs={{0,1},{1,0},{2,3},{3,2},{4,5},{5,4},{6,7},{7,6},{8,9},{9,8},{10,11... | collective-permute-start | bytes 24584 | tf_op jit(solution)/shard_map/ppermute | solution.py:275
  142.5 9.8 %collective-permute-start.2 = (bf16[16,8,40,256]{3,2,1,0:T(8,128)(2,1)}, bf16[16,8,40,256]{3,2,1,0:T(8,128)(2,1)S(1)}, u32[]{:S(2)}, u32[]{:S(2)}) collective-permute-start(bf16[16,8,40,256]{3,2,1,0:T(8,128)(2,1)} %back_oth.1), channel_id=1, source_target_pairs={{0,1},{1,0},{2,3},{3,2},{4,5},{5,4},{6,7},{7,6},{8,9},{9,8},{10,11... | collective-permute-start | bytes 7864328 | tf_op jit(solution)/shard_map/ppermute | solution.py:354
  142.5 5.6 %collective-permute-start.3 = (f32[640,8]{1,0:T(8,128)S(1)}, f32[640,8]{1,0:T(8,128)S(1)}, u32[]{:S(2)}, u32[]{:S(2)}) collective-permute-start(f32[640,8]{1,0:T(8,128)S(1)} %bitcast.128), channel_id=1, source_target_pairs={{0,1},{1,0},{2,3},{3,2},{4,5},{5,4},{6,7},{7,6},{8,9},{9,8},{10,11... | collective-permute-start | bytes 61448 | tf_op jit(solution)/shard_map/ppermute | solution.py:340
  202.2 17.1 %all-to-all-start.5 = ((bf16[8,48,256]{2,1,0:T(8,128)(2,1)}), bf16[8,48,256]{2,1,0:T(8,128)(2,1)S(1)}, u32[]{:S(2)}, u32[]{:S(2)}) async-start(bf16[8,48,256]{2,1,0:T(8,128)(2,1)} %pad_maximum_fusion.1), calls=%async_computation.5 | async-start | bytes 393216 | tf_op jit(solution)/shard_map/all_to_all | solution.py:73
  208.2 12.1 %copy-start.40 = (f32[128]{0:T(128)S(1)}, f32[128]{0:T(128)}, u32[]{:S(2)}) copy-start(f32[128]{0:T(128)} %copy-done.39) | copy-start | bytes 1540
  208.3 12.1 %copy-start.44 = (f32[128]{0:T(128)S(1)}, f32[128]{0:T(128)}, u32[]{:S(2)}) copy-start(f32[128]{0:T(128)} %copy-done.43) | copy-start | bytes 1540
  208.3 12.5 %copy-start.6 = (bf16[128,64]{0,1:T(8,128)(2,1)S(1)}, bf16[128,64]{0,1:T(8,128)(2,1)}, u32[]{:S(2)}) copy-start(bf16[128,64]{0,1:T(8,128)(2,1)} %param.15) | copy-start | bytes 49156
  222.8 17.4 %copy-start.27 = (f32[4]{0:T(128)S(1)}, f32[4]{0:T(128)}, u32[]{:S(2)}) copy-start(f32[4]{0:T(128)} %copy-done.26) | copy-start | bytes 52
  223.6 15.2 %all-to-all-start.6 = ((bf16[16,72,256]{2,1,0:T(8,128)(2,1)}), bf16[16,72,256]{2,1,0:T(8,128)(2,1)S(1)}, u32[]{:S(2)}, u32[]{:S(2)}) async-start(bf16[16,72,256]{2,1,0:T(8,128)(2,1)} %broadcast_in_dim.150), calls=%async_computation.6 | async-start | bytes 1179648 | tf_op jit(solution)/shard_map/all_to_all | solution.py:73
  239.2 1.4 collective-permute-start.4
  241.4 19.5 %all-to-all-start.7 = ((bf16[8,128,128]{2,1,0:T(8,128)(2,1)}), bf16[8,128,128]{2,1,0:T(8,128)(2,1)S(1)}, u32[]{:S(2)}, u32[]{:S(2)}) async-start(bf16[8,128,128]{2,1,0:T(8,128)(2,1)} %broadcast_in_dim.151), calls=%async_computation.7 | async-start | bytes 524288 | tf_op jit(solution)/shard_map/all_to_all | solution.py:73
  (34 other events, 274.1 us)
Sparse Core Ops, SparseCore 0:
  30.4 72.1 all-gather.1

commit v2 on v1

v2 whole, which is shorter than its diff:
```python
import functools

import jax
import jax.numpy as jnp
from jax import lax
from jax.experimental import pallas as pl
from jax.experimental.pallas import tpu as pltpu
from jax.sharding import PartitionSpec as P


HIGH = lax.Precision.HIGHEST
EPS = 1e-05
F32 = jnp.float32
BF16 = jnp.bfloat16


def dot(a, b, dims=((1,), (0,)), precision=None):
    return lax.dot_general(a, b, (dims, ((), ())), precision=precision, preferred_element_type=F32)


def head_map(heads, width):
    size = width // heads
    return (
        lax.broadcasted_iota(jnp.int32, (heads, width), 1) // size
        == lax.broadcasted_iota(jnp.int32, (heads, width), 0)
    ).astype(F32)


def lower_mask(n):
    return lax.broadcasted_iota(jnp.int32, (n, n), 0) >= lax.broadcasted_iota(jnp.int32, (n, n), 1)


def block_state(values, key_rows, log_decay):
    tri = lower_mask(values.shape[0]).astype(F32)
    spread = head_map(log_decay.shape[1], values.shape[1])
    cumulative = dot(tri, log_decay, precision=HIGH)
    total_log = cumulative[-1:]
    tail = dot(jnp.exp(total_log - cumulative), spread, precision=HIGH)
    return total_log, dot(key_rows, tail * values, ((0,), (0,)), HIGH)


def block_output(values, key_rows, queries, log_decay, state_in):
    length, width = values.shape
    heads = log_decay.shape[1]
    size = width // heads
    causal = lower_mask(length)
    tri = causal.astype(F32)
    cumulative = dot(tri, log_decay, precision=HIGH)
    cum_heads = dot(log_decay, tri, ((0,), (1,)), HIGH)
    scores = dot(queries, key_rows, ((1,), (1,)), HIGH)
    parts = []
    for h in range(heads):
        log_gap = jnp.where(causal, cumulative[:, h : h + 1] - cum_heads[h : h + 1, :], 0.0)
        decay_mat = jnp.where(causal, jnp.exp(log_gap), 0.0)
        parts.append(dot(decay_mat * scores, values[:, h * size : (h + 1) * size], precision=HIGH))
    carried = dot(queries, state_in, precision=HIGH)
    growth = dot(jnp.exp(cumulative), head_map(heads, width), precision=HIGH)
    return jnp.concatenate(parts, axis=1) + growth * carried


def split_rows(x, parts):
    rows = []
    for _ in range(parts):
        head = lax.reduce_precision(x, 8, 7)
        rows.append(head.astype(BF16))
        x = x - head
    return rows


def pad_rows(rows, count, width):
    block = jnp.concatenate(rows, axis=0)
    return jnp.pad(block, ((0, count - block.shape[0]), (0, width - block.shape[1])))


def swap(x, axis):
    return lax.all_to_all(x, axis, 0, 0, tiled=True)


def to_all(x, axis):
    return swap(jnp.broadcast_to(x[None], (lax.axis_size(axis),) + x.shape), axis)


def stacked(ref):
    return ref[...].reshape(ref.shape[0] * ref.shape[1], ref.shape[2])


def square_sums(rows_ref, like):
    total = None
    for start in range(0, rows_ref.shape[1], like.shape[1]):
        part = rows_ref[:, start : start + like.shape[1]].astype(F32)
        total = part * part if total is None else total + part * part
    return jnp.broadcast_to(jnp.sum(total, axis=1, keepdims=True), like.shape)


def open_kernel(core, rows_ref, wg_ref, wu_ref, ag_ref, au_ref, ss_ref):
    ag_ref[...] = dot(rows_ref[...], stacked(wg_ref))
    au_ref[...] = dot(rows_ref[...], stacked(wu_ref))
    ss_ref[...] = square_sums(rows_ref, ss_ref)


def close_kernel(
    core, rows_ref, wg_ref, wu_ref, ag_in, au_in, ss_in, ga_ref,
    hact_ref, dg_ref, du_ref, dgi_ref, dui_ref, sc_ref,
):
    width = 2 * rows_ref.shape[1]
    total = (ss_in[...] + square_sums(rows_ref, ss_in))[:, :1]
    inv = lax.rsqrt(total / width + EPS)
    act_gate = inv * (ag_in[...] + dot(rows_ref[...], stacked(wg_ref)))
    act_up = inv * (au_in[...] + dot(rows_ref[...], stacked(wu_ref)))
    grad_act = ga_ref[...]
    sig = jax.nn.sigmoid(act_gate)
    swish = act_gate * sig
    slope = sig * (1.0 + act_gate * (1.0 - sig))
    hact = (swish * act_up).astype(BF16)
    dg32 = grad_act * act_up * slope
    du32 = grad_act * swish
    dg = dg32.astype(BF16)
    du = du32.astype(BF16)
    hact_ref[...] = hact
    dg_ref[...] = dg
    du_ref[...] = du
    dgi_ref[...] = (inv * dg32).astype(BF16)
    dui_ref[...] = (inv * du32).astype(BF16)
    probs = jnp.sum(hact.astype(F32) * grad_act, axis=1, keepdims=True)
    inner = jnp.sum(dg.astype(F32) * act_gate + du.astype(F32) * act_up, axis=1, keepdims=True)
    lane = lax.broadcasted_iota(jnp.int32, sc_ref.shape, 1)
    sc_ref[...] = jnp.where(
        lane == 0, probs, jnp.where(lane == 1, inner, jnp.where(lane == 2, inv, 0.0))
    )


def cot_kernel(core, own_ref, oth_ref, w_own_ref, w_oth_ref, ga_ref):
    ga_ref[...] = dot(own_ref[...], stacked(w_own_ref)) + dot(oth_ref[...], stacked(w_oth_ref))


def back_term(dg_ref, du_ref, wg_ref, wu_ref, block):
    return dot(dg_ref[...], wg_ref[block], ((1,), (1,))) + dot(
        du_ref[...], wu_ref[block], ((1,), (1,))
    )


def back_kernel(core, dg_ref, du_ref, wg_ref, wu_ref, out_ref):
    feat = wg_ref.shape[1]
    for block in range(wg_ref.shape[0]):
        term = back_term(dg_ref, du_ref, wg_ref, wu_ref, block)
        out_ref[:, block * feat : (block + 1) * feat] = term.astype(BF16)


def back_add_kernel(
    ctx_count, core, dg_ref, du_ref, wg_ref, wu_ref, other_ref, sc_ref, sc_other_ref, out_ref
):
    feat = wg_ref.shape[1]
    width = wg_ref.shape[0] * feat
    for block in range(wg_ref.shape[0]):
        lanes = slice(block * feat, (block + 1) * feat)
        term = back_term(dg_ref, du_ref, wg_ref, wu_ref, block).astype(BF16).astype(F32)
        out_ref[:, lanes] = (term + other_ref[:, lanes].astype(F32)).astype(BF16)
    small = sc_ref[...] + sc_other_ref[...]
    lane = lax.broadcasted_iota(jnp.int32, small.shape, 1)
    small = jnp.where(lane == 2, small * (0.5 / ctx_count), small)
    head = small.astype(BF16).astype(F32)
    tail = pltpu.roll(small - head, 3, 1)
    out_ref[:, width:] = jnp.where(lane < 3, head, jnp.where(lane < 6, tail, 0.0)).astype(BF16)


def grads_kernel(
    core, own_ref, oth_ref, cot_own_ref, cot_oth_ref, gown_ref, goth_ref, dgi_ref, dui_ref,
    hact_ref, gate_ref, up_ref, down_ref,
):
    here = core[0]
    first = ((0,), (0,))
    for rows_ref, cot_ref, gain_ref, place in (
        (own_ref, cot_own_ref, gown_ref, here),
        (oth_ref, cot_oth_ref, goth_ref, 1 - here),
    ):
        scaled = (rows_ref[...].astype(F32) * gain_ref[...]).astype(BF16)
        gate_ref[place] = dot(scaled, dgi_ref[...], first).astype(BF16)
        up_ref[place] = dot(scaled, dui_ref[...], first).astype(BF16)
        down_ref[place] = dot(cot_ref[...], hact_ref[...], first).astype(BF16)


def sums_kernel(got_ref, out_ref):
    feat = out_ref.shape[2] - 128
    count = out_ref.shape[0]

    def total(start, width):
        acc = got_ref[0, :, start : start + width].astype(F32)
        for block in range(1, got_ref.shape[0]):
            acc += got_ref[block, :, start : start + width].astype(F32)
        return acc

    small = total(count * feat, 128)
    lane = lax.broadcasted_iota(jnp.int32, small.shape, 1)
    small = jnp.where(lane < 3, small + pltpu.roll(small, 125, 1), 0.0)
    head = small.astype(BF16).astype(F32)
    small = (head + pltpu.roll(small - head, 3, 1)).astype(BF16)
    for block in range(count):
        out_ref[block, :, :feat] = total(block * feat, feat).astype(BF16)
        out_ref[block, :, feat:] = small


def whole(shape):
    return pl.BlockSpec(shape, lambda e, *_: (0,) * len(shape))


def side_by_side(blocks):
    return jnp.concatenate([blocks[e] for e in range(blocks.shape[0])], axis=1)


def per_device(
    residual,
    ssm_values,
    ssm_keys,
    ssm_queries,
    log_decay,
    expert_ids,
    gate_probs,
    norm_gain,
    w_gate,
    w_up,
    w_down,
    out_grad,
):
    tokens, feat = residual.shape
    heads = log_decay.shape[1]
    model_width, units = w_gate.shape[1:]
    ctx_count = lax.axis_size("ctx")
    exp_count = lax.axis_size("exp")
    capacity = 5 * tokens // (2 * exp_count)
    rows_all = ctx_count * capacity
    ctx_here = lax.axis_index("ctx")
    core = lax.axis_index("dp").astype(jnp.int32).reshape(1)
    other_core = [(0, 1), (1, 0)]

    values = ssm_values.astype(F32)
    key_rows = ssm_keys.astype(F32)
    queries = ssm_queries.astype(F32)
    (total_log, state_local), state_pull = jax.vjp(block_state, values, key_rows, log_decay)
    state_rows = state_local.shape[0]
    payload = jnp.concatenate(
        [state_local.astype(BF16), pad_rows(split_rows(total_log, 3), 8, feat)], axis=0
    )
    got = to_all(payload, "ctx")
    logs = jnp.sum(got[:, state_rows : state_rows + 3, :heads].astype(F32), axis=1)
    source = lax.broadcasted_iota(jnp.int32, (ctx_count, ctx_count), 0)
    between = lax.broadcasted_iota(jnp.int32, (ctx_count, ctx_count), 1)
    spread = head_map(heads, feat)
    rank = jnp.arange(ctx_count, dtype=jnp.int32)[:, None]
    before = ((between > source) & (between < ctx_here)).astype(F32)
    after = ((between < source) & (between > ctx_here)).astype(F32)
    gap_before = jnp.sum(before[:, :, None] * logs[None], axis=1)
    gap_after = jnp.sum(after[:, :, None] * logs[None], axis=1)
    weight_before = dot(
        jnp.where(rank < ctx_here, jnp.exp(gap_before), 0.0), spread, precision=HIGH
    )
    weight_after = dot(jnp.where(rank > ctx_here, jnp.exp(gap_after), 0.0), spread, precision=HIGH)
    state_in = jnp.sum(weight_before[:, None, :] * got[:, :state_rows].astype(F32), axis=0)

    ids = expert_ids.T
    probs = gate_probs.T
    experts = jnp.arange(exp_count, dtype=jnp.int32)[:, None]
    named = [ids[k][None, :] == experts for k in range(2)]
    member = named[0] | named[1]
    strict = (~lower_mask(tokens)).astype(BF16)
    order = dot(member.astype(BF16), strict).astype(jnp.int32)
    slot = lax.broadcasted_iota(jnp.int32, (exp_count, capacity, tokens), 1)
    chosen = (order[:, None, :] == slot) & member[:, None, :]
    select = chosen.astype(BF16).reshape(exp_count * capacity, tokens)
    select_each = jnp.concatenate(
        [
            (chosen & named[k][:, None, :]).astype(BF16).reshape(exp_count * capacity, tokens)
            for k in range(2)
        ],
        axis=1,
    )
    prob_of = jnp.where(named[0], probs[0][None, :], jnp.where(named[1], probs[1][None, :], 0.0))
    prob_rows = jnp.sum(jnp.where(chosen, prob_of[:, None, :], 0.0), axis=2)

    cot = (dot(select, out_grad).reshape(exp_count, capacity, feat) * prob_rows[:, :, None]).astype(
        BF16
    )
    gain_rows = pad_rows(split_rows(norm_gain[None, :], 3), 8, feat)
    cot_payload = jnp.concatenate(
        [cot, jnp.broadcast_to(gain_rows[None], (exp_count,) + gain_rows.shape)], axis=1
    )
    got_cot = swap(cot_payload, "exp")
    gain_own = jnp.sum(got_cot[:, capacity : capacity + 3].astype(F32), axis=1)
    gain_oth = lax.ppermute(gain_own, "dp", other_core)
    gain4 = jnp.where(
        core[0] == 0,
        jnp.stack([gain_own, gain_oth], axis=1),
        jnp.stack([gain_oth, gain_own], axis=1),
    )
    gate4 = w_gate.reshape(exp_count, 2, feat, units)
    up4 = w_up.reshape(exp_count, 2, feat, units)
    down4 = w_down.reshape(exp_count, 2, feat, units)
    gate_scaled = (gate4.astype(F32) * gain4[:, :, :, None]).astype(BF16)
    up_scaled = (up4.astype(F32) * gain4[:, :, :, None]).astype(BF16)
    wide = exp_count * feat
    rows_all = ctx_count * capacity
    cot_own = lax.all_gather(side_by_side(got_cot[:, :capacity]), "ctx", axis=0).reshape(
        rows_all, wide
    )
    cot_oth = lax.ppermute(cot_own, "dp", other_core)

    mixer_out, output_pull = jax.vjp(
        block_output, values, key_rows, queries, log_decay, state_in
    )
    hidden = (residual.astype(F32) + mixer_out).astype(BF16)
    hidden_f = hidden.astype(F32)
    got_rows = swap(
        dot(select, hidden).astype(BF16).reshape(exp_count, capacity, feat), "exp"
    )
    own = to_all(side_by_side(got_rows), "ctx").reshape(rows_all, wide)
    oth = lax.ppermute(own, "dp", other_core)

    split = 2
    part = rows_all // split
    rows_spec = pl.BlockSpec((part, wide), lambda i, *_: (i, 0))
    acts = pl.BlockSpec((part, units), lambda i, *_: (i, 0))
    sums = pl.BlockSpec((part, 128), lambda i, *_: (i, 0))
    w_own = pl.BlockSpec((exp_count, None, feat, units), lambda i, s: (0, s[0], 0, 0))
    w_oth = pl.BlockSpec((exp_count, None, feat, units), lambda i, s: (0, 1 - s[0], 0, 0))
    acts_f = jax.ShapeDtypeStruct((rows_all, units), F32)
    acts_b = jax.ShapeDtypeStruct((rows_all, units), BF16)
    sums_f = jax.ShapeDtypeStruct((rows_all, 128), F32)

    def grid_of(n_scalars, steps, in_specs, out_specs):
        return pltpu.PrefetchScalarGridSpec(
            num_scalar_prefetch=n_scalars,
            grid=(steps,),
            in_specs=in_specs,
            out_specs=out_specs,
        )

    grad_act = pl.pallas_call(
        cot_kernel,
        grid_spec=grid_of(1, split, [rows_spec, rows_spec, w_own, w_oth], acts),
        out_shape=acts_f,
        name="cot",
    )(core, cot_own, cot_oth, down4, down4)
    ag, au, ss = pl.pallas_call(
        open_kernel,
        grid_spec=grid_of(1, split, [rows_spec, w_own, w_own], [acts, acts, sums]),
        out_shape=[acts_f, acts_f, sums_f],
        name="open",
    )(core, own, gate_scaled, up_scaled)
    hact, dg, du, dgi, dui, scal = pl.pallas_call(
        close_kernel,
        grid_spec=grid_of(
            1,
            split,
            [rows_spec, w_oth, w_oth, acts, acts, sums, acts],
            [acts] * 5 + [sums],
        ),
        out_shape=[acts_b] * 5 + [sums_f],
        name="close",
    )(core, oth, gate_scaled, up_scaled, ag, au, ss, grad_act)
    scal_got = lax.ppermute(scal, "dp", other_core)
    back_oth = pl.pallas_call(
        back_kernel,
        grid_spec=grid_of(1, split, [acts, acts, w_oth, w_oth], rows_spec),
        out_shape=jax.ShapeDtypeStruct((rows_all, wide), BF16),
        name="back_oth",
    )(core, dg, du, gate4, up4)
    back_got = lax.ppermute(back_oth, "dp", other_core)
    back = pl.pallas_call(
        functools.partial(back_add_kernel, ctx_count),
        grid_spec=grid_of(
            1,
            split,
            [acts, acts, w_own, w_own, rows_spec, sums, sums],
            pl.BlockSpec((part, wide + 128), lambda i, *_: (i, 0)),
        ),
        out_shape=jax.ShapeDtypeStruct((rows_all, wide + 128), BF16),
        name="back_own",
    )(core, dg, du, gate4, up4, back_got, scal, scal_got)
    columns = pl.BlockSpec((rows_all, feat), lambda e, *_: (0, e))
    gain_spec = pl.BlockSpec((None, 1, feat), lambda e, *_: (e, 0, 0))
    w_pair = pl.BlockSpec((None, 2, feat, units), lambda e, *_: (e, 0, 0, 0))
    acts_all = whole((rows_all, units))
    gate_grad, up_grad, down_grad = pl.pallas_call(
        grads_kernel,
        grid_spec=grid_of(
            1,
            exp_count,
            [
                columns,
                columns,
                columns,
                columns,
                gain_spec,
                gain_spec,
                acts_all,
                acts_all,
                acts_all,
            ],
            [w_pair] * 3,
        ),
        out_shape=[jax.ShapeDtypeStruct(gate4.shape, BF16)] * 3,
        name="grads",
    )(
        core, own, oth, cot_own, cot_oth, gain_own[:, None], gain_oth[:, None], dgi, dui, hact
    )

    got_sums = swap(back.reshape(ctx_count, capacity, wide + 128), "ctx")
    summed = pl.pallas_call(
        sums_kernel,
        out_shape=jax.ShapeDtypeStruct((exp_count, capacity, feat + 128), BF16),
        name="sums",
    )(got_sums)
    got_back = swap(summed, "exp").reshape(exp_count * capacity, feat + 128)
    grad_normed = dot(select, got_back[:, :feat], ((0,), (0,)))
    small = dot(select_each, got_back[:, feat:], ((0,), (0,)))
    small = small[:, :3] + small[:, 3:6]
    grad_probs = (
        jnp.concatenate([small[:tokens, :1], small[tokens:, :1]], axis=1) / gate_probs
    )
    inner = small[:tokens, 1:2] + small[tokens:, 1:2]
    inv_rms = small[:tokens, 2:3]
    scaled = grad_normed * norm_gain[None, :]
    grad_hidden = (
        out_grad.astype(F32)
        + inv_rms * scaled
        - hidden_f * (inv_rms * inv_rms * inner / model_width)
    )
    gain_part = jnp.sum(grad_normed * hidden_f * inv_rms, axis=0, keepdims=True)

    vals_first, keys_first, queries_part, decay_first, carry_cot = output_pull(grad_hidden)
    got_carry = to_all(
        jnp.concatenate(
            [carry_cot.astype(BF16), pad_rows(split_rows(gain_part, 3), 8, feat)], axis=0
        ),
        "ctx",
    )
    grad_state = jnp.sum(weight_after[:, None, :] * got_carry[:, :state_rows].astype(F32), axis=0)
    grad_gain = jnp.sum(got_carry[:, state_rows : state_rows + 3].astype(F32), axis=(0, 1))
    grad_total = dot(
        jnp.sum(grad_state * state_in, axis=0, keepdims=True), spread, ((1,), (1,)), HIGH
    ) * jnp.exp(total_log)
    vals_second, keys_second, decay_second = state_pull((grad_total, grad_state))
    both = jnp.concatenate([keys_first + keys_second, queries_part], axis=1).astype(BF16)
    both = (both.astype(F32) + lax.ppermute(both, "dp", other_core).astype(F32)).astype(BF16)
    both = jnp.sum(to_all(both, "exp").astype(F32), axis=0)
    return (
        grad_hidden.astype(BF16),
        (vals_first + vals_second).astype(BF16),
        both[:, :state_rows],
        both[:, state_rows:],
        decay_first + decay_second,
        grad_probs,
        grad_gain,
        gate_grad.reshape(w_gate.shape),
        up_grad.reshape(w_up.shape),
        down_grad.reshape(w_down.shape),
    )


def solution(mesh):
    rows = P("ctx", ("exp", "dp"))
    weights = P("exp", None, ("ctx", "dp"))
    ctx = P("ctx", None)
    gain = P(("exp", "dp"))
    return jax.shard_map(
        per_device,
        mesh=mesh,
        in_specs=(
            rows, rows, ctx, ctx, rows, ctx, ctx, gain, weights, weights, weights, rows,
        ),
        out_specs=(rows, rows, ctx, ctx, rows, ctx, gain, weights, weights, weights),
        check_vma=False,
    )
```

time: 273 us -> 272 us (level)
  blocking collectives: 111 us -> 57.1 us
  waiting for transfers between devices: 32.6 us -> 81.2 us
  Pallas kernels: 51.8 us -> 39.8 us
  starting transfers between devices: 26.2 us -> 37.5 us
  matrix products: 12.8 us -> 16.5 us
    all_to_all x4 -> x2, blocking collectives: 111 us -> 57.1 us  [swap(): return lax.all_to_all(x, axis, 0, 0, tiled=True)]
    all_gather x1, waiting for transfers between devices: 0.01 us -> 40.1 us  [per_device(): lax.all_gather(side_by_side(got_cot[:, :capacity]), 'ctx', axis=0)]
    pallas_call x6 -> x7, Pallas kernels: 51.8 us -> 39.8 us  [the longest x1 11.6 us: per_device(): pl.pallas_call(grads_kernel, grid_spec=grid_of(1, exp_count, [columns, co...]
    all_to_all x4 -> x6, starting transfers between devices: 24.9 us -> 36.1 us  [swap(): return lax.all_to_all(x, axis, 0, 0, tiled=True)]
    ppermute x1, waiting for transfers between devices: 0.01 us -> 8.27 us  [per_device(): gain_oth = lax.ppermute(gain_own, 'dp', other_core)]
    convert_element_type x1, other arithmetic: 0.01 us -> 4.04 us  [per_device(): up_scaled = (up4.astype(F32) * gain4[:, :, :, None]).astype(BF16)]
    dot_general x36 -> x37, matrix products: 12.5 us -> 16.5 us  [dot(): lax.dot_general(a, b, (dims, ((), ())), precision=precision, preferred_el...]
    unnamed x103 -> x97, local copies, waits for them, and re-layouts: 5.77 us -> 6.6 us
  transfers between devices with their start and end apart: 10 -> 13, of which waited for: 4 -> 7; matrix products, arithmetic and copies ran while one was open for 6% -> 9% of each run, Pallas kernels for 10% -> 8%
where the time goes in v2:
time: 272 us; the launch traced here: 269 us
  waiting for transfers between devices  81.2 us (30%)
  blocking collectives  57.1 us (21%)
  Pallas kernels  39.8 us (15%)
  starting transfers between devices  37.5 us (14%)
  matrix products  16.5 us (6%)
  between operations  15.1 us (6%)
  local copies, waits for them, and re-layouts  12.8 us (5%)
  other arithmetic  8.92 us (3%)
    all_to_all x2, blocking collectives, swap(): return lax.all_to_all(x, axis, 0, 0, tiled=True)  57.1 us
    all_gather x1, waiting for transfers between devices, per_device(): lax.all_gather(side_by_side(got_cot[:, :capacity]), 'ctx', axis=0)  40.1 us
    all_to_all x6, starting transfers between devices, swap(): return lax.all_to_all(x, axis, 0, 0, tiled=True)  36.1 us
    all_to_all x6, waiting for transfers between devices, swap(): return lax.all_to_all(x, axis, 0, 0, tiled=True)  27.7 us
    dot_general x37, matrix products, dot(): lax.dot_general(a, b, (dims, ((), ())), precision=precision, preferred_el...  16.5 us
    pallas_call x1, Pallas kernels, per_device(): pl.pallas_call(grads_kernel, grid_spec=grid_of(1, exp_count, [columns, co...  11.6 us
    ppermute x1, waiting for transfers between devices, per_device(): gain_oth = lax.ppermute(gain_own, 'dp', other_core)  8.27 us
    unnamed x97, local copies, waits for them, and re-layouts  6.6 us
  transfers between devices with their start and end apart: 13, of which 7 were waited for; matrix products, arithmetic and copies ran while one was open for 9% of the time, Pallas kernels for 8%

profile of v2, /device:TPU:2, one launch (start us, length us, event | category | flops | bytes accessed | tf_op | source)
XLA Modules:
  0.0 268.9 jit_solution(9088112247559097422)
XLA Ops:
  11.5 8.5 %all-to-all-start.3 = ((bf16[8,48,256]{2,1,0:T(8,128)(2,1)}), bf16[8,48,256]{2,1,0:T(8,128)(2,1)S(1)}, u32[]{:S(2)}, u32[]{:S(2)}) async-start(bf16[8,48,256]{2,1,0:T(8,128)(2,1)} %pad_maximum_fusion), calls=%async_computation.3 | async-start | bytes 393216 | tf_op jit(solution)/shard_map/all_to_all | solution.py:76
  31.2 7.5 %all-to-all-start = ((bf16[16,72,256]{2,1,0:T(8,128)(2,1)}), bf16[16,72,256]{2,1,0:T(8,128)(2,1)S(1)}, u32[]{:S(2)}, u32[]{:S(2)}) async-start(bf16[16,72,256]{2,1,0:T(8,128)(2,1)} %broadcast_in_dim.128), calls=%async_computation | async-start | bytes 1179648 | tf_op jit(solution)/shard_map/all_to_all | solution.py:76
  39.6 9.2 %all-to-all-done = bf16[16,72,256]{2,1,0:T(8,128)(2,1)S(1)} async-done(((bf16[16,72,256]{2,1,0:T(8,128)(2,1)}), bf16[16,72,256]{2,1,0:T(8,128)(2,1)S(1)}, u32[]{:S(2)}, u32[]{:S(2)}) %all-to-all-start) | async-done | bytes 589856 | tf_op jit(solution)/shard_map/all_to_all | solution.py:76
  50.7 16.1 %all_to_all.40 = bf16[8,40,256]{2,1,0:T(8,128)(2,1)S(1)} all-to-all(bf16[8,40,256]{2,1,0:T(8,128)(2,1)S(1)} %bitcast.190), channel_id=1, replica_groups=mesh['ctx'=16,'exp'=8,'dp'=2] {'exp'}, dimensions={0} | all-to-all | bytes 327680 | tf_op jit(solution)/shard_map/all_to_all | solution.py:76
  66.9 1.8 broadcast_in_dim.130
  68.7 5.0 %all-to-all-start.2 = ((bf16[16,40,2048]{2,1,0:T(8,128)(2,1)}), bf16[16,40,2048]{2,1,0:T(8,128)(2,1)S(1)}, u32[]{:S(2)}, u32[]{:S(2)}) async-start(bf16[16,40,2048]{2,1,0:T(8,128)(2,1)} %broadcast_in_dim.130), calls=%async_computation.2 | async-start | bytes 5242880 | tf_op jit(solution)/shard_map/all_to_all | solution.py:76
  73.7 40.1 %all-gather.3.cloned.1.call-done.own_ref.cot_own_ref = bf16[640,2048]{1,0:T(8,128)(2,1)} async-done(((bf16[40,2048]{1,0:T(8,128)(2,1)}), bf16[640,2048]{1,0:T(8,128)(2,1)}) %all-gather.3.cloned.1.call-update) | async-done | bytes 2621456 | tf_op jit(solution)/shard_map/all_gather | solution.py:301
  114.5 8.3 %collective-permute-done.1 = f32[8,256]{1,0:T(8,128)S(1)} collective-permute-done((f32[8,256]{1,0:T(8,128)S(1)}, f32[8,256]{1,0:T(8,128)S(1)}, u32[]{:S(2)}, u32[]{:S(2)}) %collective-permute-start.1) | collective-permute-done | bytes 8224 | tf_op jit(solution)/shard_map/ppermute | solution.py:288
  122.8 4.0 %multiply_convert_fusion = (bf16[8,2,256,256]{3,2,1,0:T(8,128)(2,1)}, bf16[8,2,256,256]{3,2,1,0:T(8,128)(2,1)}) fusion(bf16[8,2,256,256]{3,2,1,0:T(8,128)(2,1)} %bitcast.181, f32[8,2,256]{2,1,0:T(2,128)S(1)} %maximum_select_fusion, bf16[8,2,256,256]{3,2,1,0:T(8,128)(2,1)} %bitcast.184), kind=kLoop, calls=%fused_computation | loop fusion | flops 6291456 | bytes 8404992 | tf_op jit(solution)/shard_map/convert_element_type | solution.py:298
  126.9 4.7 %open.1 = (f32[640,256]{1,0:T(8,128)}, f32[640,256]{1,0:T(8,128)}, f32[640,128]{1,0:T(8,128)}) custom-call(s32[1]{0:T(128)} %bitcast.7.core, bf16[640,2048]{1,0:T(8,128)(2,1)} %bitcast.179, bf16[8,2,256,256]{3,2,1,0:T(8,128)(2,1)} %get-tuple-element.117.wg_ref, bf16[8,2,256,256]{3,2,1,0:T(8,128)(2,1)} %get-tuple-element.116.wu_ref), custom_call_target="tpu_custom_call" | custom-call | tf_op jit(solution)/shard_map/open/pallas_call | solution.py:342
  131.6 4.8 %cot.1.ga_ref = f32[640,256]{1,0:T(8,128)} custom-call(s32[1]{0:T(128)} %bitcast.7.core, bf16[640,2048]{1,0:T(8,128)(2,1)} %all-gather.3.cloned.1.call-done.own_ref.cot_own_ref, bf16[640,2048]{1,0:T(8,128)(2,1)} %collective-permute-done.2.oth_ref.cot_oth_ref, bf16[8,2,256,256]{3,2,1,0:T(8,128)(2,1)} %bitcast.188, bf16[8,2,256,256]{3,2,1,0:T(8,128)(2,1)} %bitcast.189), custom_call_target="tpu_custom_call" | custom-call | tf_op jit(solution)/shard_map/cot/pallas_call | solution.py:336
  136.4 5.9 %close.1 = (bf16[640,256]{1,0:T(8,128)(2,1)}, bf16[640,256]{1,0:T(8,128)(2,1)}, bf16[640,256]{1,0:T(8,128)(2,1)}, bf16[640,256]{1,0:T(8,128)(2,1)}, bf16[640,256]{1,0:T(8,128)(2,1)}, /*index=5*/f32[640,128]{1,0:T(8,128)}) custom-call(s32[1]{0:T(128)} %bitcast.7.core, bf16[640,2048]{1,0:T(8,128)(2,1)} %collective-permute-done.rows_ref.oth_ref, ...), custom_call_target="tpu_custom_call" | custom-call | tf_op jit(solution)/shard_map/close/pallas_call | solution.py:348
  142.4 4.6 %back_oth.1 = bf16[640,2048]{1,0:T(8,128)(2,1)} custom-call(s32[1]{0:T(128)} %bitcast.7.core, bf16[640,256]{1,0:T(8,128)(2,1)} %get-tuple-element.25.dg_ref, bf16[640,256]{1,0:T(8,128)(2,1)} %get-tuple-element.26.du_ref, bf16[8,2,256,256]{3,2,1,0:T(8,128)(2,1)} %bitcast.185, bf16[8,2,256,256]{3,2,1,0:T(8,128)(2,1)} %bitcast.182), custom_call_target="tpu_custom_call" | custom-call | tf_op jit(solution)/shard_map/back_oth/pallas_call | solution.py:360
  147.5 5.1 %collective-permute-done.4.sc_other_ref = f32[640,128]{1,0:T(8,128)S(1)} collective-permute-done((f32[640,128]{1,0:T(8,128)S(1)}, f32[640,128]{1,0:T(8,128)S(1)}, u32[]{:S(2)}, u32[]{:S(2)}) %collective-permute-start.4) | collective-permute-done | bytes 327712 | tf_op jit(solution)/shard_map/ppermute | solution.py:359
  153.3 1.5 copy-done.2
  154.9 5.2 %back_own.1 = bf16[640,2176]{1,0:T(8,128)(2,1)} custom-call(s32[1]{0:T(128)} %bitcast.7.core, bf16[640,256]{1,0:T(8,128)(2,1)} %get-tuple-element.25.dg_ref, bf16[640,256]{1,0:T(8,128)(2,1)} %get-tuple-element.26.du_ref, bf16[8,2,256,256]{3,2,1,0:T(8,128)(2,1)} %bitcast.186, bf16[8,2,256,256]{3,2,1,0:T(8,128)(2,1)} %bitcast.183, ...), custom_call_target="tpu_custom_call" | custom-call | tf_op jit(solution)/shard_map/back_own/pallas_call | solution.py:367
  160.1 41.0 %all_to_all.41.got_ref = bf16[16,40,2176]{2,1,0:T(8,128)(2,1)} all-to-all(bf16[16,40,2176]{2,1,0:T(8,128)(2,1)} %bitcast.187), channel_id=1, replica_groups=mesh['ctx'=16,'exp'=8,'dp'=2] {'ctx'}, dimensions={0} | all-to-all | bytes 5570560 | tf_op jit(solution)/shard_map/all_to_all | solution.py:76
  201.1 2.9 %sums.1 = bf16[8,40,384]{2,1,0:T(8,128)(2,1)} custom-call(bf16[16,40,2176]{2,1,0:T(8,128)(2,1)} %all_to_all.41.got_ref), custom_call_target="tpu_custom_call" | custom-call | tf_op jit(solution)/shard_map/sums/pallas_call | solution.py:407
  204.0 3.6 %all-to-all-start.5 = ((bf16[8,40,384]{2,1,0:T(8,128)(2,1)}), bf16[8,40,384]{2,1,0:T(8,128)(2,1)S(1)}, u32[]{:S(2)}, u32[]{:S(2)}) async-start(bf16[8,40,384]{2,1,0:T(8,128)(2,1)} %sums.1), calls=%async_computation.5 | async-start | bytes 491520 | tf_op jit(solution)/shard_map/all_to_all | solution.py:76
  208.1 11.6 %grads.1 = (bf16[8,2,256,256]{3,2,1,0:T(8,128)(2,1)}, bf16[8,2,256,256]{3,2,1,0:T(8,128)(2,1)}, bf16[8,2,256,256]{3,2,1,0:T(8,128)(2,1)}) custom-call(s32[1]{0:T(128)} %bitcast.7.core, bf16[640,2048]{1,0:T(8,128)(2,1)} %bitcast.180, bf16[640,2048]{1,0:T(8,128)(2,1)} %collective-permute-done.rows_ref.oth_ref, ...), custom_call_target="tpu_custom_call" | custom-call | tf_op jit(solution)/shard_map/grads/pallas_call | solution.py:382
  223.3 5.0 %all-to-all-start.6 = ((bf16[16,72,256]{2,1,0:T(8,128)(2,1)}), bf16[16,72,256]{2,1,0:T(8,128)(2,1)S(1)}, u32[]{:S(2)}, u32[]{:S(2)}) async-start(bf16[16,72,256]{2,1,0:T(8,128)(2,1)} %broadcast_in_dim.140), calls=%async_computation.6 | async-start | bytes 1179648 | tf_op jit(solution)/shard_map/all_to_all | solution.py:76
  231.7 7.0 %all-to-all-done.6 = bf16[16,72,256]{2,1,0:T(8,128)(2,1)S(1)} async-done(((bf16[16,72,256]{2,1,0:T(8,128)(2,1)}), bf16[16,72,256]{2,1,0:T(8,128)(2,1)S(1)}, u32[]{:S(2)}, u32[]{:S(2)}) %all-to-all-start.6) | async-done | bytes 589856 | tf_op jit(solution)/shard_map/all_to_all | solution.py:76
  241.3 6.7 %all-to-all-start.7 = ((bf16[8,128,128]{2,1,0:T(8,128)(2,1)}), bf16[8,128,128]{2,1,0:T(8,128)(2,1)S(1)}, u32[]{:S(2)}, u32[]{:S(2)}) async-start(bf16[8,128,128]{2,1,0:T(8,128)(2,1)} %broadcast_in_dim.141), calls=%async_computation.7 | async-start | bytes 524288 | tf_op jit(solution)/shard_map/all_to_all | solution.py:76
  249.6 10.9 %all-to-all-done.7 = bf16[8,128,128]{2,1,0:T(8,128)(2,1)S(1)} async-done(((bf16[8,128,128]{2,1,0:T(8,128)(2,1)}), bf16[8,128,128]{2,1,0:T(8,128)(2,1)S(1)}, u32[]{:S(2)}, u32[]{:S(2)}) %all-to-all-start.7) | async-done | bytes 262176 | tf_op jit(solution)/shard_map/all_to_all | solution.py:76
  (207 shorter events, 32.8 us)
Async XLA Ops:
  7.2 13.9 %copy-start = (bf16[128,64]{0,1:T(8,128)(2,1)S(1)}, bf16[128,64]{0,1:T(8,128)(2,1)}, u32[]{:S(2)}) copy-start(bf16[128,64]{0,1:T(8,128)(2,1)} %param.14) | copy-start | bytes 49156
  10.8 39.1 %copy-start.6 = (bf16[128,64]{0,1:T(8,128)(2,1)S(1)}, bf16[128,64]{0,1:T(8,128)(2,1)}, u32[]{:S(2)}) copy-start(bf16[128,64]{0,1:T(8,128)(2,1)} %param.15) | copy-start | bytes 49156
  11.5 18.9 %all-to-all-start.3 = ((bf16[8,48,256]{2,1,0:T(8,128)(2,1)}), bf16[8,48,256]{2,1,0:T(8,128)(2,1)S(1)}, u32[]{:S(2)}, u32[]{:S(2)}) async-start(bf16[8,48,256]{2,1,0:T(8,128)(2,1)} %pad_maximum_fusion), calls=%async_computation.3 | async-start | bytes 393216 | tf_op jit(solution)/shard_map/all_to_all | solution.py:76
  20.8 17.9 %copy-start.27 = (f32[128]{0:T(128)}, f32[128]{0:T(128)S(1)}, u32[]{:S(2)}) copy-start(f32[128]{0:T(128)S(1)} %get-tuple-element.129) | copy-start | bytes 1540
  21.1 17.6 %copy-start.31 = (f32[128]{0:T(128)}, f32[128]{0:T(128)S(1)}, u32[]{:S(2)}) copy-start(f32[128]{0:T(128)S(1)} %get-tuple-element.133) | copy-start | bytes 1540
  31.2 17.5 %all-to-all-start = ((bf16[16,72,256]{2,1,0:T(8,128)(2,1)}), bf16[16,72,256]{2,1,0:T(8,128)(2,1)S(1)}, u32[]{:S(2)}, u32[]{:S(2)}) async-start(bf16[16,72,256]{2,1,0:T(8,128)(2,1)} %broadcast_in_dim.128), calls=%async_computation | async-start | bytes 1179648 | tf_op jit(solution)/shard_map/all_to_all | solution.py:76
  38.7 75.0 %all-gather.3.cloned.1.call-start = ((), (), s32[]{:S(2)}) async-start(), calls=%async_computation.8 | async-start | bytes 2785280 | tf_op jit(solution)/shard_map/all_gather | solution.py:301
  50.5 18.2 %copy-start.7 = (bf16[128,256]{0,1:T(8,128)(2,1)}, bf16[128,256]{0,1:T(8,128)(2,1)S(1)}, u32[]{:S(2)}) copy-start(bf16[128,256]{0,1:T(8,128)(2,1)S(1)} %get-tuple-element.150) | copy-start | bytes 196612
  68.7 45.1 %all-to-all-start.2 = ((bf16[16,40,2048]{2,1,0:T(8,128)(2,1)}), bf16[16,40,2048]{2,1,0:T(8,128)(2,1)S(1)}, u32[]{:S(2)}, u32[]{:S(2)}) async-start(bf16[16,40,2048]{2,1,0:T(8,128)(2,1)} %broadcast_in_dim.130), calls=%async_computation.2 | async-start | bytes 5242880 | tf_op jit(solution)/shard_map/all_to_all | solution.py:76
  113.8 17.8 %collective-permute-start.2 = (bf16[640,2048]{1,0:T(8,128)(2,1)}, bf16[640,2048]{1,0:T(8,128)(2,1)}, u32[]{:S(2)}, u32[]{:S(2)}) collective-permute-start(bf16[640,2048]{1,0:T(8,128)(2,1)} %all-gather.3.cloned.1.call-done.own_ref.cot_own_ref), channel_id=1, source_target_pairs={{0,1},{1,0},{2,3},{3,2},{4,5},{5,4},{6,7},{7,6},{8,9},{9,8},{10,11... | collective-permute-start | bytes 7864328 | tf_op jit(solution)/shard_map/ppermute | solution.py:304
  113.8 13.1 %copy-start.1 = (bf16[16,40,2048]{2,1,0:T(8,128)(2,1)}, bf16[16,40,2048]{2,1,0:T(8,128)(2,1)S(1)}, u32[]{:S(2)}) copy-start(bf16[16,40,2048]{2,1,0:T(8,128)(2,1)S(1)} %all-to-all-done.2) | copy-start | bytes 7864324
  113.8 22.6 %collective-permute-start = (bf16[640,2048]{1,0:T(8,128)(2,1)S(1)}, bf16[640,2048]{1,0:T(8,128)(2,1)}, u32[]{:S(2)}, u32[]{:S(2)}) collective-permute-start(bf16[640,2048]{1,0:T(8,128)(2,1)S(1)} %bitcast.178), channel_id=1, source_target_pairs={{0,1},{1,0},{2,3},{3,2},{4,5},{5,4},{6,7},{7,6},{8,9},{9,8},{10,11... | collective-permute-start | bytes 7864328 | tf_op jit(solution)/shard_map/ppermute | solution.py:315
  114.3 8.5 %collective-permute-start.1 = (f32[8,256]{1,0:T(8,128)S(1)}, f32[8,256]{1,0:T(8,128)S(1)}, u32[]{:S(2)}, u32[]{:S(2)}) collective-permute-start(f32[8,256]{1,0:T(8,128)S(1)} %convert_reduce_fusion.2), channel_id=1, source_target_pairs={{0,1},{1,0},{2,3},{3,2},{4,5},{5,4},{6,7},{7,6},{8,9},{9,8},{10,11... | collective-permute-start | bytes 24584 | tf_op jit(solution)/shard_map/ppermute | solution.py:288
  114.5 12.4 %copy-start.10 = (f32[8,1,256]{2,1,0:T(1,128)}, f32[8,1,256]{2,1,0:T(1,128)S(1)}, u32[]{:S(2)}) copy-start(f32[8,1,256]{2,1,0:T(1,128)S(1)} %stack.14.gown_ref) | copy-start | bytes 24580
  147.0 6.3 %collective-permute-start.3 = (bf16[640,2048]{1,0:T(8,128)(2,1)}, bf16[640,2048]{1,0:T(8,128)(2,1)S(1)}, u32[]{:S(2)}, u32[]{:S(2)}) collective-permute-start(bf16[640,2048]{1,0:T(8,128)(2,1)} %back_oth.1), channel_id=1, source_target_pairs={{0,1},{1,0},{2,3},{3,2},{4,5},{5,4},{6,7},{7,6},{8,9},{9,8},{10,11... | collective-permute-start | bytes 7864328 | tf_op jit(solution)/shard_map/ppermute | solution.py:366
  147.1 5.4 %collective-permute-start.4 = (f32[640,128]{1,0:T(8,128)S(1)}, f32[640,128]{1,0:T(8,128)S(1)}, u32[]{:S(2)}, u32[]{:S(2)}) collective-permute-start(f32[640,128]{1,0:T(8,128)S(1)} %copy-done.4), channel_id=1, source_target_pairs={{0,1},{1,0},{2,3},{3,2},{4,5},{5,4},{6,7},{7,6},{8,9},{9,8},{10,11... | collective-permute-start | bytes 983048 | tf_op jit(solution)/shard_map/ppermute | solution.py:359
  204.0 15.7 %all-to-all-start.5 = ((bf16[8,40,384]{2,1,0:T(8,128)(2,1)}), bf16[8,40,384]{2,1,0:T(8,128)(2,1)S(1)}, u32[]{:S(2)}, u32[]{:S(2)}) async-start(bf16[8,40,384]{2,1,0:T(8,128)(2,1)} %sums.1), calls=%async_computation.5 | async-start | bytes 491520 | tf_op jit(solution)/shard_map/all_to_all | solution.py:76
  208.0 12.7 %copy-start.30 = (f32[128]{0:T(128)S(1)}, f32[128]{0:T(128)}, u32[]{:S(2)}) copy-start(f32[128]{0:T(128)} %copy-done.29) | copy-start | bytes 1540
  208.0 12.7 %copy-start.34 = (f32[128]{0:T(128)S(1)}, f32[128]{0:T(128)}, u32[]{:S(2)}) copy-start(f32[128]{0:T(128)} %copy-done.33) | copy-start | bytes 1540
  208.0 13.5 %copy-start.3 = (bf16[128,256]{1,0:T(8,128)(2,1)S(1)}, bf16[128,256]{1,0:T(8,128)(2,1)}, u32[]{:S(2)}) copy-start(bf16[128,256]{1,0:T(8,128)(2,1)} %param.13) | copy-start | bytes 196612
  223.3 16.8 %copy-start.17 = (f32[4]{0:T(128)S(1)}, f32[4]{0:T(128)}, u32[]{:S(2)}) copy-start(f32[4]{0:T(128)} %copy-done.16) | copy-start | bytes 52
  223.3 15.4 %all-to-all-start.6 = ((bf16[16,72,256]{2,1,0:T(8,128)(2,1)}), bf16[16,72,256]{2,1,0:T(8,128)(2,1)S(1)}, u32[]{:S(2)}, u32[]{:S(2)}) async-start(bf16[16,72,256]{2,1,0:T(8,128)(2,1)} %broadcast_in_dim.140), calls=%async_computation.6 | async-start | bytes 1179648 | tf_op jit(solution)/shard_map/all_to_all | solution.py:76
  239.1 1.4 collective-permute-start.5
  241.3 19.2 %all-to-all-start.7 = ((bf16[8,128,128]{2,1,0:T(8,128)(2,1)}), bf16[8,128,128]{2,1,0:T(8,128)(2,1)S(1)}, u32[]{:S(2)}, u32[]{:S(2)}) async-start(bf16[8,128,128]{2,1,0:T(8,128)(2,1)} %broadcast_in_dim.141), calls=%async_computation.7 | async-start | bytes 524288 | tf_op jit(solution)/shard_map/all_to_all | solution.py:76
  (27 other events, 192.7 us)
Sparse Core Ops, SparseCore 0:
  42.6 71.1 all-gather.2

commit v3 on v2

--- a/solution.py
+++ b/solution.py
@@ -78,6 +78,56 @@
 
 def to_all(x, axis):
     return swap(jnp.broadcast_to(x[None], (lax.axis_size(axis),) + x.shape), axis)
+
+
+SIDE = 4
+
+
+def along_y(step):
+    return [
+        (y * SIDE + x, (y + step) % SIDE * SIDE + x) for y in range(SIDE) for x in range(SIDE)
+    ]
+
+
+def along_x(step):
+    return [
+        (y * SIDE + x, y * SIDE + (x + step) % SIDE) for y in range(SIDE) for x in range(SIDE)
+    ]
+
+
+def gather_rows(block):
+    def spread(x, groups):
+        return lax.all_to_all(
+            jnp.broadcast_to(x[None], (SIDE,) + x.shape),
+            "ctx",
+            0,
+            0,
+            tiled=True,
+            axis_index_groups=groups,
+        )
+
+    row = spread(block, [[y * SIDE + x for x in range(SIDE)] for y in range(SIDE)])
+    return spread(row, [[y * SIDE + x for y in range(SIDE)] for x in range(SIDE)])
+
+
+def gather_cot(block):
+    here = lax.axis_index("ctx")
+    y, x = here // SIDE, here % SIDE
+    put = lax.dynamic_update_slice
+    above = [lax.ppermute(block, "ctx", along_y(step)) for step in (1, 2, 3)]
+    column = jnp.broadcast_to(block[None], (SIDE,) + block.shape)
+    for step, piece in zip((1, 2, 3), above):
+        column = put(column, piece[None], ((y + SIDE - step) % SIDE, 0, 0))
+    left = lax.ppermute(column, "ctx", along_x(1))
+    right = lax.ppermute(column, "ctx", along_x(3))
+    half = SIDE // 2
+    far_low = lax.ppermute(left[:half], "ctx", along_x(1))
+    far_high = lax.ppermute(right[half:], "ctx", along_x(3))
+    full = jnp.broadcast_to(column[:, None], (SIDE,) + column.shape)
+    full = put(full, left[:, None], (0, (x + 3) % SIDE, 0, 0))
+    full = put(full, right[:, None], (0, (x + 1) % SIDE, 0, 0))
+    full = put(full, far_low[:, None], (0, (x + 2) % SIDE, 0, 0))
+    return put(full, far_high[:, None], (half, (x + 2) % SIDE, 0, 0))
 
 
 def stacked(ref):
@@ -279,12 +329,16 @@
     cot = (dot(select, out_grad).reshape(exp_count, capacity, feat) * prob_rows[:, :, None]).astype(
         BF16
     )
+    mixer_out, output_pull = jax.vjp(
+        block_output, values, key_rows, queries, log_decay, state_in
+    )
+    hidden = (residual.astype(F32) + mixer_out).astype(BF16)
+    hidden_f = hidden.astype(F32)
+    rows = dot(select, hidden).astype(BF16).reshape(exp_count, capacity, feat)
     gain_rows = pad_rows(split_rows(norm_gain[None, :], 3), 8, feat)
-    cot_payload = jnp.concatenate(
-        [cot, jnp.broadcast_to(gain_rows[None], (exp_count,) + gain_rows.shape)], axis=1
-    )
-    got_cot = swap(cot_payload, "exp")
-    gain_own = jnp.sum(got_cot[:, capacity : capacity + 3].astype(F32), axis=1)
+    gain_rows = jnp.broadcast_to(gain_rows[None], (exp_count,) + gain_rows.shape)
+    got_rows = swap(jnp.concatenate([rows, cot, gain_rows], axis=1), "exp")
+    gain_own = jnp.sum(got_rows[:, 2 * capacity : 2 * capacity + 3].astype(F32), axis=1)
     gain_oth = lax.ppermute(gain_own, "dp", other_core)
     gain4 = jnp.where(
         core[0] == 0,
@@ -298,21 +352,12 @@
     up_scaled = (up4.astype(F32) * gain4[:, :, :, None]).astype(BF16)
     wide = exp_count * feat
     rows_all = ctx_count * capacity
-    cot_own = lax.all_gather(side_by_side(got_cot[:, :capacity]), "ctx", axis=0).reshape(
+    own = gather_rows(side_by_side(got_rows[:, :capacity])).reshape(rows_all, wide)
+    cot_own = gather_cot(side_by_side(got_rows[:, capacity : 2 * capacity])).reshape(
         rows_all, wide
     )
+    oth = lax.ppermute(own, "dp", other_core)
     cot_oth = lax.ppermute(cot_own, "dp", other_core)
-
-    mixer_out, output_pull = jax.vjp(
-        block_output, values, key_rows, queries, log_decay, state_in
-    )
-    hidden = (residual.astype(F32) + mixer_out).astype(BF16)
-    hidden_f = hidden.astype(F32)
-    got_rows = swap(
-        dot(select, hidden).astype(BF16).reshape(exp_count, capacity, feat), "exp"
-    )
-    own = to_all(side_by_side(got_rows), "ctx").reshape(rows_all, wide)
-    oth = lax.ppermute(own, "dp", other_core)
 
     split = 2
     part = rows_all // split

time: 272 us -> 266 us (0.978)
  blocking collectives: 57.1 us -> 81.1 us
  waiting for transfers between devices: 81.2 us -> 58.6 us
  between operations: 15.1 us -> 1.99 us
  starting transfers between devices: 37.5 us -> 42.8 us
  matrix products: 16.5 us -> 13.3 us
  local copies, waits for them, and re-layouts: 12.8 us -> 15.8 us
    all_gather x1 -> x0, waiting for transfers between devices: 40.1 us -> none  [per_device(): lax.all_gather(side_by_side(got_cot[:, :capacity]), 'ctx', axis=0)]
    all_to_all x0 -> x1, blocking collectives: none -> 18.9 us  [spread(): lax.all_to_all(jnp.broadcast_to(x[None], (SIDE,) + x.shape), 'ctx', 0, 0,...]
    all_to_all x0 -> x1, waiting for transfers between devices: none -> 17.3 us  [spread(): lax.all_to_all(jnp.broadcast_to(x[None], (SIDE,) + x.shape), 'ctx', 0, 0,...]
    ppermute x0 -> x7, waiting for transfers between devices: none -> 10.6 us  [the longest x3 5.57 us: gather_cot(): above = [lax.ppermute(block, 'ctx', along_y(step)) for step in (1, 2, 3)]]
    ppermute x0 -> x7, starting transfers between devices: none -> 7.61 us  [the longest x3 3.4 us: gather_cot(): above = [lax.ppermute(block, 'ctx', along_y(step)) for step in (1, 2, 3)]]
    all_to_all x6 -> x4, starting transfers between devices: 36.1 us -> 29.1 us  [swap(): return lax.all_to_all(x, axis, 0, 0, tiled=True)]
    all_to_all x6 -> x4, waiting for transfers between devices: 27.7 us -> 21.9 us  [swap(): return lax.all_to_all(x, axis, 0, 0, tiled=True)]
    all_to_all x2, blocking collectives: 57.1 us -> 62.1 us  [swap(): return lax.all_to_all(x, axis, 0, 0, tiled=True)]
  transfers between devices with their start and end apart: 13 -> 18, of which waited for: 7 -> 10; matrix products, arithmetic and copies ran while one was open for 9% -> 8% of each run, Pallas kernels for 8% -> 8%
where the time goes in v3:
time: 266 us; the launch traced here: 262 us
  blocking collectives  81.1 us (30%)
  waiting for transfers between devices  58.6 us (22%)
  starting transfers between devices  42.8 us (16%)
  Pallas kernels  39.8 us (15%)
  local copies, waits for them, and re-layouts  15.8 us (6%)
  matrix products  13.3 us (5%)
  other arithmetic  9.08 us (3%)
    all_to_all x2, blocking collectives, swap(): return lax.all_to_all(x, axis, 0, 0, tiled=True)  62.1 us
    all_to_all x4, starting transfers between devices, swap(): return lax.all_to_all(x, axis, 0, 0, tiled=True)  29.1 us
    all_to_all x4, waiting for transfers between devices, swap(): return lax.all_to_all(x, axis, 0, 0, tiled=True)  21.9 us
    all_to_all x1, blocking collectives, spread(): lax.all_to_all(jnp.broadcast_to(x[None], (SIDE,) + x.shape), 'ctx', 0, 0,...  18.9 us
    all_to_all x1, waiting for transfers between devices, spread(): lax.all_to_all(jnp.broadcast_to(x[None], (SIDE,) + x.shape), 'ctx', 0, 0,...  17.3 us
    dot_general x37, matrix products, dot(): lax.dot_general(a, b, (dims, ((), ())), precision=precision, preferred_el...  13.3 us
    pallas_call x1, Pallas kernels, per_device(): pl.pallas_call(grads_kernel, grid_spec=grid_of(1, exp_count, [columns, co...  11.6 us
    unnamed x124, local copies, waits for them, and re-layouts  8.86 us
  transfers between devices with their start and end apart: 18, of which 10 were waited for; matrix products, arithmetic and copies ran while one was open for 8% of the time, Pallas kernels for 8%

profile of v3, /device:TPU:2, one launch (start us, length us, event | category | flops | bytes accessed | tf_op | source)
XLA Modules:
  0.0 262.4 jit_solution(1257440037926834127)
XLA Ops:
  4.3 7.5 %all-to-all-start = ((bf16[16,72,256]{2,1,0:T(8,128)(2,1)}), bf16[16,72,256]{2,1,0:T(8,128)(2,1)S(1)}, u32[]{:S(2)}, u32[]{:S(2)}) async-start(bf16[16,72,256]{2,1,0:T(8,128)(2,1)} %broadcast_in_dim.167), calls=%async_computation | async-start | bytes 1179648 | tf_op jit(solution)/shard_map/all_to_all | solution.py:76
  18.7 4.0 %all-to-all-done = bf16[16,72,256]{2,1,0:T(8,128)(2,1)S(1)} async-done(((bf16[16,72,256]{2,1,0:T(8,128)(2,1)}), bf16[16,72,256]{2,1,0:T(8,128)(2,1)S(1)}, u32[]{:S(2)}, u32[]{:S(2)}) %all-to-all-start) | async-done | bytes 589856 | tf_op jit(solution)/shard_map/all_to_all | solution.py:76
  25.4 20.9 %all_to_all.40 = bf16[8,88,256]{2,1,0:T(8,128)(2,1)S(1)} all-to-all(bf16[8,88,256]{2,1,0:T(8,128)(2,1)S(1)} %pad_maximum_fusion), channel_id=1, replica_groups=mesh['ctx'=16,'exp'=8,'dp'=2] {'exp'}, dimensions={0} | all-to-all | bytes 720896 | tf_op jit(solution)/shard_map/all_to_all | solution.py:76
  50.5 4.8 %collective-permute-done.2 = bf16[40,2048]{1,0:T(8,128)(2,1)S(1)} collective-permute-done((bf16[40,2048]{1,0:T(8,128)(2,1)S(1)}, bf16[40,2048]{1,0:T(8,128)(2,1)S(1)}, u32[]{:S(2)}, u32[]{:S(2)}) %collective-permute-start.2) | collective-permute-done | bytes 163872 | tf_op jit(solution)/shard_map/ppermute | solution.py:117
  58.3 18.9 %all_to_all.41 = bf16[4,40,2048]{2,1,0:T(8,128)(2,1)S(1)} all-to-all(bf16[4,40,2048]{2,1,0:T(8,128)(2,1)S(1)} %broadcast_in_dim.177), channel_id=1, replica_groups={{0,16,32,48},{64,80,96,112},{128,144,160,176},{192,208,224,240},{1,17,3..., dimensions={0} | all-to-all | bytes 1310720 | tf_op jit(solution)/shard_map/all_to_all | solution.py:100
  79.1 4.6 %all-to-all-start.3 = ((bf16[4,4,40,2048]{3,2,1,0:T(8,128)(2,1)}), bf16[4,4,40,2048]{3,2,1,0:T(8,128)(2,1)}, u32[]{:S(2)}, u32[]{:S(2)}) async-start(bf16[4,4,40,2048]{3,2,1,0:T(8,128)(2,1)} %broadcast_in_dim.178), calls=%async_computation.3 | async-start | bytes 5242880 | tf_op jit(solution)/shard_map/all_to_all | solution.py:100
  88.1 2.9 %collective-permute-done.7 = bf16[2,40,2048]{2,1,0:T(8,128)(2,1)S(1)} collective-permute-done((bf16[2,40,2048]{2,1,0:T(8,128)(2,1)S(1)}, bf16[2,40,2048]{2,1,0:T(8,128)(2,1)S(1)}, u32[]{:S(2)}, u32[]{:S(2)}) %collective-permute-start.7) | collective-permute-done | bytes 327712 | tf_op jit(solution)/shard_map/ppermute | solution.py:124
  93.3 17.3 %all-to-all-done.3 = bf16[4,4,40,2048]{3,2,1,0:T(8,128)(2,1)} async-done(((bf16[4,4,40,2048]{3,2,1,0:T(8,128)(2,1)}), bf16[4,4,40,2048]{3,2,1,0:T(8,128)(2,1)}, u32[]{:S(2)}, u32[]{:S(2)}) %all-to-all-start.3) | async-done | bytes 2621472 | tf_op jit(solution)/shard_map/all_to_all | solution.py:100
  112.2 3.7 %collective-permute-done.1 = f32[8,256]{1,0:T(8,128)S(1)} collective-permute-done((f32[8,256]{1,0:T(8,128)S(1)}, f32[8,256]{1,0:T(8,128)S(1)}, u32[]{:S(2)}, u32[]{:S(2)}) %collective-permute-start.1) | collective-permute-done | bytes 8224 | tf_op jit(solution)/shard_map/ppermute | solution.py:342
  116.5 4.0 %multiply_convert_fusion = (bf16[8,2,256,256]{3,2,1,0:T(8,128)(2,1)}, bf16[8,2,256,256]{3,2,1,0:T(8,128)(2,1)}) fusion(bf16[8,2,256,256]{3,2,1,0:T(8,128)(2,1)} %bitcast.202, f32[8,2,256]{2,1,0:T(2,128)S(1)} %maximum_select_fusion, bf16[8,2,256,256]{3,2,1,0:T(8,128)(2,1)} %bitcast.205), kind=kLoop, calls=%fused_computation | loop fusion | flops 6291456 | bytes 8404992 | tf_op jit(solution)/shard_map/convert_element_type | solution.py:352
  120.5 4.7 %open.1 = (f32[640,256]{1,0:T(8,128)}, f32[640,256]{1,0:T(8,128)}, f32[640,128]{1,0:T(8,128)}) custom-call(s32[1]{0:T(128)} %bitcast.7.core, bf16[640,2048]{1,0:T(8,128)(2,1)} %bitcast.32.rows_ref.own_ref, bf16[8,2,256,256]{3,2,1,0:T(8,128)(2,1)} %get-tuple-element.133.wg_ref, bf16[8,2,256,256]{3,2,1,0:T(8,128)(2,1)} %get-tuple-element.132.wu_ref), custom_call_target="tpu_custom_call" | custom-call | tf_op jit(solution)/shard_map/open/pallas_call | solution.py:387
  125.2 4.8 %cot.1.ga_ref = f32[640,256]{1,0:T(8,128)} custom-call(s32[1]{0:T(128)} %bitcast.7.core, bf16[640,2048]{1,0:T(8,128)(2,1)} %bitcast.200, bf16[640,2048]{1,0:T(8,128)(2,1)} %collective-permute-done.9.oth_ref.cot_oth_ref, bf16[8,2,256,256]{3,2,1,0:T(8,128)(2,1)} %bitcast.209, bf16[8,2,256,256]{3,2,1,0:T(8,128)(2,1)} %bitcast.210), custom_call_target="tpu_custom_call" | custom-call | tf_op jit(solution)/shard_map/cot/pallas_call | solution.py:381
  130.0 5.9 %close.1 = (bf16[640,256]{1,0:T(8,128)(2,1)}, bf16[640,256]{1,0:T(8,128)(2,1)}, bf16[640,256]{1,0:T(8,128)(2,1)}, bf16[640,256]{1,0:T(8,128)(2,1)}, bf16[640,256]{1,0:T(8,128)(2,1)}, /*index=5*/f32[640,128]{1,0:T(8,128)}) custom-call(s32[1]{0:T(128)} %bitcast.7.core, bf16[640,2048]{1,0:T(8,128)(2,1)} %collective-permute-done.rows_ref.oth_ref, ...), custom_call_target="tpu_custom_call" | custom-call | tf_op jit(solution)/shard_map/close/pallas_call | solution.py:393
  135.9 4.6 %back_oth.1 = bf16[640,2048]{1,0:T(8,128)(2,1)} custom-call(s32[1]{0:T(128)} %bitcast.7.core, bf16[640,256]{1,0:T(8,128)(2,1)} %get-tuple-element.25.dg_ref, bf16[640,256]{1,0:T(8,128)(2,1)} %get-tuple-element.26.du_ref, bf16[8,2,256,256]{3,2,1,0:T(8,128)(2,1)} %bitcast.206, bf16[8,2,256,256]{3,2,1,0:T(8,128)(2,1)} %bitcast.203), custom_call_target="tpu_custom_call" | custom-call | tf_op jit(solution)/shard_map/back_oth/pallas_call | solution.py:405
  141.1 5.1 %collective-permute-done.11.sc_other_ref = f32[640,128]{1,0:T(8,128)S(1)} collective-permute-done((f32[640,128]{1,0:T(8,128)S(1)}, f32[640,128]{1,0:T(8,128)S(1)}, u32[]{:S(2)}, u32[]{:S(2)}) %collective-permute-start.11) | collective-permute-done | bytes 327712 | tf_op jit(solution)/shard_map/ppermute | solution.py:404
  148.4 5.2 %back_own.1 = bf16[640,2176]{1,0:T(8,128)(2,1)} custom-call(s32[1]{0:T(128)} %bitcast.7.core, bf16[640,256]{1,0:T(8,128)(2,1)} %get-tuple-element.25.dg_ref, bf16[640,256]{1,0:T(8,128)(2,1)} %get-tuple-element.26.du_ref, bf16[8,2,256,256]{3,2,1,0:T(8,128)(2,1)} %bitcast.207, bf16[8,2,256,256]{3,2,1,0:T(8,128)(2,1)} %bitcast.204, ...), custom_call_target="tpu_custom_call" | custom-call | tf_op jit(solution)/shard_map/back_own/pallas_call | solution.py:412
  153.6 41.3 %all_to_all.42.got_ref = bf16[16,40,2176]{2,1,0:T(8,128)(2,1)} all-to-all(bf16[16,40,2176]{2,1,0:T(8,128)(2,1)} %bitcast.208), channel_id=1, replica_groups=mesh['ctx'=16,'exp'=8,'dp'=2] {'ctx'}, dimensions={0} | all-to-all | bytes 5570560 | tf_op jit(solution)/shard_map/all_to_all | solution.py:76
  194.9 2.9 %sums.1 = bf16[8,40,384]{2,1,0:T(8,128)(2,1)} custom-call(bf16[16,40,2176]{2,1,0:T(8,128)(2,1)} %all_to_all.42.got_ref), custom_call_target="tpu_custom_call" | custom-call | tf_op jit(solution)/shard_map/sums/pallas_call | solution.py:452
  197.8 9.7 %all-to-all-start.5 = ((bf16[8,40,384]{2,1,0:T(8,128)(2,1)}), bf16[8,40,384]{2,1,0:T(8,128)(2,1)S(1)}, u32[]{:S(2)}, u32[]{:S(2)}) async-start(bf16[8,40,384]{2,1,0:T(8,128)(2,1)} %sums.1), calls=%async_computation.5 | async-start | bytes 491520 | tf_op jit(solution)/shard_map/all_to_all | solution.py:76
  208.1 11.6 %grads.1 = (bf16[8,2,256,256]{3,2,1,0:T(8,128)(2,1)}, bf16[8,2,256,256]{3,2,1,0:T(8,128)(2,1)}, bf16[8,2,256,256]{3,2,1,0:T(8,128)(2,1)}) custom-call(s32[1]{0:T(128)} %bitcast.7.core, bf16[640,2048]{1,0:T(8,128)(2,1)} %bitcast.32.rows_ref.own_ref, bf16[640,2048]{1,0:T(8,128)(2,1)} %collective-permute-done.rows_ref.oth_ref, bf16[640,2048]{1,0:T(8,128)(2,1)} %bitcast.201, ...), custom_call_target="tpu_custom_call" | custom-call | tf_op jit(solution)/shard_map/grads/pallas_call | solution.py:427
  223.4 5.0 %all-to-all-start.6 = ((bf16[16,72,256]{2,1,0:T(8,128)(2,1)}), bf16[16,72,256]{2,1,0:T(8,128)(2,1)S(1)}, u32[]{:S(2)}, u32[]{:S(2)}) async-start(bf16[16,72,256]{2,1,0:T(8,128)(2,1)} %broadcast_in_dim.189), calls=%async_computation.6 | async-start | bytes 1179648 | tf_op jit(solution)/shard_map/all_to_all | solution.py:76
  231.8 7.0 %all-to-all-done.6 = bf16[16,72,256]{2,1,0:T(8,128)(2,1)S(1)} async-done(((bf16[16,72,256]{2,1,0:T(8,128)(2,1)}), bf16[16,72,256]{2,1,0:T(8,128)(2,1)S(1)}, u32[]{:S(2)}, u32[]{:S(2)}) %all-to-all-start.6) | async-done | bytes 589856 | tf_op jit(solution)/shard_map/all_to_all | solution.py:76
  241.4 7.0 %all-to-all-start.7 = ((bf16[8,128,128]{2,1,0:T(8,128)(2,1)}), bf16[8,128,128]{2,1,0:T(8,128)(2,1)S(1)}, u32[]{:S(2)}, u32[]{:S(2)}) async-start(bf16[8,128,128]{2,1,0:T(8,128)(2,1)} %broadcast_in_dim.190), calls=%async_computation.7 | async-start | bytes 524288 | tf_op jit(solution)/shard_map/all_to_all | solution.py:76
  250.0 10.9 %all-to-all-done.7 = bf16[8,128,128]{2,1,0:T(8,128)(2,1)S(1)} async-done(((bf16[8,128,128]{2,1,0:T(8,128)(2,1)}), bf16[8,128,128]{2,1,0:T(8,128)(2,1)S(1)}, u32[]{:S(2)}, u32[]{:S(2)}) %all-to-all-start.7) | async-done | bytes 262176 | tf_op jit(solution)/shard_map/all_to_all | solution.py:76
  (255 shorter events, 46.2 us)
Async XLA Ops:
  1.6 23.7 %copy-start.22 = (f32[128,4]{0,1:T(4,128)}, f32[128,4]{0,1:T(4,128)S(1)}, u32[]{:S(2)}) copy-start(f32[128,4]{0,1:T(4,128)S(1)} %fusion.39) | copy-start | bytes 6148
  2.0 23.3 %copy-start.28 = (pred[4,256]{1,0:T(4,128)(4,1)}, pred[4,256]{1,0:T(4,128)(4,1)S(1)}, u32[]{:S(2)}) copy-start(pred[4,256]{1,0:T(4,128)(4,1)S(1)} %iota_compare_fusion.10) | copy-start | bytes 3076
  4.3 18.4 %all-to-all-start = ((bf16[16,72,256]{2,1,0:T(8,128)(2,1)}), bf16[16,72,256]{2,1,0:T(8,128)(2,1)S(1)}, u32[]{:S(2)}, u32[]{:S(2)}) async-start(bf16[16,72,256]{2,1,0:T(8,128)(2,1)} %broadcast_in_dim.167), calls=%async_computation | async-start | bytes 1179648 | tf_op jit(solution)/shard_map/all_to_all | solution.py:76
  18.1 28.9 %copy-start.20 = (pred[320,128]{1,0:T(32,128)(4,1)}, pred[320,128]{1,0:T(32,128)(4,1)S(1)}, u32[]{:S(2)}) copy-start(pred[320,128]{1,0:T(32,128)(4,1)S(1)} %get-tuple-element.134) | copy-start | bytes 122884
  23.8 26.6 %copy-start.12 = (f32[64,256]{1,0:T(8,128)}, f32[64,256]{1,0:T(8,128)S(1)}, u32[]{:S(2)}) copy-start(f32[64,256]{1,0:T(8,128)S(1)} %multiply_reduce_fusion.1) | copy-start | bytes 196612
  25.1 25.4 %copy-start.18 = (bf16[128,256]{0,1:T(8,128)(2,1)}, bf16[128,256]{0,1:T(8,128)(2,1)S(1)}, u32[]{:S(2)}) copy-start(bf16[128,256]{0,1:T(8,128)(2,1)S(1)} %get-tuple-element.166) | copy-start | bytes 196612
  47.0 8.3 %collective-permute-start.2 = (bf16[40,2048]{1,0:T(8,128)(2,1)S(1)}, bf16[40,2048]{1,0:T(8,128)(2,1)S(1)}, u32[]{:S(2)}, u32[]{:S(2)}) collective-permute-start(bf16[40,2048]{1,0:T(8,128)(2,1)S(1)} %get-tuple-element.112), channel_id=1, source_target_pairs={{0,64},{16,80},{32,96},{48,112},{64,128},{80,144},{96,160},{112,17... | collective-permute-start | bytes 491528 | tf_op jit(solution)/shard_map/ppermute | solution.py:117
  47.0 8.3 %collective-permute-start.3 = (bf16[40,2048]{1,0:T(8,128)(2,1)S(1)}, bf16[40,2048]{1,0:T(8,128)(2,1)S(1)}, u32[]{:S(2)}, u32[]{:S(2)}) collective-permute-start(bf16[40,2048]{1,0:T(8,128)(2,1)S(1)} %get-tuple-element.112), channel_id=1, source_target_pairs={{0,128},{16,144},{32,160},{48,176},{64,192},{80,208},{96,224},{112... | collective-permute-start | bytes 491528 | tf_op jit(solution)/shard_map/ppermute | solution.py:117
  49.3 6.9 %collective-permute-start.4 = (bf16[40,2048]{1,0:T(8,128)(2,1)S(1)}, bf16[40,2048]{1,0:T(8,128)(2,1)S(1)}, u32[]{:S(2)}, u32[]{:S(2)}) collective-permute-start(bf16[40,2048]{1,0:T(8,128)(2,1)S(1)} %get-tuple-element.112), channel_id=1, source_target_pairs={{0,192},{16,208},{32,224},{48,240},{64,0},{80,16},{96,32},{112,48}... | collective-permute-start | bytes 491528 | tf_op jit(solution)/shard_map/ppermute | solution.py:117
  56.2 27.6 %collective-permute-start.5 = (bf16[4,40,2048]{2,1,0:T(8,128)(2,1)S(1)}, bf16[4,40,2048]{2,1,0:T(8,128)(2,1)S(1)}, u32[]{:S(2)}, u32[]{:S(2)}) collective-permute-start(bf16[4,40,2048]{2,1,0:T(8,128)(2,1)S(1)} %bitcast_dynamic-update-slice_fusion.4), channel_id=1, source_target_pairs={{0,16},{16,32},{32,48},{48,0},{64,80},{80,96},{96,112},{112,64},{1... | collective-permute-start | bytes 1966088 | tf_op jit(solution)/shard_map/ppermute | solution.py:121
  57.2 26.9 %collective-permute-start.6 = (bf16[4,40,2048]{2,1,0:T(8,128)(2,1)S(1)}, bf16[4,40,2048]{2,1,0:T(8,128)(2,1)S(1)}, u32[]{:S(2)}, u32[]{:S(2)}) collective-permute-start(bf16[4,40,2048]{2,1,0:T(8,128)(2,1)S(1)} %bitcast_dynamic-update-slice_fusion.4), channel_id=1, source_target_pairs={{0,48},{16,0},{32,16},{48,32},{64,112},{80,64},{96,80},{112,96},{1... | collective-permute-start | bytes 1966088 | tf_op jit(solution)/shard_map/ppermute | solution.py:122
  79.1 31.5 %all-to-all-start.3 = ((bf16[4,4,40,2048]{3,2,1,0:T(8,128)(2,1)}), bf16[4,4,40,2048]{3,2,1,0:T(8,128)(2,1)}, u32[]{:S(2)}, u32[]{:S(2)}) async-start(bf16[4,4,40,2048]{3,2,1,0:T(8,128)(2,1)} %broadcast_in_dim.178), calls=%async_computation.3 | async-start | bytes 5242880 | tf_op jit(solution)/shard_map/all_to_all | solution.py:100
  83.8 7.2 %collective-permute-start.7 = (bf16[2,40,2048]{2,1,0:T(8,128)(2,1)S(1)}, bf16[2,40,2048]{2,1,0:T(8,128)(2,1)S(1)}, u32[]{:S(2)}, u32[]{:S(2)}) collective-permute-start(bf16[2,40,2048]{2,1,0:T(8,128)(2,1)S(1)} %slice.241), channel_id=1, source_target_pairs={{0,16},{16,32},{32,48},{48,0},{64,80},{80,96},{96,112},{112,64},{1... | collective-permute-start | bytes 983048 | tf_op jit(solution)/shard_map/ppermute | solution.py:124
  85.0 8.2 %collective-permute-start.8 = (bf16[2,40,2048]{2,1,0:T(8,128)(2,1)S(1)}, bf16[2,40,2048]{2,1,0:T(8,128)(2,1)S(1)}, u32[]{:S(2)}, u32[]{:S(2)}) collective-permute-start(bf16[2,40,2048]{2,1,0:T(8,128)(2,1)S(1)} %slice.242), channel_id=1, source_target_pairs={{0,48},{16,0},{32,16},{48,32},{64,112},{80,64},{96,80},{112,96},{1... | collective-permute-start | bytes 983048 | tf_op jit(solution)/shard_map/ppermute | solution.py:125
  93.2 27.3 %copy-start.1 = (bf16[4,4,40,2048]{3,2,1,0:T(8,128)(2,1)}, bf16[4,4,40,2048]{3,2,1,0:T(8,128)(2,1)S(1)}, u32[]{:S(2)}) copy-start(bf16[4,4,40,2048]{3,2,1,0:T(8,128)(2,1)S(1)} %bitcast_dynamic-update-slice_fusion.3) | copy-start | bytes 7864324
  93.2 32.0 %collective-permute-start.9 = (bf16[640,2048]{1,0:T(8,128)(2,1)S(1)}, bf16[640,2048]{1,0:T(8,128)(2,1)}, u32[]{:S(2)}, u32[]{:S(2)}) collective-permute-start(bf16[640,2048]{1,0:T(8,128)(2,1)S(1)} %bitcast.199), channel_id=1, source_target_pairs={{0,1},{1,0},{2,3},{3,2},{4,5},{5,4},{6,7},{7,6},{8,9},{9,8},{10,11... | collective-permute-start | bytes 7864328 | tf_op jit(solution)/shard_map/ppermute | solution.py:360
  110.6 19.4 %collective-permute-start = (bf16[640,2048]{1,0:T(8,128)(2,1)}, bf16[640,2048]{1,0:T(8,128)(2,1)}, u32[]{:S(2)}, u32[]{:S(2)}) collective-permute-start(bf16[640,2048]{1,0:T(8,128)(2,1)} %bitcast.32.rows_ref.own_ref), channel_id=1, source_target_pairs={{0,1},{1,0},{2,3},{3,2},{4,5},{5,4},{6,7},{7,6},{8,9},{9,8},{10,11... | collective-permute-start | bytes 7864328 | tf_op jit(solution)/shard_map/ppermute | solution.py:359
  111.4 4.5 %collective-permute-start.1 = (f32[8,256]{1,0:T(8,128)S(1)}, f32[8,256]{1,0:T(8,128)S(1)}, u32[]{:S(2)}, u32[]{:S(2)}) collective-permute-start(f32[8,256]{1,0:T(8,128)S(1)} %convert_reduce_fusion.2), channel_id=1, source_target_pairs={{0,1},{1,0},{2,3},{3,2},{4,5},{5,4},{6,7},{7,6},{8,9},{9,8},{10,11... | collective-permute-start | bytes 24584 | tf_op jit(solution)/shard_map/ppermute | solution.py:342
  140.6 5.6 %collective-permute-start.10 = (bf16[640,2048]{1,0:T(8,128)(2,1)}, bf16[640,2048]{1,0:T(8,128)(2,1)S(1)}, u32[]{:S(2)}, u32[]{:S(2)}) collective-permute-start(bf16[640,2048]{1,0:T(8,128)(2,1)} %back_oth.1), channel_id=1, source_target_pairs={{0,1},{1,0},{2,3},{3,2},{4,5},{5,4},{6,7},{7,6},{8,9},{9,8},{10,11... | collective-permute-start | bytes 7864328 | tf_op jit(solution)/shard_map/ppermute | solution.py:411
  140.7 5.5 %collective-permute-start.11 = (f32[640,128]{1,0:T(8,128)S(1)}, f32[640,128]{1,0:T(8,128)S(1)}, u32[]{:S(2)}, u32[]{:S(2)}) collective-permute-start(f32[640,128]{1,0:T(8,128)S(1)} %copy-done.14), channel_id=1, source_target_pairs={{0,1},{1,0},{2,3},{3,2},{4,5},{5,4},{6,7},{7,6},{8,9},{9,8},{10,11... | collective-permute-start | bytes 983048 | tf_op jit(solution)/shard_map/ppermute | solution.py:404
  197.8 21.9 %all-to-all-start.5 = ((bf16[8,40,384]{2,1,0:T(8,128)(2,1)}), bf16[8,40,384]{2,1,0:T(8,128)(2,1)S(1)}, u32[]{:S(2)}, u32[]{:S(2)}) async-start(bf16[8,40,384]{2,1,0:T(8,128)(2,1)} %sums.1), calls=%async_computation.5 | async-start | bytes 491520 | tf_op jit(solution)/shard_map/all_to_all | solution.py:76
  223.4 15.4 %all-to-all-start.6 = ((bf16[16,72,256]{2,1,0:T(8,128)(2,1)}), bf16[16,72,256]{2,1,0:T(8,128)(2,1)S(1)}, u32[]{:S(2)}, u32[]{:S(2)}) async-start(bf16[16,72,256]{2,1,0:T(8,128)(2,1)} %broadcast_in_dim.189), calls=%async_computation.6 | async-start | bytes 1179648 | tf_op jit(solution)/shard_map/all_to_all | solution.py:76
  239.1 1.4 collective-permute-start.12
  241.4 19.5 %all-to-all-start.7 = ((bf16[8,128,128]{2,1,0:T(8,128)(2,1)}), bf16[8,128,128]{2,1,0:T(8,128)(2,1)S(1)}, u32[]{:S(2)}, u32[]{:S(2)}) async-start(bf16[8,128,128]{2,1,0:T(8,128)(2,1)} %broadcast_in_dim.190), calls=%async_computation.7 | async-start | bytes 524288 | tf_op jit(solution)/shard_map/all_to_all | solution.py:76
  (49 other events, 391.7 us)

commit v4 on v3

--- a/solution.py
+++ b/solution.py
@@ -128,6 +128,45 @@
     full = put(full, right[:, None], (0, (x + 1) % SIDE, 0, 0))
     full = put(full, far_low[:, None], (0, (x + 2) % SIDE, 0, 0))
     return put(full, far_high[:, None], (half, (x + 2) % SIDE, 0, 0))
+
+
+def sum_low(blocks):
+    groups_y = [[y * SIDE + x for y in range(SIDE)] for x in range(SIDE)]
+    groups_x = [[y * SIDE + x for x in range(SIDE)] for y in range(SIDE)]
+    got = lax.all_to_all(blocks, "ctx", 0, 0, tiled=True, axis_index_groups=groups_y)
+    part = jnp.sum(got.astype(F32), axis=0).astype(BF16)
+    return lax.all_to_all(part, "ctx", 0, 0, tiled=True, axis_index_groups=groups_x)
+
+
+def sum_high(blocks):
+    here = lax.axis_index("ctx")
+    y, x = here // SIDE, here % SIDE
+    half = SIDE // 2
+
+    def column(step, start=0, count=SIDE):
+        piece = lax.dynamic_slice(
+            blocks, (start, (x + step) % SIDE, 0, 0), (count, 1) + blocks.shape[2:]
+        )
+        return piece[:, 0]
+
+    def added(a, b):
+        return (a.astype(F32) + b.astype(F32)).astype(BF16)
+
+    low = lax.ppermute(column(2, 0, half), "ctx", along_x(1))
+    high = lax.ppermute(column(2, half, half), "ctx", along_x(3))
+    right = jnp.concatenate([added(column(1, 0, half), low), column(1, half, half)])
+    left = jnp.concatenate([column(3, 0, half), added(column(3, half, half), high)])
+    got_left = lax.ppermute(right, "ctx", along_x(1))
+    got_right = lax.ppermute(left, "ctx", along_x(3))
+    part = column(0).astype(F32) + got_left.astype(F32) + got_right.astype(F32)
+    part = part.astype(BF16)
+    pieces = [
+        lax.dynamic_index_in_dim(part, (y + step) % SIDE, 0, keepdims=False)
+        for step in range(SIDE)
+    ]
+    return pieces[:1] + [
+        lax.ppermute(pieces[step], "ctx", along_y(step)) for step in (1, 2, 3)
+    ]
 
 
 def stacked(ref):
@@ -179,8 +218,12 @@
     )
 
 
-def cot_kernel(core, own_ref, oth_ref, w_own_ref, w_oth_ref, ga_ref):
-    ga_ref[...] = dot(own_ref[...], stacked(w_own_ref)) + dot(oth_ref[...], stacked(w_oth_ref))
+def near_kernel(core, rows_ref, w_ref, ga_ref):
+    ga_ref[...] = dot(rows_ref[...], stacked(w_ref))
+
+
+def far_kernel(core, rows_ref, w_ref, ga_in, ga_ref):
+    ga_ref[...] = ga_in[...] + dot(rows_ref[...], stacked(w_ref))
 
 
 def back_term(dg_ref, du_ref, wg_ref, wu_ref, block):
@@ -197,46 +240,48 @@
 
 
 def back_add_kernel(
-    ctx_count, core, dg_ref, du_ref, wg_ref, wu_ref, other_ref, sc_ref, sc_other_ref, out_ref
+    ctx_count, core, dg_ref, du_ref, wg_ref, wu_ref, other_ref, sc_ref, sc_other_ref,
+    low_ref, high_ref,
 ):
     feat = wg_ref.shape[1]
-    width = wg_ref.shape[0] * feat
+    width = wg_ref.shape[0] // 2 * feat
     for block in range(wg_ref.shape[0]):
         lanes = slice(block * feat, (block + 1) * feat)
         term = back_term(dg_ref, du_ref, wg_ref, wu_ref, block).astype(BF16).astype(F32)
-        out_ref[:, lanes] = (term + other_ref[:, lanes].astype(F32)).astype(BF16)
+        both = (term + other_ref[:, lanes].astype(F32)).astype(BF16)
+        if block * feat < width:
+            low_ref[:, lanes] = both
+        else:
+            high_ref[:, block * feat - width : (block + 1) * feat - width] = both
     small = sc_ref[...] + sc_other_ref[...]
     lane = lax.broadcasted_iota(jnp.int32, small.shape, 1)
     small = jnp.where(lane == 2, small * (0.5 / ctx_count), small)
     head = small.astype(BF16).astype(F32)
     tail = pltpu.roll(small - head, 3, 1)
-    out_ref[:, width:] = jnp.where(lane < 3, head, jnp.where(lane < 6, tail, 0.0)).astype(BF16)
-
-
-def grads_kernel(
-    core, own_ref, oth_ref, cot_own_ref, cot_oth_ref, gown_ref, goth_ref, dgi_ref, dui_ref,
-    hact_ref, gate_ref, up_ref, down_ref,
-):
+    low_ref[:, width:] = jnp.where(lane < 3, head, jnp.where(lane < 6, tail, 0.0)).astype(BF16)
+
+
+def scaled_grads_kernel(core, own_ref, oth_ref, gown_ref, goth_ref, act_ref, out_ref):
     here = core[0]
-    first = ((0,), (0,))
-    for rows_ref, cot_ref, gain_ref, place in (
-        (own_ref, cot_own_ref, gown_ref, here),
-        (oth_ref, cot_oth_ref, goth_ref, 1 - here),
-    ):
+    for rows_ref, gain_ref, place in ((own_ref, gown_ref, here), (oth_ref, goth_ref, 1 - here)):
         scaled = (rows_ref[...].astype(F32) * gain_ref[...]).astype(BF16)
-        gate_ref[place] = dot(scaled, dgi_ref[...], first).astype(BF16)
-        up_ref[place] = dot(scaled, dui_ref[...], first).astype(BF16)
-        down_ref[place] = dot(cot_ref[...], hact_ref[...], first).astype(BF16)
-
-
-def sums_kernel(got_ref, out_ref):
+        out_ref[place] = dot(scaled, act_ref[...], ((0,), (0,))).astype(BF16)
+
+
+def plain_grads_kernel(core, own_ref, oth_ref, act_ref, out_ref):
+    here = core[0]
+    out_ref[here] = dot(own_ref[...], act_ref[...], ((0,), (0,))).astype(BF16)
+    out_ref[1 - here] = dot(oth_ref[...], act_ref[...], ((0,), (0,))).astype(BF16)
+
+
+def sums_kernel(low_ref, h0_ref, h1_ref, h2_ref, h3_ref, out_ref):
     feat = out_ref.shape[2] - 128
-    count = out_ref.shape[0]
+    count = out_ref.shape[0] // 2
 
     def total(start, width):
-        acc = got_ref[0, :, start : start + width].astype(F32)
-        for block in range(1, got_ref.shape[0]):
-            acc += got_ref[block, :, start : start + width].astype(F32)
+        acc = low_ref[0, :, start : start + width].astype(F32)
+        for block in range(1, low_ref.shape[0]):
+            acc += low_ref[block, :, start : start + width].astype(F32)
         return acc
 
     small = total(count * feat, 128)
@@ -247,6 +292,12 @@
     for block in range(count):
         out_ref[block, :, :feat] = total(block * feat, feat).astype(BF16)
         out_ref[block, :, feat:] = small
+        lanes = slice(block * feat, (block + 1) * feat)
+        high = h0_ref[:, lanes].astype(F32)
+        for ref in (h1_ref, h2_ref, h3_ref):
+            high += ref[:, lanes].astype(F32)
+        out_ref[count + block, :, :feat] = high.astype(BF16)
+        out_ref[count + block, :, feat:] = small
 
 
 def whole(shape):
@@ -379,11 +430,17 @@
         )
 
     grad_act = pl.pallas_call(
-        cot_kernel,
-        grid_spec=grid_of(1, split, [rows_spec, rows_spec, w_own, w_oth], acts),
+        near_kernel,
+        grid_spec=grid_of(1, split, [rows_spec, w_own], acts),
         out_shape=acts_f,
-        name="cot",
-    )(core, cot_own, cot_oth, down4, down4)
+        name="cot_near",
+    )(core, cot_own, down4)
+    grad_act = pl.pallas_call(
+        far_kernel,
+        grid_spec=grid_of(1, split, [rows_spec, w_oth, acts], acts),
+        out_shape=acts_f,
+        name="cot_far",
+    )(core, cot_oth, down4, grad_act)
     ag, au, ss = pl.pallas_call(
         open_kernel,
         grid_spec=grid_of(1, split, [rows_spec, w_own, w_own], [acts, acts, sums]),
@@ -409,52 +466,57 @@
         name="back_oth",
     )(core, dg, du, gate4, up4)
     back_got = lax.ppermute(back_oth, "dp", other_core)
-    back = pl.pallas_call(
+    narrow = wide // 2
+    low, high = pl.pallas_call(
         functools.partial(back_add_kernel, ctx_count),
         grid_spec=grid_of(
             1,
             split,
             [acts, acts, w_own, w_own, rows_spec, sums, sums],
-            pl.BlockSpec((part, wide + 128), lambda i, *_: (i, 0)),
+            [
+                pl.BlockSpec((part, narrow + 128), lambda i, *_: (i, 0)),
+                pl.BlockSpec((part, narrow), lambda i, *_: (i, 0)),
+            ],
         ),
-        out_shape=jax.ShapeDtypeStruct((rows_all, wide + 128), BF16),
+        out_shape=[
+            jax.ShapeDtypeStruct((rows_all, narrow + 128), BF16),
+            jax.ShapeDtypeStruct((rows_all, narrow), BF16),
+        ],
         name="back_own",
     )(core, dg, du, gate4, up4, back_got, scal, scal_got)
     columns = pl.BlockSpec((rows_all, feat), lambda e, *_: (0, e))
     gain_spec = pl.BlockSpec((None, 1, feat), lambda e, *_: (e, 0, 0))
     w_pair = pl.BlockSpec((None, 2, feat, units), lambda e, *_: (e, 0, 0, 0))
     acts_all = whole((rows_all, units))
-    gate_grad, up_grad, down_grad = pl.pallas_call(
-        grads_kernel,
-        grid_spec=grid_of(
-            1,
-            exp_count,
-            [
-                columns,
-                columns,
-                columns,
-                columns,
-                gain_spec,
-                gain_spec,
-                acts_all,
-                acts_all,
-                acts_all,
-            ],
-            [w_pair] * 3,
-        ),
-        out_shape=[jax.ShapeDtypeStruct(gate4.shape, BF16)] * 3,
-        name="grads",
-    )(
-        core, own, oth, cot_own, cot_oth, gain_own[:, None], gain_oth[:, None], dgi, dui, hact
-    )
-
-    got_sums = swap(back.reshape(ctx_count, capacity, wide + 128), "ctx")
+    grads_shape = jax.ShapeDtypeStruct(gate4.shape, BF16)
+
+    def scaled_grads(act):
+        return pl.pallas_call(
+            scaled_grads_kernel,
+            grid_spec=grid_of(
+                1, exp_count, [columns, columns, gain_spec, gain_spec, acts_all], w_pair
+            ),
+            out_shape=grads_shape,
+        )(core, own, oth, gain_own[:, None], gain_oth[:, None], act)
+
+    gate_grad = scaled_grads(dgi)
+    up_grad = scaled_grads(dui)
+    down_grad = pl.pallas_call(
+        plain_grads_kernel,
+        grid_spec=grid_of(1, exp_count, [columns, columns, acts_all], w_pair),
+        out_shape=grads_shape,
+        name="down_grads",
+    )(core, cot_own, cot_oth, hact)
+
+    low = sum_low(low.reshape(SIDE, SIDE, capacity, narrow + 128))
+    high = sum_high(high.reshape(SIDE, SIDE, capacity, narrow))
     summed = pl.pallas_call(
         sums_kernel,
         out_shape=jax.ShapeDtypeStruct((exp_count, capacity, feat + 128), BF16),
         name="sums",
-    )(got_sums)
-    got_back = swap(summed, "exp").reshape(exp_count * capacity, feat + 128)
+    )(low, *high)
+    got_back = swap(summed, "exp")
+    got_back = got_back.reshape(exp_count * capacity, feat + 128)
     grad_normed = dot(select, got_back[:, :feat], ((0,), (0,)))
     small = dot(select_each, got_back[:, feat:], ((0,), (0,)))
     small = small[:, :3] + small[:, 3:6]
@@ -486,7 +548,8 @@
     vals_second, keys_second, decay_second = state_pull((grad_total, grad_state))
     both = jnp.concatenate([keys_first + keys_second, queries_part], axis=1).astype(BF16)
     both = (both.astype(F32) + lax.ppermute(both, "dp", other_core).astype(F32)).astype(BF16)
-    both = jnp.sum(to_all(both, "exp").astype(F32), axis=0)
+    both = to_all(both, "exp")
+    both = jnp.sum(both.astype(F32), axis=0)
     return (
         grad_hidden.astype(BF16),
         (vals_first + vals_second).astype(BF16),

time: 266 us -> 280 us (1.053)
  blocking collectives: 81.1 us -> 39.8 us
  starting transfers between devices: 42.8 us -> 61.6 us
  Pallas kernels: 39.8 us -> 53.5 us
  waiting for transfers between devices: 58.6 us -> 67.7 us
  local copies, waits for them, and re-layouts: 15.8 us -> 24.8 us
  other arithmetic: 9.08 us -> 13 us
    all_to_all x2 -> x1, blocking collectives: 62.1 us -> 20.9 us  [swap(): return lax.all_to_all(x, axis, 0, 0, tiled=True)]
    pallas_call x2 -> x5, Pallas kernels: 16.4 us -> 31.1 us  [the longest x2 16.2 us: scaled_grads(): pl.pallas_call(scaled_grads_kernel, grid_spec=grid_of(1, exp_count, [colu...]
    all_to_all x0 -> x2, waiting for transfers between devices: none -> 9.22 us  [the longest x1 9.22 us: sum_low(): lax.all_to_all(blocks, 'ctx', 0, 0, tiled=True, axis_index_groups=groups_y)]
    all_to_all x0 -> x2, starting transfers between devices: none -> 8.89 us  [the longest x1 5.19 us: sum_low(): lax.all_to_all(part, 'ctx', 0, 0, tiled=True, axis_index_groups=groups_x)]
    ppermute x0 -> x7, waiting for transfers between devices: none -> 8.74 us  [the longest x1 4.25 us: sum_high(): low = lax.ppermute(column(2, 0, half), 'ctx', along_x(1))]
    ppermute x0 -> x7, starting transfers between devices: none -> 7.95 us  [the longest x3 3.24 us: sum_high(): lax.ppermute(pieces[step], 'ctx', along_y(step))]
    ppermute x1, waiting for transfers between devices: 2.86 us -> 0.01 us  [gather_cot(): far_low = lax.ppermute(left[:half], 'ctx', along_x(1))]
    unnamed x124 -> x120, local copies, waits for them, and re-layouts: 8.86 us -> 8.22 us
  transfers between devices with their start and end apart: 18 -> 27, of which waited for: 10 -> 14; matrix products, arithmetic and copies ran while one was open for 8% -> 13% of each run, Pallas kernels for 8% -> 13%
where the time goes in v4:
time: 280 us; the launch traced here: 276 us
  waiting for transfers between devices  67.7 us (24%)
  starting transfers between devices  61.6 us (22%)
  Pallas kernels  53.5 us (19%)
  blocking collectives  39.8 us (14%)
  local copies, waits for them, and re-layouts  24.8 us (9%)
  matrix products  14 us (5%)
  other arithmetic  13 us (5%)
    all_to_all x4, starting transfers between devices, swap(): return lax.all_to_all(x, axis, 0, 0, tiled=True)  31.8 us
    all_to_all x1, blocking collectives, swap(): return lax.all_to_all(x, axis, 0, 0, tiled=True)  20.9 us
    all_to_all x4, waiting for transfers between devices, swap(): return lax.all_to_all(x, axis, 0, 0, tiled=True)  20.7 us
    all_to_all x1, blocking collectives, spread(): lax.all_to_all(jnp.broadcast_to(x[None], (SIDE,) + x.shape), 'ctx', 0, 0,...  18.9 us
    pallas_call x2, Pallas kernels, scaled_grads(): pl.pallas_call(scaled_grads_kernel, grid_spec=grid_of(1, exp_count, [colu...  16.2 us
    all_to_all x1, waiting for transfers between devices, spread(): lax.all_to_all(jnp.broadcast_to(x[None], (SIDE,) + x.shape), 'ctx', 0, 0,...  14.9 us
    dot_general x37, matrix products, dot(): lax.dot_general(a, b, (dims, ((), ())), precision=precision, preferred_el...  14 us
    all_to_all x1, waiting for transfers between devices, sum_low(): lax.all_to_all(blocks, 'ctx', 0, 0, tiled=True, axis_index_groups=groups_y)  9.22 us
  transfers between devices with their start and end apart: 27, of which 14 were waited for; matrix products, arithmetic and copies ran while one was open for 13% of the time, Pallas kernels for 13%

profile of v4, /device:TPU:2, one launch (start us, length us, event | category | flops | bytes accessed | tf_op | source)
XLA Modules:
  0.0 276.2 jit_solution(11075771513179391519)
XLA Ops:
  4.3 7.5 %all-to-all-start = ((bf16[16,72,256]{2,1,0:T(8,128)(2,1)}), bf16[16,72,256]{2,1,0:T(8,128)(2,1)S(1)}, u32[]{:S(2)}, u32[]{:S(2)}) async-start(bf16[16,72,256]{2,1,0:T(8,128)(2,1)} %broadcast_in_dim.169), calls=%async_computation | async-start | bytes 1179648 | tf_op jit(solution)/shard_map/all_to_all | solution.py:76
  18.6 4.1 %all-to-all-done = bf16[16,72,256]{2,1,0:T(8,128)(2,1)S(1)} async-done(((bf16[16,72,256]{2,1,0:T(8,128)(2,1)}), bf16[16,72,256]{2,1,0:T(8,128)(2,1)S(1)}, u32[]{:S(2)}, u32[]{:S(2)}) %all-to-all-start) | async-done | bytes 589856 | tf_op jit(solution)/shard_map/all_to_all | solution.py:76
  25.4 20.9 %all_to_all.45 = bf16[8,88,256]{2,1,0:T(8,128)(2,1)S(1)} all-to-all(bf16[8,88,256]{2,1,0:T(8,128)(2,1)S(1)} %pad_maximum_fusion), channel_id=1, replica_groups=mesh['ctx'=16,'exp'=8,'dp'=2] {'exp'}, dimensions={0} | all-to-all | bytes 720896 | tf_op jit(solution)/shard_map/all_to_all | solution.py:76
  50.5 4.8 %collective-permute-done.2 = bf16[40,2048]{1,0:T(8,128)(2,1)S(1)} collective-permute-done((bf16[40,2048]{1,0:T(8,128)(2,1)S(1)}, bf16[40,2048]{1,0:T(8,128)(2,1)S(1)}, u32[]{:S(2)}, u32[]{:S(2)}) %collective-permute-start.2) | collective-permute-done | bytes 163872 | tf_op jit(solution)/shard_map/ppermute | solution.py:117
  58.4 18.9 %all_to_all.46 = bf16[4,40,2048]{2,1,0:T(8,128)(2,1)S(1)} all-to-all(bf16[4,40,2048]{2,1,0:T(8,128)(2,1)S(1)} %broadcast_in_dim.179), channel_id=1, replica_groups={{0,16,32,48},{64,80,96,112},{128,144,160,176},{192,208,224,240},{1,17,3..., dimensions={0} | all-to-all | bytes 1310720 | tf_op jit(solution)/shard_map/all_to_all | solution.py:100
  79.1 3.9 %all-to-all-start.3 = ((bf16[4,4,40,2048]{3,2,1,0:T(8,128)(2,1)}), bf16[4,4,40,2048]{3,2,1,0:T(8,128)(2,1)S(1)}, u32[]{:S(2)}, u32[]{:S(2)}) async-start(bf16[4,4,40,2048]{3,2,1,0:T(8,128)(2,1)} %broadcast_in_dim.180), calls=%async_computation.3 | async-start | bytes 5242880 | tf_op jit(solution)/shard_map/all_to_all | solution.py:100
  94.7 14.9 %all-to-all-done.3 = bf16[4,4,40,2048]{3,2,1,0:T(8,128)(2,1)S(1)} async-done(((bf16[4,4,40,2048]{3,2,1,0:T(8,128)(2,1)}), bf16[4,4,40,2048]{3,2,1,0:T(8,128)(2,1)S(1)}, u32[]{:S(2)}, u32[]{:S(2)}) %all-to-all-start.3) | async-done | bytes 2621472 | tf_op jit(solution)/shard_map/all_to_all | solution.py:100
  114.7 4.0 %multiply_convert_fusion = (bf16[8,2,256,256]{3,2,1,0:T(8,128)(2,1)}, bf16[8,2,256,256]{3,2,1,0:T(8,128)(2,1)}) fusion(bf16[8,2,256,256]{3,2,1,0:T(8,128)(2,1)} %bitcast.235, f32[8,2,256]{2,1,0:T(2,128)S(1)} %maximum_select_fusion, bf16[8,2,256,256]{3,2,1,0:T(8,128)(2,1)} %bitcast.238), kind=kLoop, calls=%fused_computation | loop fusion | flops 6291456 | bytes 8404992 | tf_op jit(solution)/shard_map/convert_element_type | solution.py:403
  122.2 4.7 %open.1 = (f32[640,256]{1,0:T(8,128)}, f32[640,256]{1,0:T(8,128)}, f32[640,128]{1,0:T(8,128)}) custom-call(s32[1]{0:T(128)} %bitcast.7.core, bf16[640,2048]{1,0:T(8,128)(2,1)} %bitcast.232, bf16[8,2,256,256]{3,2,1,0:T(8,128)(2,1)} %get-tuple-element.141.wg_ref, bf16[8,2,256,256]{3,2,1,0:T(8,128)(2,1)} %get-tuple-element.140.wu_ref), custom_call_target="tpu_custom_call" | custom-call | tf_op jit(solution)/shard_map/open/pallas_call | solution.py:444
  130.4 6.0 %close.1 = (bf16[640,256]{1,0:T(8,128)(2,1)}, bf16[640,256]{1,0:T(8,128)(2,1)}, bf16[640,256]{1,0:T(8,128)(2,1)}, bf16[640,256]{1,0:T(8,128)(2,1)}, bf16[640,256]{1,0:T(8,128)(2,1)}, /*index=5*/f32[640,128]{1,0:T(8,128)}) custom-call(s32[1]{0:T(128)} %bitcast.7.core, bf16[640,2048]{1,0:T(8,128)(2,1)} %collective-permute-done.rows_ref.oth_ref, ...), custom_call_target="tpu_custom_call" | custom-call | tf_op jit(solution)/shard_map/close/pallas_call | solution.py:450
  136.4 4.6 %back_oth.1 = bf16[640,2048]{1,0:T(8,128)(2,1)} custom-call(s32[1]{0:T(128)} %bitcast.7.core, bf16[640,256]{1,0:T(8,128)(2,1)} %get-tuple-element.24.dg_ref, bf16[640,256]{1,0:T(8,128)(2,1)} %get-tuple-element.25.du_ref, bf16[8,2,256,256]{3,2,1,0:T(8,128)(2,1)} %bitcast.239, bf16[8,2,256,256]{3,2,1,0:T(8,128)(2,1)} %bitcast.236), custom_call_target="tpu_custom_call" | custom-call | tf_op jit(solution)/shard_map/back_oth/pallas_call | solution.py:462
  141.5 5.1 %collective-permute-done.11.sc_other_ref = f32[640,128]{1,0:T(8,128)S(1)} collective-permute-done((f32[640,128]{1,0:T(8,128)S(1)}, f32[640,128]{1,0:T(8,128)S(1)}, u32[]{:S(2)}, u32[]{:S(2)}) %collective-permute-start.11) | collective-permute-done | bytes 327712 | tf_op jit(solution)/shard_map/ppermute | solution.py:461
  148.9 5.2 %back_own.1 = (bf16[640,1152]{1,0:T(8,128)(2,1)}, bf16[640,1024]{1,0:T(8,128)(2,1)}) custom-call(s32[1]{0:T(128)} %bitcast.7.core, bf16[640,256]{1,0:T(8,128)(2,1)} %get-tuple-element.24.dg_ref, bf16[640,256]{1,0:T(8,128)(2,1)} %get-tuple-element.25.du_ref, bf16[8,2,256,256]{3,2,1,0:T(8,128)(2,1)} %bitcast.240, bf16[8,2,256,256]{3,2,1,0:T(8,128)(2,1)} %bitcast.237, ...), custom_call_target="tpu_custom_call" | custom-call | tf_op jit(solution)/shard_map/back_own/pallas_call | solution.py:470
  159.9 4.2 %collective-permute-done.12 = bf16[2,40,1024]{2,1,0:T(8,128)(2,1)S(1)} collective-permute-done((bf16[2,40,1024]{2,1,0:T(8,128)(2,1)S(1)}, bf16[2,40,1024]{2,1,0:T(8,128)(2,1)S(1)}, u32[]{:S(2)}, u32[]{:S(2)}) %collective-permute-start.12) | collective-permute-done | bytes 163872 | tf_op jit(solution)/shard_map/ppermute | solution.py:155
  168.8 9.2 %all-to-all-done.4 = bf16[4,4,40,1152]{3,2,1,0:T(8,128)(2,1)S(1)} async-done(((bf16[4,4,40,1152]{3,2,1,0:T(8,128)(2,1)}), bf16[4,4,40,1152]{3,2,1,0:T(8,128)(2,1)S(1)}, u32[]{:S(2)}, u32[]{:S(2)}) %all-to-all-start.4) | async-done | bytes 1474592 | tf_op jit(solution)/shard_map/all_to_all | solution.py:136
  179.0 5.2 %all-to-all-start.5 = ((bf16[4,40,1152]{2,1,0:T(8,128)(2,1)}), bf16[4,40,1152]{2,1,0:T(8,128)(2,1)S(1)}, u32[]{:S(2)}, u32[]{:S(2)}) async-start(bf16[4,40,1152]{2,1,0:T(8,128)(2,1)} %reduce_sum.199), calls=%async_computation.5 | async-start | bytes 737280 | tf_op jit(solution)/shard_map/all_to_all | solution.py:138
  196.2 10.3 %all-to-all-start.6 = ((bf16[8,40,384]{2,1,0:T(8,128)(2,1)}), bf16[8,40,384]{2,1,0:T(8,128)(2,1)S(1)}, u32[]{:S(2)}, u32[]{:S(2)}) async-start(bf16[8,40,384]{2,1,0:T(8,128)(2,1)} %sums.1), calls=%async_computation.6 | async-start | bytes 491520 | tf_op jit(solution)/shard_map/all_to_all | solution.py:76
  208.4 8.1 %shard_map.195 = bf16[8,2,256,256]{3,2,1,0:T(8,128)(2,1)} custom-call(s32[1]{0:T(128)} %bitcast.7.core, bf16[640,2048]{1,0:T(8,128)(2,1)} %bitcast.233, bf16[640,2048]{1,0:T(8,128)(2,1)} %collective-permute-done.rows_ref.oth_ref, f32[8,1,256]{2,1,0:T(1,128)} %copy-done.20, f32[8,1,256]{2,1,0:T(1,128)} %copy-done.21, bf16[640,256]{1,0:T(8,128)(2,1)} %get-tuple-element.29.act_ref), custom_call_target="tpu_custom_call" | custom-call | tf_op jit(solution)/shard_map/pallas_call | solution.py:494
  216.5 8.1 %shard_map.196 = bf16[8,2,256,256]{3,2,1,0:T(8,128)(2,1)} custom-call(s32[1]{0:T(128)} %bitcast.7.core, bf16[640,2048]{1,0:T(8,128)(2,1)} %bitcast.234, bf16[640,2048]{1,0:T(8,128)(2,1)} %collective-permute-done.rows_ref.oth_ref, f32[8,1,256]{2,1,0:T(1,128)} %copy-done.20, f32[8,1,256]{2,1,0:T(1,128)} %copy-done.21, bf16[640,256]{1,0:T(8,128)(2,1)} %get-tuple-element.30.act_ref), custom_call_target="tpu_custom_call" | custom-call | tf_op jit(solution)/shard_map/pallas_call | solution.py:494
  224.8 7.9 %down_grads.1 = bf16[8,2,256,256]{3,2,1,0:T(8,128)(2,1)} custom-call(s32[1]{0:T(128)} %bitcast.7.core, bf16[640,2048]{1,0:T(8,128)(2,1)} %bitcast.53.rows_ref.own_ref, bf16[640,2048]{1,0:T(8,128)(2,1)} %collective-permute-done.9.rows_ref.oth_ref, bf16[640,256]{1,0:T(8,128)(2,1)} %get-tuple-element.31.act_ref), custom_call_target="tpu_custom_call" | custom-call | tf_op jit(solution)/shard_map/down_grads/pallas_call | solution.py:504
  236.4 6.8 %all-to-all-start.7 = ((bf16[16,72,256]{2,1,0:T(8,128)(2,1)}), bf16[16,72,256]{2,1,0:T(8,128)(2,1)S(1)}, u32[]{:S(2)}, u32[]{:S(2)}) async-start(bf16[16,72,256]{2,1,0:T(8,128)(2,1)} %broadcast_in_dim.191), calls=%async_computation.7 | async-start | bytes 1179648 | tf_op jit(solution)/shard_map/all_to_all | solution.py:76
  246.6 5.7 %all-to-all-done.7 = bf16[16,72,256]{2,1,0:T(8,128)(2,1)S(1)} async-done(((bf16[16,72,256]{2,1,0:T(8,128)(2,1)}), bf16[16,72,256]{2,1,0:T(8,128)(2,1)S(1)}, u32[]{:S(2)}, u32[]{:S(2)}) %all-to-all-start.7) | async-done | bytes 589856 | tf_op jit(solution)/shard_map/all_to_all | solution.py:76
  254.9 7.2 %all-to-all-start.8 = ((bf16[8,128,128]{2,1,0:T(8,128)(2,1)}), bf16[8,128,128]{2,1,0:T(8,128)(2,1)S(1)}, u32[]{:S(2)}, u32[]{:S(2)}) async-start(bf16[8,128,128]{2,1,0:T(8,128)(2,1)} %broadcast_in_dim.192), calls=%async_computation.8 | async-start | bytes 524288 | tf_op jit(solution)/shard_map/all_to_all | solution.py:76
  263.8 10.9 %all-to-all-done.8 = bf16[8,128,128]{2,1,0:T(8,128)(2,1)S(1)} async-done(((bf16[8,128,128]{2,1,0:T(8,128)(2,1)}), bf16[8,128,128]{2,1,0:T(8,128)(2,1)S(1)}, u32[]{:S(2)}, u32[]{:S(2)}) %all-to-all-start.8) | async-done | bytes 262176 | tf_op jit(solution)/shard_map/all_to_all | solution.py:76
  (278 shorter events, 86.2 us)
Async XLA Ops:
  4.3 18.4 %all-to-all-start = ((bf16[16,72,256]{2,1,0:T(8,128)(2,1)}), bf16[16,72,256]{2,1,0:T(8,128)(2,1)S(1)}, u32[]{:S(2)}, u32[]{:S(2)}) async-start(bf16[16,72,256]{2,1,0:T(8,128)(2,1)} %broadcast_in_dim.169), calls=%async_computation | async-start | bytes 1179648 | tf_op jit(solution)/shard_map/all_to_all | solution.py:76
  47.0 8.3 %collective-permute-start.2 = (bf16[40,2048]{1,0:T(8,128)(2,1)S(1)}, bf16[40,2048]{1,0:T(8,128)(2,1)S(1)}, u32[]{:S(2)}, u32[]{:S(2)}) collective-permute-start(bf16[40,2048]{1,0:T(8,128)(2,1)S(1)} %get-tuple-element.116), channel_id=1, source_target_pairs={{0,64},{16,80},{32,96},{48,112},{64,128},{80,144},{96,160},{112,17... | collective-permute-start | bytes 491528 | tf_op jit(solution)/shard_map/ppermute | solution.py:117
  47.0 8.4 %collective-permute-start.3 = (bf16[40,2048]{1,0:T(8,128)(2,1)S(1)}, bf16[40,2048]{1,0:T(8,128)(2,1)S(1)}, u32[]{:S(2)}, u32[]{:S(2)}) collective-permute-start(bf16[40,2048]{1,0:T(8,128)(2,1)S(1)} %get-tuple-element.116), channel_id=1, source_target_pairs={{0,128},{16,144},{32,160},{48,176},{64,192},{80,208},{96,224},{112... | collective-permute-start | bytes 491528 | tf_op jit(solution)/shard_map/ppermute | solution.py:117
  49.3 6.9 %collective-permute-start.4 = (bf16[40,2048]{1,0:T(8,128)(2,1)S(1)}, bf16[40,2048]{1,0:T(8,128)(2,1)S(1)}, u32[]{:S(2)}, u32[]{:S(2)}) collective-permute-start(bf16[40,2048]{1,0:T(8,128)(2,1)S(1)} %get-tuple-element.116), channel_id=1, source_target_pairs={{0,192},{16,208},{32,224},{48,240},{64,0},{80,16},{96,32},{112,48}... | collective-permute-start | bytes 491528 | tf_op jit(solution)/shard_map/ppermute | solution.py:117
  56.2 26.9 %collective-permute-start.5 = (bf16[4,40,2048]{2,1,0:T(8,128)(2,1)S(1)}, bf16[4,40,2048]{2,1,0:T(8,128)(2,1)}, u32[]{:S(2)}, u32[]{:S(2)}) collective-permute-start(bf16[4,40,2048]{2,1,0:T(8,128)(2,1)S(1)} %bitcast_dynamic-update-slice_fusion.4), channel_id=1, source_target_pairs={{0,16},{16,32},{32,48},{48,0},{64,80},{80,96},{96,112},{112,64},{1... | collective-permute-start | bytes 1966088 | tf_op jit(solution)/shard_map/ppermute | solution.py:121
  57.2 27.2 %collective-permute-start.6 = (bf16[4,40,2048]{2,1,0:T(8,128)(2,1)S(1)}, bf16[4,40,2048]{2,1,0:T(8,128)(2,1)}, u32[]{:S(2)}, u32[]{:S(2)}) collective-permute-start(bf16[4,40,2048]{2,1,0:T(8,128)(2,1)S(1)} %bitcast_dynamic-update-slice_fusion.4), channel_id=1, source_target_pairs={{0,48},{16,0},{32,16},{48,32},{64,112},{80,64},{96,80},{112,96},{1... | collective-permute-start | bytes 1966088 | tf_op jit(solution)/shard_map/ppermute | solution.py:122
  79.1 30.5 %all-to-all-start.3 = ((bf16[4,4,40,2048]{3,2,1,0:T(8,128)(2,1)}), bf16[4,4,40,2048]{3,2,1,0:T(8,128)(2,1)S(1)}, u32[]{:S(2)}, u32[]{:S(2)}) async-start(bf16[4,4,40,2048]{3,2,1,0:T(8,128)(2,1)} %broadcast_in_dim.180), calls=%async_computation.3 | async-start | bytes 5242880 | tf_op jit(solution)/shard_map/all_to_all | solution.py:100
  84.0 9.1 %collective-permute-start.7 = (bf16[2,40,2048]{2,1,0:T(8,128)(2,1)S(1)}, bf16[2,40,2048]{2,1,0:T(8,128)(2,1)S(1)}, u32[]{:S(2)}, u32[]{:S(2)}) collective-permute-start(bf16[2,40,2048]{2,1,0:T(8,128)(2,1)S(1)} %slice.241), channel_id=1, source_target_pairs={{0,16},{16,32},{32,48},{48,0},{64,80},{80,96},{96,112},{112,64},{1... | collective-permute-start | bytes 983048 | tf_op jit(solution)/shard_map/ppermute | solution.py:124
  85.4 8.5 %collective-permute-start.8 = (bf16[2,40,2048]{2,1,0:T(8,128)(2,1)S(1)}, bf16[2,40,2048]{2,1,0:T(8,128)(2,1)S(1)}, u32[]{:S(2)}, u32[]{:S(2)}) collective-permute-start(bf16[2,40,2048]{2,1,0:T(8,128)(2,1)S(1)} %slice.242), channel_id=1, source_target_pairs={{0,48},{16,0},{32,16},{48,32},{64,112},{80,64},{96,80},{112,96},{1... | collective-permute-start | bytes 983048 | tf_op jit(solution)/shard_map/ppermute | solution.py:125
  94.7 32.2 %collective-permute-start.9 = (bf16[640,2048]{1,0:T(8,128)(2,1)}, bf16[640,2048]{1,0:T(8,128)(2,1)}, u32[]{:S(2)}, u32[]{:S(2)}) collective-permute-start(bf16[640,2048]{1,0:T(8,128)(2,1)} %bitcast.53.rows_ref.own_ref), channel_id=1, source_target_pairs={{0,1},{1,0},{2,3},{3,2},{4,5},{5,4},{6,7},{7,6},{8,9},{9,8},{10,11... | collective-permute-start | bytes 7864328 | tf_op jit(solution)/shard_map/ppermute | solution.py:411
  109.6 20.8 %collective-permute-start = (bf16[640,2048]{1,0:T(8,128)(2,1)S(1)}, bf16[640,2048]{1,0:T(8,128)(2,1)}, u32[]{:S(2)}, u32[]{:S(2)}) collective-permute-start(bf16[640,2048]{1,0:T(8,128)(2,1)S(1)} %bitcast.231), channel_id=1, source_target_pairs={{0,1},{1,0},{2,3},{3,2},{4,5},{5,4},{6,7},{7,6},{8,9},{9,8},{10,11... | collective-permute-start | bytes 7864328 | tf_op jit(solution)/shard_map/ppermute | solution.py:410
  141.0 5.6 %collective-permute-start.10 = (bf16[640,2048]{1,0:T(8,128)(2,1)}, bf16[640,2048]{1,0:T(8,128)(2,1)S(1)}, u32[]{:S(2)}, u32[]{:S(2)}) collective-permute-start(bf16[640,2048]{1,0:T(8,128)(2,1)} %back_oth.1), channel_id=1, source_target_pairs={{0,1},{1,0},{2,3},{3,2},{4,5},{5,4},{6,7},{7,6},{8,9},{9,8},{10,11... | collective-permute-start | bytes 7864328 | tf_op jit(solution)/shard_map/ppermute | solution.py:468
  141.1 5.5 %collective-permute-start.11 = (f32[640,128]{1,0:T(8,128)S(1)}, f32[640,128]{1,0:T(8,128)S(1)}, u32[]{:S(2)}, u32[]{:S(2)}) collective-permute-start(f32[640,128]{1,0:T(8,128)S(1)} %copy-done.12), channel_id=1, source_target_pairs={{0,1},{1,0},{2,3},{3,2},{4,5},{5,4},{6,7},{7,6},{8,9},{9,8},{10,11... | collective-permute-start | bytes 983048 | tf_op jit(solution)/shard_map/ppermute | solution.py:461
  154.1 23.9 %all-to-all-start.4 = ((bf16[4,4,40,1152]{3,2,1,0:T(8,128)(2,1)}), bf16[4,4,40,1152]{3,2,1,0:T(8,128)(2,1)S(1)}, u32[]{:S(2)}, u32[]{:S(2)}) async-start(bf16[4,4,40,1152]{3,2,1,0:T(8,128)(2,1)} %bitcast.246), calls=%async_computation.4 | async-start | bytes 2949120 | tf_op jit(solution)/shard_map/all_to_all | solution.py:136
  157.8 6.4 %collective-permute-start.12 = (bf16[2,40,1024]{2,1,0:T(8,128)(2,1)S(1)}, bf16[2,40,1024]{2,1,0:T(8,128)(2,1)S(1)}, u32[]{:S(2)}, u32[]{:S(2)}) collective-permute-start(bf16[2,40,1024]{2,1,0:T(8,128)(2,1)S(1)} %get-tuple-element.112), channel_id=1, source_target_pairs={{0,16},{16,32},{32,48},{48,0},{64,80},{80,96},{96,112},{112,64},{1... | collective-permute-start | bytes 491528 | tf_op jit(solution)/shard_map/ppermute | solution.py:155
  158.2 6.4 %collective-permute-start.14 = (bf16[2,40,1024]{2,1,0:T(8,128)(2,1)S(1)}, bf16[2,40,1024]{2,1,0:T(8,128)(2,1)S(1)}, u32[]{:S(2)}, u32[]{:S(2)}) collective-permute-start(bf16[2,40,1024]{2,1,0:T(8,128)(2,1)S(1)} %get-tuple-element.115), channel_id=1, source_target_pairs={{0,48},{16,0},{32,16},{48,32},{64,112},{80,64},{96,80},{112,96},{1... | collective-permute-start | bytes 491528 | tf_op jit(solution)/shard_map/ppermute | solution.py:156
  165.4 18.8 %collective-permute-start.15 = (bf16[4,40,1024]{2,1,0:T(8,128)(2,1)}, bf16[4,40,1024]{2,1,0:T(8,128)(2,1)}, u32[]{:S(2)}, u32[]{:S(2)}) collective-permute-start(bf16[4,40,1024]{2,1,0:T(8,128)(2,1)} %pad_maximum_fusion.2), channel_id=1, source_target_pairs={{0,48},{16,0},{32,16},{48,32},{64,112},{80,64},{96,80},{112,96},{1... | collective-permute-start | bytes 983048 | tf_op jit(solution)/shard_map/ppermute | solution.py:160
  168.7 15.5 %collective-permute-start.13 = (bf16[4,40,1024]{2,1,0:T(8,128)(2,1)}, bf16[4,40,1024]{2,1,0:T(8,128)(2,1)}, u32[]{:S(2)}, u32[]{:S(2)}) collective-permute-start(bf16[4,40,1024]{2,1,0:T(8,128)(2,1)} %pad_maximum_fusion.1), channel_id=1, source_target_pairs={{0,16},{16,32},{32,48},{48,0},{64,80},{80,96},{96,112},{112,64},{1... | collective-permute-start | bytes 983048 | tf_op jit(solution)/shard_map/ppermute | solution.py:159
  179.0 14.5 %all-to-all-start.5 = ((bf16[4,40,1152]{2,1,0:T(8,128)(2,1)}), bf16[4,40,1152]{2,1,0:T(8,128)(2,1)S(1)}, u32[]{:S(2)}, u32[]{:S(2)}) async-start(bf16[4,40,1152]{2,1,0:T(8,128)(2,1)} %reduce_sum.199), calls=%async_computation.5 | async-start | bytes 737280 | tf_op jit(solution)/shard_map/all_to_all | solution.py:138
  186.1 5.7 %collective-permute-start.16 = (bf16[40,1024]{1,0:T(8,128)(2,1)S(1)}, bf16[40,1024]{1,0:T(8,128)(2,1)S(1)}, u32[]{:S(2)}, u32[]{:S(2)}) collective-permute-start(bf16[40,1024]{1,0:T(8,128)(2,1)S(1)} %get-tuple-element.134), channel_id=1, source_target_pairs={{0,64},{16,80},{32,96},{48,112},{64,128},{80,144},{96,160},{112,17... | collective-permute-start | bytes 245768 | tf_op jit(solution)/shard_map/ppermute | solution.py:168
  186.7 6.0 %collective-permute-start.17 = (bf16[40,1024]{1,0:T(8,128)(2,1)S(1)}, bf16[40,1024]{1,0:T(8,128)(2,1)S(1)}, u32[]{:S(2)}, u32[]{:S(2)}) collective-permute-start(bf16[40,1024]{1,0:T(8,128)(2,1)S(1)} %get-tuple-element.133), channel_id=1, source_target_pairs={{0,128},{16,144},{32,160},{48,176},{64,192},{80,208},{96,224},{112... | collective-permute-start | bytes 245768 | tf_op jit(solution)/shard_map/ppermute | solution.py:168
  196.2 36.5 %all-to-all-start.6 = ((bf16[8,40,384]{2,1,0:T(8,128)(2,1)}), bf16[8,40,384]{2,1,0:T(8,128)(2,1)S(1)}, u32[]{:S(2)}, u32[]{:S(2)}) async-start(bf16[8,40,384]{2,1,0:T(8,128)(2,1)} %sums.1), calls=%async_computation.6 | async-start | bytes 491520 | tf_op jit(solution)/shard_map/all_to_all | solution.py:76
  236.4 15.9 %all-to-all-start.7 = ((bf16[16,72,256]{2,1,0:T(8,128)(2,1)}), bf16[16,72,256]{2,1,0:T(8,128)(2,1)S(1)}, u32[]{:S(2)}, u32[]{:S(2)}) async-start(bf16[16,72,256]{2,1,0:T(8,128)(2,1)} %broadcast_in_dim.191), calls=%async_computation.7 | async-start | bytes 1179648 | tf_op jit(solution)/shard_map/all_to_all | solution.py:76
  254.9 19.7 %all-to-all-start.8 = ((bf16[8,128,128]{2,1,0:T(8,128)(2,1)}), bf16[8,128,128]{2,1,0:T(8,128)(2,1)S(1)}, u32[]{:S(2)}, u32[]{:S(2)}) async-start(bf16[8,128,128]{2,1,0:T(8,128)(2,1)} %broadcast_in_dim.192), calls=%async_computation.8 | async-start | bytes 524288 | tf_op jit(solution)/shard_map/all_to_all | solution.py:76
  (56 other events, 566.4 us)

commit v5 on v4

--- a/solution.py
+++ b/solution.py
@@ -96,18 +96,12 @@
 
 
 def gather_rows(block):
-    def spread(x, groups):
-        return lax.all_to_all(
-            jnp.broadcast_to(x[None], (SIDE,) + x.shape),
-            "ctx",
-            0,
-            0,
-            tiled=True,
-            axis_index_groups=groups,
-        )
-
-    row = spread(block, [[y * SIDE + x for x in range(SIDE)] for y in range(SIDE)])
-    return spread(row, [[y * SIDE + x for y in range(SIDE)] for x in range(SIDE)])
+    groups_x = [[y * SIDE + x for x in range(SIDE)] for y in range(SIDE)]
+    groups_y = [[y * SIDE + x for y in range(SIDE)] for x in range(SIDE)]
+    block = jnp.broadcast_to(block[None], (SIDE,) + block.shape)
+    row = lax.all_to_all(block, "ctx", 0, 0, tiled=True, axis_index_groups=groups_x)
+    row = jnp.broadcast_to(row[None], (SIDE,) + row.shape)
+    return lax.all_to_all(row, "ctx", 0, 0, tiled=True, axis_index_groups=groups_y)
 
 
 def gather_cot(block):
@@ -218,12 +212,8 @@
     )
 
 
-def near_kernel(core, rows_ref, w_ref, ga_ref):
-    ga_ref[...] = dot(rows_ref[...], stacked(w_ref))
-
-
-def far_kernel(core, rows_ref, w_ref, ga_in, ga_ref):
-    ga_ref[...] = ga_in[...] + dot(rows_ref[...], stacked(w_ref))
+def cot_kernel(core, own_ref, oth_ref, w_own_ref, w_oth_ref, ga_ref):
+    ga_ref[...] = dot(own_ref[...], stacked(w_own_ref)) + dot(oth_ref[...], stacked(w_oth_ref))
 
 
 def back_term(dg_ref, du_ref, wg_ref, wu_ref, block):
@@ -261,11 +251,14 @@
     low_ref[:, width:] = jnp.where(lane < 3, head, jnp.where(lane < 6, tail, 0.0)).astype(BF16)
 
 
-def scaled_grads_kernel(core, own_ref, oth_ref, gown_ref, goth_ref, act_ref, out_ref):
+def scaled_grads_kernel(
+    core, own_ref, oth_ref, gown_ref, goth_ref, dgi_ref, dui_ref, gate_ref, up_ref
+):
     here = core[0]
     for rows_ref, gain_ref, place in ((own_ref, gown_ref, here), (oth_ref, goth_ref, 1 - here)):
         scaled = (rows_ref[...].astype(F32) * gain_ref[...]).astype(BF16)
-        out_ref[place] = dot(scaled, act_ref[...], ((0,), (0,))).astype(BF16)
+        gate_ref[place] = dot(scaled, dgi_ref[...], ((0,), (0,))).astype(BF16)
+        up_ref[place] = dot(scaled, dui_ref[...], ((0,), (0,))).astype(BF16)
 
 
 def plain_grads_kernel(core, own_ref, oth_ref, act_ref, out_ref):
@@ -430,17 +423,11 @@
         )
 
     grad_act = pl.pallas_call(
-        near_kernel,
-        grid_spec=grid_of(1, split, [rows_spec, w_own], acts),
+        cot_kernel,
+        grid_spec=grid_of(1, split, [rows_spec, rows_spec, w_own, w_oth], acts),
         out_shape=acts_f,
-        name="cot_near",
-    )(core, cot_own, down4)
-    grad_act = pl.pallas_call(
-        far_kernel,
-        grid_spec=grid_of(1, split, [rows_spec, w_oth, acts], acts),
-        out_shape=acts_f,
-        name="cot_far",
-    )(core, cot_oth, down4, grad_act)
+        name="cot",
+    )(core, cot_own, cot_oth, down4, down4)
     ag, au, ss = pl.pallas_call(
         open_kernel,
         grid_spec=grid_of(1, split, [rows_spec, w_own, w_own], [acts, acts, sums]),
@@ -490,17 +477,17 @@
     acts_all = whole((rows_all, units))
     grads_shape = jax.ShapeDtypeStruct(gate4.shape, BF16)
 
-    def scaled_grads(act):
-        return pl.pallas_call(
-            scaled_grads_kernel,
-            grid_spec=grid_of(
-                1, exp_count, [columns, columns, gain_spec, gain_spec, acts_all], w_pair
-            ),
-            out_shape=grads_shape,
-        )(core, own, oth, gain_own[:, None], gain_oth[:, None], act)
-
-    gate_grad = scaled_grads(dgi)
-    up_grad = scaled_grads(dui)
+    gate_grad, up_grad = pl.pallas_call(
+        scaled_grads_kernel,
+        grid_spec=grid_of(
+            1,
+            exp_count,
+            [columns, columns, gain_spec, gain_spec, acts_all, acts_all],
+            [w_pair] * 2,
+        ),
+        out_shape=[grads_shape] * 2,
+        name="gate_grads",
+    )(core, own, oth, gain_own[:, None], gain_oth[:, None], dgi, dui)
     down_grad = pl.pallas_call(
         plain_grads_kernel,
         grid_spec=grid_of(1, exp_count, [columns, columns, acts_all], w_pair),
@@ -549,12 +536,13 @@
     both = jnp.concatenate([keys_first + keys_second, queries_part], axis=1).astype(BF16)
     both = (both.astype(F32) + lax.ppermute(both, "dp", other_core).astype(F32)).astype(BF16)
     both = to_all(both, "exp")
-    both = jnp.sum(both.astype(F32), axis=0)
+    keys_grad = jnp.sum(both[:, :, :state_rows].astype(F32), axis=0)
+    queries_grad = jnp.sum(both[:, :, state_rows:].astype(F32), axis=0)
     return (
         grad_hidden.astype(BF16),
         (vals_first + vals_second).astype(BF16),
-        both[:, :state_rows],
-        both[:, state_rows:],
+        keys_grad,
+        queries_grad,
         decay_first + decay_second,
         grad_probs,
         grad_gain,

time: 280 us -> 271 us (0.968)
  Pallas kernels: 53.5 us -> 44.6 us
  local copies, waits for them, and re-layouts: 24.8 us -> 16.6 us
  waiting for transfers between devices: 67.7 us -> 75.3 us
    pallas_call x4 -> x2, Pallas kernels: 23.2 us -> 14.3 us  [the longest x1 9.48 us: per_device(): pl.pallas_call(scaled_grads_kernel, grid_spec=grid_of(1, exp_count, [colu...]
    ppermute x1, waiting for transfers between devices: 0.01 us -> 2.86 us  [gather_cot(): far_low = lax.ppermute(left[:half], 'ctx', along_x(1))]
    unnamed x120 -> x126, local copies, waits for them, and re-layouts: 8.22 us -> 9.13 us
  transfers between devices with their start and end apart: 27 -> 27, of which waited for: 14 -> 16; matrix products, arithmetic and copies ran while one was open for 13% -> 10% of each run, Pallas kernels for 13% -> 10%
where the time goes in v5:
time: 271 us; the launch traced here: 268 us
  waiting for transfers between devices  75.3 us (28%)
  starting transfers between devices  61.7 us (23%)
  Pallas kernels  44.6 us (16%)
  blocking collectives  39.8 us (15%)
  local copies, waits for them, and re-layouts  16.6 us (6%)
  matrix products  14 us (5%)
  other arithmetic  13.6 us (5%)
    all_to_all x4, starting transfers between devices, swap(): return lax.all_to_all(x, axis, 0, 0, tiled=True)  31.1 us
    all_to_all x1, blocking collectives, swap(): return lax.all_to_all(x, axis, 0, 0, tiled=True)  20.9 us
    all_to_all x4, waiting for transfers between devices, swap(): return lax.all_to_all(x, axis, 0, 0, tiled=True)  20.7 us
    all_to_all x1, blocking collectives, gather_rows(): lax.all_to_all(block, 'ctx', 0, 0, tiled=True, axis_index_groups=groups_x)  18.9 us
    all_to_all x1, waiting for transfers between devices, gather_rows(): lax.all_to_all(row, 'ctx', 0, 0, tiled=True, axis_index_groups=groups_y)  17.3 us
    dot_general x37, matrix products, dot(): lax.dot_general(a, b, (dims, ((), ())), precision=precision, preferred_el...  14 us
    pallas_call x1, Pallas kernels, per_device(): pl.pallas_call(scaled_grads_kernel, grid_spec=grid_of(1, exp_count, [colu...  9.48 us
    all_to_all x1, waiting for transfers between devices, sum_low(): lax.all_to_all(blocks, 'ctx', 0, 0, tiled=True, axis_index_groups=groups_y)  9.23 us
  transfers between devices with their start and end apart: 27, of which 16 were waited for; matrix products, arithmetic and copies ran while one was open for 10% of the time, Pallas kernels for 10%

profile of v5, /device:TPU:2, one launch (start us, length us, event | category | flops | bytes accessed | tf_op | source)
XLA Modules:
  0.0 267.5 jit_solution(13778881807297556461)
XLA Ops:
  4.3 7.5 %all-to-all-start = ((bf16[16,72,256]{2,1,0:T(8,128)(2,1)}), bf16[16,72,256]{2,1,0:T(8,128)(2,1)S(1)}, u32[]{:S(2)}, u32[]{:S(2)}) async-start(bf16[16,72,256]{2,1,0:T(8,128)(2,1)} %broadcast_in_dim.167), calls=%async_computation | async-start | bytes 1179648 | tf_op jit(solution)/shard_map/all_to_all | solution.py:76
  18.6 4.1 %all-to-all-done = bf16[16,72,256]{2,1,0:T(8,128)(2,1)S(1)} async-done(((bf16[16,72,256]{2,1,0:T(8,128)(2,1)}), bf16[16,72,256]{2,1,0:T(8,128)(2,1)S(1)}, u32[]{:S(2)}, u32[]{:S(2)}) %all-to-all-start) | async-done | bytes 589856 | tf_op jit(solution)/shard_map/all_to_all | solution.py:76
  25.4 20.9 %all_to_all.45 = bf16[8,88,256]{2,1,0:T(8,128)(2,1)S(1)} all-to-all(bf16[8,88,256]{2,1,0:T(8,128)(2,1)S(1)} %pad_maximum_fusion), channel_id=1, replica_groups=mesh['ctx'=16,'exp'=8,'dp'=2] {'exp'}, dimensions={0} | all-to-all | bytes 720896 | tf_op jit(solution)/shard_map/all_to_all | solution.py:76
  50.5 4.8 %collective-permute-done.2 = bf16[40,2048]{1,0:T(8,128)(2,1)S(1)} collective-permute-done((bf16[40,2048]{1,0:T(8,128)(2,1)S(1)}, bf16[40,2048]{1,0:T(8,128)(2,1)S(1)}, u32[]{:S(2)}, u32[]{:S(2)}) %collective-permute-start.2) | collective-permute-done | bytes 163872 | tf_op jit(solution)/shard_map/ppermute | solution.py:111
  58.4 18.9 %all_to_all.46 = bf16[4,40,2048]{2,1,0:T(8,128)(2,1)S(1)} all-to-all(bf16[4,40,2048]{2,1,0:T(8,128)(2,1)S(1)} %broadcast_in_dim.177), channel_id=1, replica_groups={{0,16,32,48},{64,80,96,112},{128,144,160,176},{192,208,224,240},{1,17,3..., dimensions={0} | all-to-all | bytes 1310720 | tf_op jit(solution)/shard_map/all_to_all | solution.py:102
  79.1 4.6 %all-to-all-start.3 = ((bf16[4,4,40,2048]{3,2,1,0:T(8,128)(2,1)}), bf16[4,4,40,2048]{3,2,1,0:T(8,128)(2,1)}, u32[]{:S(2)}, u32[]{:S(2)}) async-start(bf16[4,4,40,2048]{3,2,1,0:T(8,128)(2,1)} %broadcast_in_dim.178), calls=%async_computation.3 | async-start | bytes 5242880 | tf_op jit(solution)/shard_map/all_to_all | solution.py:104
  93.3 17.3 %all-to-all-done.3 = bf16[4,4,40,2048]{3,2,1,0:T(8,128)(2,1)} async-done(((bf16[4,4,40,2048]{3,2,1,0:T(8,128)(2,1)}), bf16[4,4,40,2048]{3,2,1,0:T(8,128)(2,1)}, u32[]{:S(2)}, u32[]{:S(2)}) %all-to-all-start.3) | async-done | bytes 2621472 | tf_op jit(solution)/shard_map/all_to_all | solution.py:104
  116.5 4.0 %multiply_convert_fusion = (bf16[8,2,256,256]{3,2,1,0:T(8,128)(2,1)}, bf16[8,2,256,256]{3,2,1,0:T(8,128)(2,1)}) fusion(bf16[8,2,256,256]{3,2,1,0:T(8,128)(2,1)} %bitcast.234, f32[8,2,256]{2,1,0:T(2,128)S(1)} %maximum_select_fusion, bf16[8,2,256,256]{3,2,1,0:T(8,128)(2,1)} %bitcast.237), kind=kLoop, calls=%fused_computation | loop fusion | flops 6291456 | bytes 8404992 | tf_op jit(solution)/shard_map/convert_element_type | solution.py:396
  120.5 4.7 %open.1 = (f32[640,256]{1,0:T(8,128)}, f32[640,256]{1,0:T(8,128)}, f32[640,128]{1,0:T(8,128)}) custom-call(s32[1]{0:T(128)} %bitcast.7.core, bf16[640,2048]{1,0:T(8,128)(2,1)} %bitcast.32.rows_ref.own_ref, bf16[8,2,256,256]{3,2,1,0:T(8,128)(2,1)} %get-tuple-element.145.wg_ref, bf16[8,2,256,256]{3,2,1,0:T(8,128)(2,1)} %get-tuple-element.144.wu_ref), custom_call_target="tpu_custom_call" | custom-call | tf_op jit(solution)/shard_map/open/pallas_call | solution.py:431
  125.2 4.8 %cot.1.ga_ref = f32[640,256]{1,0:T(8,128)} custom-call(s32[1]{0:T(128)} %bitcast.7.core, bf16[640,2048]{1,0:T(8,128)(2,1)} %bitcast.232, bf16[640,2048]{1,0:T(8,128)(2,1)} %collective-permute-done.9.oth_ref, bf16[8,2,256,256]{3,2,1,0:T(8,128)(2,1)} %bitcast.240, bf16[8,2,256,256]{3,2,1,0:T(8,128)(2,1)} %bitcast.241), custom_call_target="tpu_custom_call" | custom-call | tf_op jit(solution)/shard_map/cot/pallas_call | solution.py:425
  130.1 5.9 %close.1 = (bf16[640,256]{1,0:T(8,128)(2,1)}, bf16[640,256]{1,0:T(8,128)(2,1)}, bf16[640,256]{1,0:T(8,128)(2,1)}, bf16[640,256]{1,0:T(8,128)(2,1)}, bf16[640,256]{1,0:T(8,128)(2,1)}, /*index=5*/f32[640,128]{1,0:T(8,128)}) custom-call(s32[1]{0:T(128)} %bitcast.7.core, bf16[640,2048]{1,0:T(8,128)(2,1)} %collective-permute-done.rows_ref.oth_ref, ...), custom_call_target="tpu_custom_call" | custom-call | tf_op jit(solution)/shard_map/close/pallas_call | solution.py:437
  136.0 4.7 %back_oth.1 = bf16[640,2048]{1,0:T(8,128)(2,1)} custom-call(s32[1]{0:T(128)} %bitcast.7.core, bf16[640,256]{1,0:T(8,128)(2,1)} %get-tuple-element.26.dg_ref, bf16[640,256]{1,0:T(8,128)(2,1)} %get-tuple-element.27.du_ref, bf16[8,2,256,256]{3,2,1,0:T(8,128)(2,1)} %bitcast.238, bf16[8,2,256,256]{3,2,1,0:T(8,128)(2,1)} %bitcast.235), custom_call_target="tpu_custom_call" | custom-call | tf_op jit(solution)/shard_map/back_oth/pallas_call | solution.py:449
  141.2 5.1 %collective-permute-done.11.sc_other_ref = f32[640,128]{1,0:T(8,128)S(1)} collective-permute-done((f32[640,128]{1,0:T(8,128)S(1)}, f32[640,128]{1,0:T(8,128)S(1)}, u32[]{:S(2)}, u32[]{:S(2)}) %collective-permute-start.11) | collective-permute-done | bytes 327712 | tf_op jit(solution)/shard_map/ppermute | solution.py:448
  148.6 5.2 %back_own.1 = (bf16[640,1152]{1,0:T(8,128)(2,1)}, bf16[640,1024]{1,0:T(8,128)(2,1)}) custom-call(s32[1]{0:T(128)} %bitcast.7.core, bf16[640,256]{1,0:T(8,128)(2,1)} %get-tuple-element.26.dg_ref, bf16[640,256]{1,0:T(8,128)(2,1)} %get-tuple-element.27.du_ref, bf16[8,2,256,256]{3,2,1,0:T(8,128)(2,1)} %bitcast.239, bf16[8,2,256,256]{3,2,1,0:T(8,128)(2,1)} %bitcast.236, ...), custom_call_target="tpu_custom_call" | custom-call | tf_op jit(solution)/shard_map/back_own/pallas_call | solution.py:457
  159.7 4.2 %collective-permute-done.12 = bf16[2,40,1024]{2,1,0:T(8,128)(2,1)S(1)} collective-permute-done((bf16[2,40,1024]{2,1,0:T(8,128)(2,1)S(1)}, bf16[2,40,1024]{2,1,0:T(8,128)(2,1)S(1)}, u32[]{:S(2)}, u32[]{:S(2)}) %collective-permute-start.12) | collective-permute-done | bytes 163872 | tf_op jit(solution)/shard_map/ppermute | solution.py:149
  168.5 9.2 %all-to-all-done.4 = bf16[4,4,40,1152]{3,2,1,0:T(8,128)(2,1)S(1)} async-done(((bf16[4,4,40,1152]{3,2,1,0:T(8,128)(2,1)}), bf16[4,4,40,1152]{3,2,1,0:T(8,128)(2,1)S(1)}, u32[]{:S(2)}, u32[]{:S(2)}) %all-to-all-start.4) | async-done | bytes 1474592 | tf_op jit(solution)/shard_map/all_to_all | solution.py:130
  178.8 5.2 %all-to-all-start.5 = ((bf16[4,40,1152]{2,1,0:T(8,128)(2,1)}), bf16[4,40,1152]{2,1,0:T(8,128)(2,1)S(1)}, u32[]{:S(2)}, u32[]{:S(2)}) async-start(bf16[4,40,1152]{2,1,0:T(8,128)(2,1)} %reduce_sum.208), calls=%async_computation.5 | async-start | bytes 737280 | tf_op jit(solution)/shard_map/all_to_all | solution.py:132
  196.0 9.7 %all-to-all-start.6 = ((bf16[8,40,384]{2,1,0:T(8,128)(2,1)}), bf16[8,40,384]{2,1,0:T(8,128)(2,1)S(1)}, u32[]{:S(2)}, u32[]{:S(2)}) async-start(bf16[8,40,384]{2,1,0:T(8,128)(2,1)} %sums.1), calls=%async_computation.6 | async-start | bytes 491520 | tf_op jit(solution)/shard_map/all_to_all | solution.py:76
  207.5 7.8 %down_grads.1 = bf16[8,2,256,256]{3,2,1,0:T(8,128)(2,1)} custom-call(s32[1]{0:T(128)} %bitcast.7.core, bf16[640,2048]{1,0:T(8,128)(2,1)} %bitcast.233, bf16[640,2048]{1,0:T(8,128)(2,1)} %collective-permute-done.9.oth_ref, bf16[640,256]{1,0:T(8,128)(2,1)} %get-tuple-element.35.act_ref), custom_call_target="tpu_custom_call" | custom-call | tf_op jit(solution)/shard_map/down_grads/pallas_call | solution.py:491
  215.5 9.5 %gate_grads.1 = (bf16[8,2,256,256]{3,2,1,0:T(8,128)(2,1)}, bf16[8,2,256,256]{3,2,1,0:T(8,128)(2,1)}) custom-call(s32[1]{0:T(128)} %bitcast.7.core, bf16[640,2048]{1,0:T(8,128)(2,1)} %bitcast.32.rows_ref.own_ref, bf16[640,2048]{1,0:T(8,128)(2,1)} %collective-permute-done.rows_ref.oth_ref, f32[8,1,256]{2,1,0:T(1,128)} %copy-done.29, f32[8,1,256]{2,1,0:T(1,128)} %copy-done.30, ...), custom_call_target="tpu_custom_call" | custom-call | tf_op jit(solution)/shard_map/gate_grads/pallas_call | solution.py:480
  228.7 6.8 %all-to-all-start.7 = ((bf16[16,72,256]{2,1,0:T(8,128)(2,1)}), bf16[16,72,256]{2,1,0:T(8,128)(2,1)S(1)}, u32[]{:S(2)}, u32[]{:S(2)}) async-start(bf16[16,72,256]{2,1,0:T(8,128)(2,1)} %broadcast_in_dim.189), calls=%async_computation.7 | async-start | bytes 1179648 | tf_op jit(solution)/shard_map/all_to_all | solution.py:76
  238.9 5.7 %all-to-all-done.7 = bf16[16,72,256]{2,1,0:T(8,128)(2,1)S(1)} async-done(((bf16[16,72,256]{2,1,0:T(8,128)(2,1)}), bf16[16,72,256]{2,1,0:T(8,128)(2,1)S(1)}, u32[]{:S(2)}, u32[]{:S(2)}) %all-to-all-start.7) | async-done | bytes 589856 | tf_op jit(solution)/shard_map/all_to_all | solution.py:76
  247.1 7.2 %all-to-all-start.8 = ((bf16[8,128,128]{1,2,0:T(8,128)(2,1)}), bf16[8,128,128]{1,2,0:T(8,128)(2,1)S(1)}, u32[]{:S(2)}, u32[]{:S(2)}) async-start(bf16[8,128,128]{1,2,0:T(8,128)(2,1)} %broadcast_in_dim.190), calls=%async_computation.8 | async-start | bytes 524288 | tf_op jit(solution)/shard_map/all_to_all | solution.py:76
  255.9 10.9 %all-to-all-done.8 = bf16[8,128,128]{1,2,0:T(8,128)(2,1)S(1)} async-done(((bf16[8,128,128]{1,2,0:T(8,128)(2,1)}), bf16[8,128,128]{1,2,0:T(8,128)(2,1)S(1)}, u32[]{:S(2)}, u32[]{:S(2)}) %all-to-all-start.8) | async-done | bytes 262176 | tf_op jit(solution)/shard_map/all_to_all | solution.py:76
  (280 shorter events, 76.9 us)
Async XLA Ops:
  4.3 18.4 %all-to-all-start = ((bf16[16,72,256]{2,1,0:T(8,128)(2,1)}), bf16[16,72,256]{2,1,0:T(8,128)(2,1)S(1)}, u32[]{:S(2)}, u32[]{:S(2)}) async-start(bf16[16,72,256]{2,1,0:T(8,128)(2,1)} %broadcast_in_dim.167), calls=%async_computation | async-start | bytes 1179648 | tf_op jit(solution)/shard_map/all_to_all | solution.py:76
  47.0 8.3 %collective-permute-start.2 = (bf16[40,2048]{1,0:T(8,128)(2,1)S(1)}, bf16[40,2048]{1,0:T(8,128)(2,1)S(1)}, u32[]{:S(2)}, u32[]{:S(2)}) collective-permute-start(bf16[40,2048]{1,0:T(8,128)(2,1)S(1)} %get-tuple-element.122), channel_id=1, source_target_pairs={{0,64},{16,80},{32,96},{48,112},{64,128},{80,144},{96,160},{112,17... | collective-permute-start | bytes 491528 | tf_op jit(solution)/shard_map/ppermute | solution.py:111
  47.0 8.4 %collective-permute-start.3 = (bf16[40,2048]{1,0:T(8,128)(2,1)S(1)}, bf16[40,2048]{1,0:T(8,128)(2,1)S(1)}, u32[]{:S(2)}, u32[]{:S(2)}) collective-permute-start(bf16[40,2048]{1,0:T(8,128)(2,1)S(1)} %get-tuple-element.122), channel_id=1, source_target_pairs={{0,128},{16,144},{32,160},{48,176},{64,192},{80,208},{96,224},{112... | collective-permute-start | bytes 491528 | tf_op jit(solution)/shard_map/ppermute | solution.py:111
  49.3 6.9 %collective-permute-start.4 = (bf16[40,2048]{1,0:T(8,128)(2,1)S(1)}, bf16[40,2048]{1,0:T(8,128)(2,1)S(1)}, u32[]{:S(2)}, u32[]{:S(2)}) collective-permute-start(bf16[40,2048]{1,0:T(8,128)(2,1)S(1)} %get-tuple-element.122), channel_id=1, source_target_pairs={{0,192},{16,208},{32,224},{48,240},{64,0},{80,16},{96,32},{112,48}... | collective-permute-start | bytes 491528 | tf_op jit(solution)/shard_map/ppermute | solution.py:111
  56.2 27.6 %collective-permute-start.5 = (bf16[4,40,2048]{2,1,0:T(8,128)(2,1)S(1)}, bf16[4,40,2048]{2,1,0:T(8,128)(2,1)S(1)}, u32[]{:S(2)}, u32[]{:S(2)}) collective-permute-start(bf16[4,40,2048]{2,1,0:T(8,128)(2,1)S(1)} %bitcast_dynamic-update-slice_fusion.4), channel_id=1, source_target_pairs={{0,16},{16,32},{32,48},{48,0},{64,80},{80,96},{96,112},{112,64},{1... | collective-permute-start | bytes 1966088 | tf_op jit(solution)/shard_map/ppermute | solution.py:115
  57.2 26.9 %collective-permute-start.6 = (bf16[4,40,2048]{2,1,0:T(8,128)(2,1)S(1)}, bf16[4,40,2048]{2,1,0:T(8,128)(2,1)S(1)}, u32[]{:S(2)}, u32[]{:S(2)}) collective-permute-start(bf16[4,40,2048]{2,1,0:T(8,128)(2,1)S(1)} %bitcast_dynamic-update-slice_fusion.4), channel_id=1, source_target_pairs={{0,48},{16,0},{32,16},{48,32},{64,112},{80,64},{96,80},{112,96},{1... | collective-permute-start | bytes 1966088 | tf_op jit(solution)/shard_map/ppermute | solution.py:116
  79.1 31.5 %all-to-all-start.3 = ((bf16[4,4,40,2048]{3,2,1,0:T(8,128)(2,1)}), bf16[4,4,40,2048]{3,2,1,0:T(8,128)(2,1)}, u32[]{:S(2)}, u32[]{:S(2)}) async-start(bf16[4,4,40,2048]{3,2,1,0:T(8,128)(2,1)} %broadcast_in_dim.178), calls=%async_computation.3 | async-start | bytes 5242880 | tf_op jit(solution)/shard_map/all_to_all | solution.py:104
  83.8 7.2 %collective-permute-start.7 = (bf16[2,40,2048]{2,1,0:T(8,128)(2,1)S(1)}, bf16[2,40,2048]{2,1,0:T(8,128)(2,1)S(1)}, u32[]{:S(2)}, u32[]{:S(2)}) collective-permute-start(bf16[2,40,2048]{2,1,0:T(8,128)(2,1)S(1)} %slice.241), channel_id=1, source_target_pairs={{0,16},{16,32},{32,48},{48,0},{64,80},{80,96},{96,112},{112,64},{1... | collective-permute-start | bytes 983048 | tf_op jit(solution)/shard_map/ppermute | solution.py:118
  85.0 8.2 %collective-permute-start.8 = (bf16[2,40,2048]{2,1,0:T(8,128)(2,1)S(1)}, bf16[2,40,2048]{2,1,0:T(8,128)(2,1)S(1)}, u32[]{:S(2)}, u32[]{:S(2)}) collective-permute-start(bf16[2,40,2048]{2,1,0:T(8,128)(2,1)S(1)} %slice.242), channel_id=1, source_target_pairs={{0,48},{16,0},{32,16},{48,32},{64,112},{80,64},{96,80},{112,96},{1... | collective-permute-start | bytes 983048 | tf_op jit(solution)/shard_map/ppermute | solution.py:119
  93.2 32.0 %collective-permute-start.9 = (bf16[640,2048]{1,0:T(8,128)(2,1)S(1)}, bf16[640,2048]{1,0:T(8,128)(2,1)}, u32[]{:S(2)}, u32[]{:S(2)}) collective-permute-start(bf16[640,2048]{1,0:T(8,128)(2,1)S(1)} %bitcast.231), channel_id=1, source_target_pairs={{0,1},{1,0},{2,3},{3,2},{4,5},{5,4},{6,7},{7,6},{8,9},{9,8},{10,11... | collective-permute-start | bytes 7864328 | tf_op jit(solution)/shard_map/ppermute | solution.py:404
  110.6 19.4 %collective-permute-start = (bf16[640,2048]{1,0:T(8,128)(2,1)}, bf16[640,2048]{1,0:T(8,128)(2,1)}, u32[]{:S(2)}, u32[]{:S(2)}) collective-permute-start(bf16[640,2048]{1,0:T(8,128)(2,1)} %bitcast.32.rows_ref.own_ref), channel_id=1, source_target_pairs={{0,1},{1,0},{2,3},{3,2},{4,5},{5,4},{6,7},{7,6},{8,9},{9,8},{10,11... | collective-permute-start | bytes 7864328 | tf_op jit(solution)/shard_map/ppermute | solution.py:403
  140.7 5.6 %collective-permute-start.10 = (bf16[640,2048]{1,0:T(8,128)(2,1)}, bf16[640,2048]{1,0:T(8,128)(2,1)S(1)}, u32[]{:S(2)}, u32[]{:S(2)}) collective-permute-start(bf16[640,2048]{1,0:T(8,128)(2,1)} %back_oth.1), channel_id=1, source_target_pairs={{0,1},{1,0},{2,3},{3,2},{4,5},{5,4},{6,7},{7,6},{8,9},{9,8},{10,11... | collective-permute-start | bytes 7864328 | tf_op jit(solution)/shard_map/ppermute | solution.py:455
  140.8 5.4 %collective-permute-start.11 = (f32[640,128]{1,0:T(8,128)S(1)}, f32[640,128]{1,0:T(8,128)S(1)}, u32[]{:S(2)}, u32[]{:S(2)}) collective-permute-start(f32[640,128]{1,0:T(8,128)S(1)} %copy-done.16), channel_id=1, source_target_pairs={{0,1},{1,0},{2,3},{3,2},{4,5},{5,4},{6,7},{7,6},{8,9},{9,8},{10,11... | collective-permute-start | bytes 983048 | tf_op jit(solution)/shard_map/ppermute | solution.py:448
  153.8 23.9 %all-to-all-start.4 = ((bf16[4,4,40,1152]{3,2,1,0:T(8,128)(2,1)}), bf16[4,4,40,1152]{3,2,1,0:T(8,128)(2,1)S(1)}, u32[]{:S(2)}, u32[]{:S(2)}) async-start(bf16[4,4,40,1152]{3,2,1,0:T(8,128)(2,1)} %bitcast.243), calls=%async_computation.4 | async-start | bytes 2949120 | tf_op jit(solution)/shard_map/all_to_all | solution.py:130
  157.6 6.3 %collective-permute-start.12 = (bf16[2,40,1024]{2,1,0:T(8,128)(2,1)S(1)}, bf16[2,40,1024]{2,1,0:T(8,128)(2,1)S(1)}, u32[]{:S(2)}, u32[]{:S(2)}) collective-permute-start(bf16[2,40,1024]{2,1,0:T(8,128)(2,1)S(1)} %get-tuple-element.118), channel_id=1, source_target_pairs={{0,16},{16,32},{32,48},{48,0},{64,80},{80,96},{96,112},{112,64},{1... | collective-permute-start | bytes 491528 | tf_op jit(solution)/shard_map/ppermute | solution.py:149
  157.9 6.4 %collective-permute-start.14 = (bf16[2,40,1024]{2,1,0:T(8,128)(2,1)S(1)}, bf16[2,40,1024]{2,1,0:T(8,128)(2,1)S(1)}, u32[]{:S(2)}, u32[]{:S(2)}) collective-permute-start(bf16[2,40,1024]{2,1,0:T(8,128)(2,1)S(1)} %get-tuple-element.121), channel_id=1, source_target_pairs={{0,48},{16,0},{32,16},{48,32},{64,112},{80,64},{96,80},{112,96},{1... | collective-permute-start | bytes 491528 | tf_op jit(solution)/shard_map/ppermute | solution.py:150
  165.1 18.9 %collective-permute-start.15 = (bf16[4,40,1024]{2,1,0:T(8,128)(2,1)}, bf16[4,40,1024]{2,1,0:T(8,128)(2,1)}, u32[]{:S(2)}, u32[]{:S(2)}) collective-permute-start(bf16[4,40,1024]{2,1,0:T(8,128)(2,1)} %pad_maximum_fusion.2), channel_id=1, source_target_pairs={{0,48},{16,0},{32,16},{48,32},{64,112},{80,64},{96,80},{112,96},{1... | collective-permute-start | bytes 983048 | tf_op jit(solution)/shard_map/ppermute | solution.py:154
  168.5 15.5 %collective-permute-start.13 = (bf16[4,40,1024]{2,1,0:T(8,128)(2,1)}, bf16[4,40,1024]{2,1,0:T(8,128)(2,1)}, u32[]{:S(2)}, u32[]{:S(2)}) collective-permute-start(bf16[4,40,1024]{2,1,0:T(8,128)(2,1)} %pad_maximum_fusion.1), channel_id=1, source_target_pairs={{0,16},{16,32},{32,48},{48,0},{64,80},{80,96},{96,112},{112,64},{1... | collective-permute-start | bytes 983048 | tf_op jit(solution)/shard_map/ppermute | solution.py:153
  178.8 14.5 %all-to-all-start.5 = ((bf16[4,40,1152]{2,1,0:T(8,128)(2,1)}), bf16[4,40,1152]{2,1,0:T(8,128)(2,1)S(1)}, u32[]{:S(2)}, u32[]{:S(2)}) async-start(bf16[4,40,1152]{2,1,0:T(8,128)(2,1)} %reduce_sum.208), calls=%async_computation.5 | async-start | bytes 737280 | tf_op jit(solution)/shard_map/all_to_all | solution.py:132
  185.9 5.7 %collective-permute-start.16 = (bf16[40,1024]{1,0:T(8,128)(2,1)S(1)}, bf16[40,1024]{1,0:T(8,128)(2,1)S(1)}, u32[]{:S(2)}, u32[]{:S(2)}) collective-permute-start(bf16[40,1024]{1,0:T(8,128)(2,1)S(1)} %get-tuple-element.140), channel_id=1, source_target_pairs={{0,64},{16,80},{32,96},{48,112},{64,128},{80,144},{96,160},{112,17... | collective-permute-start | bytes 245768 | tf_op jit(solution)/shard_map/ppermute | solution.py:162
  186.5 6.0 %collective-permute-start.17 = (bf16[40,1024]{1,0:T(8,128)(2,1)S(1)}, bf16[40,1024]{1,0:T(8,128)(2,1)S(1)}, u32[]{:S(2)}, u32[]{:S(2)}) collective-permute-start(bf16[40,1024]{1,0:T(8,128)(2,1)S(1)} %get-tuple-element.139), channel_id=1, source_target_pairs={{0,128},{16,144},{32,160},{48,176},{64,192},{80,208},{96,224},{112... | collective-permute-start | bytes 245768 | tf_op jit(solution)/shard_map/ppermute | solution.py:162
  196.0 29.0 %all-to-all-start.6 = ((bf16[8,40,384]{2,1,0:T(8,128)(2,1)}), bf16[8,40,384]{2,1,0:T(8,128)(2,1)S(1)}, u32[]{:S(2)}, u32[]{:S(2)}) async-start(bf16[8,40,384]{2,1,0:T(8,128)(2,1)} %sums.1), calls=%async_computation.6 | async-start | bytes 491520 | tf_op jit(solution)/shard_map/all_to_all | solution.py:76
  228.7 15.9 %all-to-all-start.7 = ((bf16[16,72,256]{2,1,0:T(8,128)(2,1)}), bf16[16,72,256]{2,1,0:T(8,128)(2,1)S(1)}, u32[]{:S(2)}, u32[]{:S(2)}) async-start(bf16[16,72,256]{2,1,0:T(8,128)(2,1)} %broadcast_in_dim.189), calls=%async_computation.7 | async-start | bytes 1179648 | tf_op jit(solution)/shard_map/all_to_all | solution.py:76
  247.1 19.7 %all-to-all-start.8 = ((bf16[8,128,128]{1,2,0:T(8,128)(2,1)}), bf16[8,128,128]{1,2,0:T(8,128)(2,1)S(1)}, u32[]{:S(2)}, u32[]{:S(2)}) async-start(bf16[8,128,128]{1,2,0:T(8,128)(2,1)} %broadcast_in_dim.190), calls=%async_computation.8 | async-start | bytes 524288 | tf_op jit(solution)/shard_map/all_to_all | solution.py:76
  (60 other events, 563.0 us)

commit v6 on v5

--- a/solution.py
+++ b/solution.py
@@ -229,26 +229,29 @@
         out_ref[:, block * feat : (block + 1) * feat] = term.astype(BF16)
 
 
-def back_add_kernel(
-    ctx_count, core, dg_ref, du_ref, wg_ref, wu_ref, other_ref, sc_ref, sc_other_ref,
-    low_ref, high_ref,
-):
+def back_add(dg_ref, du_ref, wg_ref, wu_ref, other_ref, out_ref):
     feat = wg_ref.shape[1]
-    width = wg_ref.shape[0] // 2 * feat
     for block in range(wg_ref.shape[0]):
         lanes = slice(block * feat, (block + 1) * feat)
         term = back_term(dg_ref, du_ref, wg_ref, wu_ref, block).astype(BF16).astype(F32)
-        both = (term + other_ref[:, lanes].astype(F32)).astype(BF16)
-        if block * feat < width:
-            low_ref[:, lanes] = both
-        else:
-            high_ref[:, block * feat - width : (block + 1) * feat - width] = both
+        out_ref[:, lanes] = (term + other_ref[:, lanes].astype(F32)).astype(BF16)
+
+
+def back_high_kernel(core, dg_ref, du_ref, wg_ref, wu_ref, other_ref, out_ref):
+    back_add(dg_ref, du_ref, wg_ref, wu_ref, other_ref, out_ref)
+
+
+def back_low_kernel(
+    ctx_count, core, dg_ref, du_ref, wg_ref, wu_ref, other_ref, sc_ref, sc_other_ref, out_ref
+):
+    back_add(dg_ref, du_ref, wg_ref, wu_ref, other_ref, out_ref)
     small = sc_ref[...] + sc_other_ref[...]
     lane = lax.broadcasted_iota(jnp.int32, small.shape, 1)
     small = jnp.where(lane == 2, small * (0.5 / ctx_count), small)
     head = small.astype(BF16).astype(F32)
     tail = pltpu.roll(small - head, 3, 1)
-    low_ref[:, width:] = jnp.where(lane < 3, head, jnp.where(lane < 6, tail, 0.0)).astype(BF16)
+    small = jnp.where(lane < 3, head, jnp.where(lane < 6, tail, 0.0))
+    out_ref[:, other_ref.shape[1] :] = small.astype(BF16)
 
 
 def scaled_grads_kernel(
@@ -446,31 +449,37 @@
         name="close",
     )(core, oth, gate_scaled, up_scaled, ag, au, ss, grad_act)
     scal_got = lax.ppermute(scal, "dp", other_core)
-    back_oth = pl.pallas_call(
-        back_kernel,
-        grid_spec=grid_of(1, split, [acts, acts, w_oth, w_oth], rows_spec),
-        out_shape=jax.ShapeDtypeStruct((rows_all, wide), BF16),
-        name="back_oth",
-    )(core, dg, du, gate4, up4)
-    back_got = lax.ppermute(back_oth, "dp", other_core)
     narrow = wide // 2
-    low, high = pl.pallas_call(
-        functools.partial(back_add_kernel, ctx_count),
+    half_rows = pl.BlockSpec((part, narrow), lambda i, *_: (i, 0))
+    half_shape = jax.ShapeDtypeStruct((rows_all, narrow), BF16)
+    half_w = (exp_count // 2, None, feat, units)
+    near = [pl.BlockSpec(half_w, lambda i, s, k=k: (k, s[0], 0, 0)) for k in range(2)]
+    far = [pl.BlockSpec(half_w, lambda i, s, k=k: (k, 1 - s[0], 0, 0)) for k in range(2)]
+    swapped = []
+    for k in range(2):
+        sent = pl.pallas_call(
+            back_kernel,
+            grid_spec=grid_of(1, split, [acts, acts, far[k], far[k]], half_rows),
+            out_shape=half_shape,
+        )(core, dg, du, gate4, up4)
+        swapped.append(lax.ppermute(sent, "dp", other_core))
+    low = pl.pallas_call(
+        functools.partial(back_low_kernel, ctx_count),
         grid_spec=grid_of(
             1,
             split,
-            [acts, acts, w_own, w_own, rows_spec, sums, sums],
-            [
-                pl.BlockSpec((part, narrow + 128), lambda i, *_: (i, 0)),
-                pl.BlockSpec((part, narrow), lambda i, *_: (i, 0)),
-            ],
+            [acts, acts, near[0], near[0], half_rows, sums, sums],
+            pl.BlockSpec((part, narrow + 128), lambda i, *_: (i, 0)),
         ),
-        out_shape=[
-            jax.ShapeDtypeStruct((rows_all, narrow + 128), BF16),
-            jax.ShapeDtypeStruct((rows_all, narrow), BF16),
-        ],
-        name="back_own",
-    )(core, dg, du, gate4, up4, back_got, scal, scal_got)
+        out_shape=jax.ShapeDtypeStruct((rows_all, narrow + 128), BF16),
+        name="own_low",
+    )(core, dg, du, gate4, up4, swapped[0], scal, scal_got)
+    high = pl.pallas_call(
+        back_high_kernel,
+        grid_spec=grid_of(1, split, [acts, acts, near[1], near[1], half_rows], half_rows),
+        out_shape=half_shape,
+        name="own_high",
+    )(core, dg, du, gate4, up4, swapped[1])
     columns = pl.BlockSpec((rows_all, feat), lambda e, *_: (0, e))
     gain_spec = pl.BlockSpec((None, 1, feat), lambda e, *_: (e, 0, 0))
     w_pair = pl.BlockSpec((None, 2, feat, units), lambda e, *_: (e, 0, 0, 0))

time: 271 us -> 266 us (0.982)
  waiting for transfers between devices: 75.3 us -> 64.3 us
  Pallas kernels: 44.6 us -> 48.8 us
    all_to_all x1, waiting for transfers between devices: 9.23 us -> 4.7 us  [sum_low(): lax.all_to_all(blocks, 'ctx', 0, 0, tiled=True, axis_index_groups=groups_y)]
    unnamed x126 -> x102, local copies, waits for them, and re-layouts: 9.13 us -> 4.76 us
    pallas_call x2 -> x4, Pallas kernels: 9.9 us -> 14 us  [the longest x2 6.68 us: per_device(): pl.pallas_call(back_kernel, grid_spec=grid_of(1, split, [acts, acts, far[...]
  transfers between devices with their start and end apart: 27 -> 28, of which waited for: 16 -> 15; matrix products, arithmetic and copies ran while one was open for 10% -> 12% of each run, Pallas kernels for 10% -> 14%
where the time goes in v6:
time: 266 us; the launch traced here: 263 us
  waiting for transfers between devices  64.3 us (24%)
  starting transfers between devices  63.9 us (24%)
  Pallas kernels  48.8 us (18%)
  blocking collectives  39.8 us (15%)
  local copies, waits for them, and re-layouts  19.2 us (7%)
  matrix products  13.3 us (5%)
  other arithmetic  11.5 us (4%)
    all_to_all x4, starting transfers between devices, swap(): return lax.all_to_all(x, axis, 0, 0, tiled=True)  31.7 us
    all_to_all x1, blocking collectives, swap(): return lax.all_to_all(x, axis, 0, 0, tiled=True)  20.9 us
    all_to_all x4, waiting for transfers between devices, swap(): return lax.all_to_all(x, axis, 0, 0, tiled=True)  20.6 us
    all_to_all x1, blocking collectives, gather_rows(): lax.all_to_all(block, 'ctx', 0, 0, tiled=True, axis_index_groups=groups_x)  18.9 us
    all_to_all x1, waiting for transfers between devices, gather_rows(): lax.all_to_all(row, 'ctx', 0, 0, tiled=True, axis_index_groups=groups_y)  17.4 us
    dot_general x37, matrix products, dot(): lax.dot_general(a, b, (dims, ((), ())), precision=precision, preferred_el...  13.3 us
    pallas_call x1, Pallas kernels, per_device(): pl.pallas_call(scaled_grads_kernel, grid_spec=grid_of(1, exp_count, [colu...  9.47 us
    pallas_call x1, Pallas kernels, per_device(): pl.pallas_call(plain_grads_kernel, grid_spec=grid_of(1, exp_count, [colum...  7.84 us
  transfers between devices with their start and end apart: 28, of which 15 were waited for; matrix products, arithmetic and copies ran while one was open for 12% of the time, Pallas kernels for 14%

profile of v6, /device:TPU:2, one launch (start us, length us, event | category | flops | bytes accessed | tf_op | source)
XLA Modules:
  0.0 262.7 jit_solution(5741531985036593649)
XLA Ops:
  4.3 7.5 %all-to-all-start = ((bf16[16,72,256]{2,1,0:T(8,128)(2,1)}), bf16[16,72,256]{2,1,0:T(8,128)(2,1)S(1)}, u32[]{:S(2)}, u32[]{:S(2)}) async-start(bf16[16,72,256]{2,1,0:T(8,128)(2,1)} %broadcast_in_dim.167), calls=%async_computation | async-start | bytes 1179648 | tf_op jit(solution)/shard_map/all_to_all | solution.py:76
  18.6 4.0 %all-to-all-done = bf16[16,72,256]{2,1,0:T(8,128)(2,1)S(1)} async-done(((bf16[16,72,256]{2,1,0:T(8,128)(2,1)}), bf16[16,72,256]{2,1,0:T(8,128)(2,1)S(1)}, u32[]{:S(2)}, u32[]{:S(2)}) %all-to-all-start) | async-done | bytes 589856 | tf_op jit(solution)/shard_map/all_to_all | solution.py:76
  24.7 20.9 %all_to_all.45 = bf16[8,88,256]{2,1,0:T(8,128)(2,1)S(1)} all-to-all(bf16[8,88,256]{2,1,0:T(8,128)(2,1)S(1)} %pad_maximum_fusion), channel_id=1, replica_groups=mesh['ctx'=16,'exp'=8,'dp'=2] {'exp'}, dimensions={0} | all-to-all | bytes 720896 | tf_op jit(solution)/shard_map/all_to_all | solution.py:76
  49.3 4.8 %collective-permute-done.2 = bf16[40,2048]{1,0:T(8,128)(2,1)S(1)} collective-permute-done((bf16[40,2048]{1,0:T(8,128)(2,1)S(1)}, bf16[40,2048]{1,0:T(8,128)(2,1)S(1)}, u32[]{:S(2)}, u32[]{:S(2)}) %collective-permute-start.2) | collective-permute-done | bytes 163872 | tf_op jit(solution)/shard_map/ppermute | solution.py:111
  57.2 18.9 %all_to_all.46 = bf16[4,40,2048]{2,1,0:T(8,128)(2,1)S(1)} all-to-all(bf16[4,40,2048]{2,1,0:T(8,128)(2,1)S(1)} %broadcast_in_dim.177), channel_id=1, replica_groups={{0,16,32,48},{64,80,96,112},{128,144,160,176},{192,208,224,240},{1,17,3..., dimensions={0} | all-to-all | bytes 1310720 | tf_op jit(solution)/shard_map/all_to_all | solution.py:102
  77.9 4.5 %all-to-all-start.3 = ((bf16[4,4,40,2048]{3,2,1,0:T(8,128)(2,1)}), bf16[4,4,40,2048]{3,2,1,0:T(8,128)(2,1)}, u32[]{:S(2)}, u32[]{:S(2)}) async-start(bf16[4,4,40,2048]{3,2,1,0:T(8,128)(2,1)} %broadcast_in_dim.178), calls=%async_computation.3 | async-start | bytes 5242880 | tf_op jit(solution)/shard_map/all_to_all | solution.py:104
  92.0 17.4 %all-to-all-done.3 = bf16[4,4,40,2048]{3,2,1,0:T(8,128)(2,1)} async-done(((bf16[4,4,40,2048]{3,2,1,0:T(8,128)(2,1)}), bf16[4,4,40,2048]{3,2,1,0:T(8,128)(2,1)}, u32[]{:S(2)}, u32[]{:S(2)}) %all-to-all-start.3) | async-done | bytes 2621472 | tf_op jit(solution)/shard_map/all_to_all | solution.py:104
  110.2 4.4 %collective-permute-done.1 = f32[8,256]{1,0:T(8,128)S(1)} collective-permute-done((f32[8,256]{1,0:T(8,128)S(1)}, f32[8,256]{1,0:T(8,128)S(1)}, u32[]{:S(2)}, u32[]{:S(2)}) %collective-permute-start.1) | collective-permute-done | bytes 8224 | tf_op jit(solution)/shard_map/ppermute | solution.py:389
  114.7 3.7 %multiply_convert_fusion = (bf16[8,2,256,256]{3,2,1,0:T(8,128)(2,1)}, bf16[8,2,256,256]{3,2,1,0:T(8,128)(2,1)}) fusion(bf16[8,2,256,256]{3,2,1,0:T(8,128)(2,1)S(1)} %bitcast.235, f32[8,2,256]{2,1,0:T(2,128)S(1)} %maximum_select_fusion, bf16[8,2,256,256]{3,2,1,0:T(8,128)(2,1)} %bitcast.236), kind=kLoop, calls=%fused_computation | loop fusion | flops 6291456 | bytes 8404992 | tf_op jit(solution)/shard_map/convert_element_type | solution.py:399
  118.5 4.7 %open.1 = (f32[640,256]{1,0:T(8,128)}, f32[640,256]{1,0:T(8,128)}, f32[640,128]{1,0:T(8,128)}) custom-call(s32[1]{0:T(128)} %bitcast.7.core, bf16[640,2048]{1,0:T(8,128)(2,1)} %bitcast.32.rows_ref.own_ref, bf16[8,2,256,256]{3,2,1,0:T(8,128)(2,1)} %get-tuple-element.141.wg_ref, bf16[8,2,256,256]{3,2,1,0:T(8,128)(2,1)} %get-tuple-element.140.wu_ref), custom_call_target="tpu_custom_call" | custom-call | tf_op jit(solution)/shard_map/open/pallas_call | solution.py:434
  123.2 4.8 %cot.1.ga_ref = f32[640,256]{1,0:T(8,128)} custom-call(s32[1]{0:T(128)} %bitcast.7.core, bf16[640,2048]{1,0:T(8,128)(2,1)} %bitcast.53.own_ref, bf16[640,2048]{1,0:T(8,128)(2,1)} %collective-permute-done.9.oth_ref, bf16[8,2,256,256]{3,2,1,0:T(8,128)(2,1)} %bitcast.241, bf16[8,2,256,256]{3,2,1,0:T(8,128)(2,1)} %bitcast.242), custom_call_target="tpu_custom_call" | custom-call | tf_op jit(solution)/shard_map/cot/pallas_call | solution.py:428
  128.0 6.0 %close.1 = (bf16[640,256]{1,0:T(8,128)(2,1)}, bf16[640,256]{1,0:T(8,128)(2,1)}, bf16[640,256]{1,0:T(8,128)(2,1)}, bf16[640,256]{1,0:T(8,128)(2,1)}, bf16[640,256]{1,0:T(8,128)(2,1)}, /*index=5*/f32[640,128]{1,0:T(8,128)}) custom-call(s32[1]{0:T(128)} %bitcast.7.core, bf16[640,2048]{1,0:T(8,128)(2,1)} %collective-permute-done.rows_ref.oth_ref, ...), custom_call_target="tpu_custom_call" | custom-call | tf_op jit(solution)/shard_map/close/pallas_call | solution.py:440
  146.2 3.8 %own_low.1 = bf16[640,1152]{1,0:T(8,128)(2,1)} custom-call(s32[1]{0:T(128)} %bitcast.7.core, bf16[640,256]{1,0:T(8,128)(2,1)} %get-tuple-element.24.dg_ref, bf16[640,256]{1,0:T(8,128)(2,1)} %get-tuple-element.25.du_ref, bf16[8,2,256,256]{3,2,1,0:T(8,128)(2,1)} %bitcast.239, bf16[8,2,256,256]{3,2,1,0:T(8,128)(2,1)} %bitcast.233, bf16[640,1024]{1,0:T(8,128)(2,1)} %copy-done.5, ...), custom_call_target="tpu_custom_call" | custom-call | tf_op jit(solution)/shard_map/own_low/pallas_call | solution.py:466
  153.6 3.6 %own_high.1 = bf16[640,1024]{1,0:T(8,128)(2,1)} custom-call(s32[1]{0:T(128)} %bitcast.7.core, bf16[640,256]{1,0:T(8,128)(2,1)} %get-tuple-element.24.dg_ref, bf16[640,256]{1,0:T(8,128)(2,1)} %get-tuple-element.25.du_ref, bf16[8,2,256,256]{3,2,1,0:T(8,128)(2,1)} %bitcast.240, bf16[8,2,256,256]{3,2,1,0:T(8,128)(2,1)} %bitcast.234, ...), custom_call_target="tpu_custom_call" | custom-call | tf_op jit(solution)/shard_map/own_high/pallas_call | solution.py:477
  160.5 4.5 %collective-permute-done.13 = bf16[2,40,1024]{2,1,0:T(8,128)(2,1)S(1)} collective-permute-done((bf16[2,40,1024]{2,1,0:T(8,128)(2,1)S(1)}, bf16[2,40,1024]{2,1,0:T(8,128)(2,1)S(1)}, u32[]{:S(2)}, u32[]{:S(2)}) %collective-permute-start.13) | collective-permute-done | bytes 163872 | tf_op jit(solution)/shard_map/ppermute | solution.py:149
  169.3 4.7 %all-to-all-done.4 = bf16[4,4,40,1152]{3,2,1,0:T(8,128)(2,1)S(1)} async-done(((bf16[4,4,40,1152]{3,2,1,0:T(8,128)(2,1)}), bf16[4,4,40,1152]{3,2,1,0:T(8,128)(2,1)S(1)}, u32[]{:S(2)}, u32[]{:S(2)}) %all-to-all-start.4) | async-done | bytes 1474592 | tf_op jit(solution)/shard_map/all_to_all | solution.py:130
  175.1 5.2 %all-to-all-start.5 = ((bf16[4,40,1152]{2,1,0:T(8,128)(2,1)}), bf16[4,40,1152]{2,1,0:T(8,128)(2,1)S(1)}, u32[]{:S(2)}, u32[]{:S(2)}) async-start(bf16[4,40,1152]{2,1,0:T(8,128)(2,1)} %reduce_sum.208), calls=%async_computation.5 | async-start | bytes 737280 | tf_op jit(solution)/shard_map/all_to_all | solution.py:132
  192.3 9.7 %all-to-all-start.6 = ((bf16[8,40,384]{2,1,0:T(8,128)(2,1)}), bf16[8,40,384]{2,1,0:T(8,128)(2,1)S(1)}, u32[]{:S(2)}, u32[]{:S(2)}) async-start(bf16[8,40,384]{2,1,0:T(8,128)(2,1)} %sums.1), calls=%async_computation.6 | async-start | bytes 491520 | tf_op jit(solution)/shard_map/all_to_all | solution.py:76
  202.3 7.8 %down_grads.1 = bf16[8,2,256,256]{3,2,1,0:T(8,128)(2,1)} custom-call(s32[1]{0:T(128)} %bitcast.7.core, bf16[640,2048]{1,0:T(8,128)(2,1)} %bitcast.53.own_ref, bf16[640,2048]{1,0:T(8,128)(2,1)} %collective-permute-done.9.oth_ref, bf16[640,256]{1,0:T(8,128)(2,1)} %get-tuple-element.31.act_ref), custom_call_target="tpu_custom_call" | custom-call | tf_op jit(solution)/shard_map/down_grads/pallas_call | solution.py:500
  210.2 9.5 %gate_grads.1 = (bf16[8,2,256,256]{3,2,1,0:T(8,128)(2,1)}, bf16[8,2,256,256]{3,2,1,0:T(8,128)(2,1)}) custom-call(s32[1]{0:T(128)} %bitcast.7.core, bf16[640,2048]{1,0:T(8,128)(2,1)} %bitcast.32.rows_ref.own_ref, bf16[640,2048]{1,0:T(8,128)(2,1)} %collective-permute-done.rows_ref.oth_ref, f32[8,1,256]{2,1,0:T(1,128)} %copy-done.19, f32[8,1,256]{2,1,0:T(1,128)} %copy-done.20, ...), custom_call_target="tpu_custom_call" | custom-call | tf_op jit(solution)/shard_map/gate_grads/pallas_call | solution.py:489
  223.4 7.3 %all-to-all-start.7 = ((bf16[16,72,256]{2,1,0:T(8,128)(2,1)}), bf16[16,72,256]{2,1,0:T(8,128)(2,1)S(1)}, u32[]{:S(2)}, u32[]{:S(2)}) async-start(bf16[16,72,256]{2,1,0:T(8,128)(2,1)} %broadcast_in_dim.189), calls=%async_computation.7 | async-start | bytes 1179648 | tf_op jit(solution)/shard_map/all_to_all | solution.py:76
  234.2 5.7 %all-to-all-done.7 = bf16[16,72,256]{2,1,0:T(8,128)(2,1)S(1)} async-done(((bf16[16,72,256]{2,1,0:T(8,128)(2,1)}), bf16[16,72,256]{2,1,0:T(8,128)(2,1)S(1)}, u32[]{:S(2)}, u32[]{:S(2)}) %all-to-all-start.7) | async-done | bytes 589856 | tf_op jit(solution)/shard_map/all_to_all | solution.py:76
  242.4 7.2 %all-to-all-start.8 = ((bf16[8,128,128]{1,2,0:T(8,128)(2,1)}), bf16[8,128,128]{1,2,0:T(8,128)(2,1)S(1)}, u32[]{:S(2)}, u32[]{:S(2)}) async-start(bf16[8,128,128]{1,2,0:T(8,128)(2,1)} %broadcast_in_dim.190), calls=%async_computation.8 | async-start | bytes 524288 | tf_op jit(solution)/shard_map/all_to_all | solution.py:76
  251.2 10.9 %all-to-all-done.8 = bf16[8,128,128]{1,2,0:T(8,128)(2,1)S(1)} async-done(((bf16[8,128,128]{1,2,0:T(8,128)(2,1)}), bf16[8,128,128]{1,2,0:T(8,128)(2,1)S(1)}, u32[]{:S(2)}, u32[]{:S(2)}) %all-to-all-start.8) | async-done | bytes 262176 | tf_op jit(solution)/shard_map/all_to_all | solution.py:76
  (260 shorter events, 79.3 us)
Async XLA Ops:
  4.3 18.4 %all-to-all-start = ((bf16[16,72,256]{2,1,0:T(8,128)(2,1)}), bf16[16,72,256]{2,1,0:T(8,128)(2,1)S(1)}, u32[]{:S(2)}, u32[]{:S(2)}) async-start(bf16[16,72,256]{2,1,0:T(8,128)(2,1)} %broadcast_in_dim.167), calls=%async_computation | async-start | bytes 1179648 | tf_op jit(solution)/shard_map/all_to_all | solution.py:76
  45.7 8.4 %collective-permute-start.2 = (bf16[40,2048]{1,0:T(8,128)(2,1)S(1)}, bf16[40,2048]{1,0:T(8,128)(2,1)S(1)}, u32[]{:S(2)}, u32[]{:S(2)}) collective-permute-start(bf16[40,2048]{1,0:T(8,128)(2,1)S(1)} %get-tuple-element.118), channel_id=1, source_target_pairs={{0,64},{16,80},{32,96},{48,112},{64,128},{80,144},{96,160},{112,17... | collective-permute-start | bytes 491528 | tf_op jit(solution)/shard_map/ppermute | solution.py:111
  45.9 8.3 %collective-permute-start.3 = (bf16[40,2048]{1,0:T(8,128)(2,1)S(1)}, bf16[40,2048]{1,0:T(8,128)(2,1)S(1)}, u32[]{:S(2)}, u32[]{:S(2)}) collective-permute-start(bf16[40,2048]{1,0:T(8,128)(2,1)S(1)} %get-tuple-element.118), channel_id=1, source_target_pairs={{0,128},{16,144},{32,160},{48,176},{64,192},{80,208},{96,224},{112... | collective-permute-start | bytes 491528 | tf_op jit(solution)/shard_map/ppermute | solution.py:111
  48.1 6.9 %collective-permute-start.4 = (bf16[40,2048]{1,0:T(8,128)(2,1)S(1)}, bf16[40,2048]{1,0:T(8,128)(2,1)S(1)}, u32[]{:S(2)}, u32[]{:S(2)}) collective-permute-start(bf16[40,2048]{1,0:T(8,128)(2,1)S(1)} %get-tuple-element.118), channel_id=1, source_target_pairs={{0,192},{16,208},{32,224},{48,240},{64,0},{80,16},{96,32},{112,48}... | collective-permute-start | bytes 491528 | tf_op jit(solution)/shard_map/ppermute | solution.py:111
  55.0 27.6 %collective-permute-start.5 = (bf16[4,40,2048]{2,1,0:T(8,128)(2,1)S(1)}, bf16[4,40,2048]{2,1,0:T(8,128)(2,1)S(1)}, u32[]{:S(2)}, u32[]{:S(2)}) collective-permute-start(bf16[4,40,2048]{2,1,0:T(8,128)(2,1)S(1)} %bitcast_dynamic-update-slice_fusion.4), channel_id=1, source_target_pairs={{0,16},{16,32},{32,48},{48,0},{64,80},{80,96},{96,112},{112,64},{1... | collective-permute-start | bytes 1966088 | tf_op jit(solution)/shard_map/ppermute | solution.py:115
  56.0 26.9 %collective-permute-start.6 = (bf16[4,40,2048]{2,1,0:T(8,128)(2,1)S(1)}, bf16[4,40,2048]{2,1,0:T(8,128)(2,1)S(1)}, u32[]{:S(2)}, u32[]{:S(2)}) collective-permute-start(bf16[4,40,2048]{2,1,0:T(8,128)(2,1)S(1)} %bitcast_dynamic-update-slice_fusion.4), channel_id=1, source_target_pairs={{0,48},{16,0},{32,16},{48,32},{64,112},{80,64},{96,80},{112,96},{1... | collective-permute-start | bytes 1966088 | tf_op jit(solution)/shard_map/ppermute | solution.py:116
  77.9 31.5 %all-to-all-start.3 = ((bf16[4,4,40,2048]{3,2,1,0:T(8,128)(2,1)}), bf16[4,4,40,2048]{3,2,1,0:T(8,128)(2,1)}, u32[]{:S(2)}, u32[]{:S(2)}) async-start(bf16[4,4,40,2048]{3,2,1,0:T(8,128)(2,1)} %broadcast_in_dim.178), calls=%async_computation.3 | async-start | bytes 5242880 | tf_op jit(solution)/shard_map/all_to_all | solution.py:104
  82.6 7.2 %collective-permute-start.7 = (bf16[2,40,2048]{2,1,0:T(8,128)(2,1)S(1)}, bf16[2,40,2048]{2,1,0:T(8,128)(2,1)S(1)}, u32[]{:S(2)}, u32[]{:S(2)}) collective-permute-start(bf16[2,40,2048]{2,1,0:T(8,128)(2,1)S(1)} %slice.241), channel_id=1, source_target_pairs={{0,16},{16,32},{32,48},{48,0},{64,80},{80,96},{96,112},{112,64},{1... | collective-permute-start | bytes 983048 | tf_op jit(solution)/shard_map/ppermute | solution.py:118
  83.0 8.2 %collective-permute-start.8 = (bf16[2,40,2048]{2,1,0:T(8,128)(2,1)S(1)}, bf16[2,40,2048]{2,1,0:T(8,128)(2,1)S(1)}, u32[]{:S(2)}, u32[]{:S(2)}) collective-permute-start(bf16[2,40,2048]{2,1,0:T(8,128)(2,1)S(1)} %slice.242), channel_id=1, source_target_pairs={{0,48},{16,0},{32,16},{48,32},{64,112},{80,64},{96,80},{112,96},{1... | collective-permute-start | bytes 983048 | tf_op jit(solution)/shard_map/ppermute | solution.py:119
  92.0 31.2 %collective-permute-start.9 = (bf16[640,2048]{1,0:T(8,128)(2,1)}, bf16[640,2048]{1,0:T(8,128)(2,1)}, u32[]{:S(2)}, u32[]{:S(2)}) collective-permute-start(bf16[640,2048]{1,0:T(8,128)(2,1)} %bitcast.53.own_ref), channel_id=1, source_target_pairs={{0,1},{1,0},{2,3},{3,2},{4,5},{5,4},{6,7},{7,6},{8,9},{9,8},{10,11... | collective-permute-start | bytes 7864328 | tf_op jit(solution)/shard_map/ppermute | solution.py:407
  109.4 18.6 %collective-permute-start = (bf16[640,2048]{1,0:T(8,128)(2,1)}, bf16[640,2048]{1,0:T(8,128)(2,1)}, u32[]{:S(2)}, u32[]{:S(2)}) collective-permute-start(bf16[640,2048]{1,0:T(8,128)(2,1)} %bitcast.32.rows_ref.own_ref), channel_id=1, source_target_pairs={{0,1},{1,0},{2,3},{3,2},{4,5},{5,4},{6,7},{7,6},{8,9},{9,8},{10,11... | collective-permute-start | bytes 7864328 | tf_op jit(solution)/shard_map/ppermute | solution.py:406
  137.3 7.2 %collective-permute-start.10 = (bf16[640,1024]{1,0:T(8,128)(2,1)}, bf16[640,1024]{1,0:T(8,128)(2,1)S(1)}, u32[]{:S(2)}, u32[]{:S(2)}) collective-permute-start(bf16[640,1024]{1,0:T(8,128)(2,1)} %shard_map.195), channel_id=1, source_target_pairs={{0,1},{1,0},{2,3},{3,2},{4,5},{5,4},{6,7},{7,6},{8,9},{9,8},{10,11... | collective-permute-start | bytes 3932168 | tf_op jit(solution)/shard_map/ppermute | solution.py:465
  140.8 12.8 %collective-permute-start.12 = (bf16[640,1024]{1,0:T(8,128)(2,1)}, bf16[640,1024]{1,0:T(8,128)(2,1)}, u32[]{:S(2)}, u32[]{:S(2)}) collective-permute-start(bf16[640,1024]{1,0:T(8,128)(2,1)} %shard_map.196), channel_id=1, source_target_pairs={{0,1},{1,0},{2,3},{3,2},{4,5},{5,4},{6,7},{7,6},{8,9},{9,8},{10,11... | collective-permute-start | bytes 3932168 | tf_op jit(solution)/shard_map/ppermute | solution.py:465
  150.0 24.0 %all-to-all-start.4 = ((bf16[4,4,40,1152]{3,2,1,0:T(8,128)(2,1)}), bf16[4,4,40,1152]{3,2,1,0:T(8,128)(2,1)S(1)}, u32[]{:S(2)}, u32[]{:S(2)}) async-start(bf16[4,4,40,1152]{3,2,1,0:T(8,128)(2,1)} %bitcast.243), calls=%async_computation.4 | async-start | bytes 2949120 | tf_op jit(solution)/shard_map/all_to_all | solution.py:130
  158.4 6.6 %collective-permute-start.13 = (bf16[2,40,1024]{2,1,0:T(8,128)(2,1)S(1)}, bf16[2,40,1024]{2,1,0:T(8,128)(2,1)S(1)}, u32[]{:S(2)}, u32[]{:S(2)}) collective-permute-start(bf16[2,40,1024]{2,1,0:T(8,128)(2,1)S(1)} %get-tuple-element.114), channel_id=1, source_target_pairs={{0,16},{16,32},{32,48},{48,0},{64,80},{80,96},{96,112},{112,64},{1... | collective-permute-start | bytes 491528 | tf_op jit(solution)/shard_map/ppermute | solution.py:149
  158.6 6.7 %collective-permute-start.15 = (bf16[2,40,1024]{2,1,0:T(8,128)(2,1)S(1)}, bf16[2,40,1024]{2,1,0:T(8,128)(2,1)S(1)}, u32[]{:S(2)}, u32[]{:S(2)}) collective-permute-start(bf16[2,40,1024]{2,1,0:T(8,128)(2,1)S(1)} %get-tuple-element.117), channel_id=1, source_target_pairs={{0,48},{16,0},{32,16},{48,32},{64,112},{80,64},{96,80},{112,96},{1... | collective-permute-start | bytes 491528 | tf_op jit(solution)/shard_map/ppermute | solution.py:150
  166.4 13.9 %collective-permute-start.16 = (bf16[4,40,1024]{2,1,0:T(8,128)(2,1)S(1)}, bf16[4,40,1024]{2,1,0:T(8,128)(2,1)}, u32[]{:S(2)}, u32[]{:S(2)}) collective-permute-start(bf16[4,40,1024]{2,1,0:T(8,128)(2,1)S(1)} %pad_maximum_fusion.2), channel_id=1, source_target_pairs={{0,48},{16,0},{32,16},{48,32},{64,112},{80,64},{96,80},{112,96},{1... | collective-permute-start | bytes 983048 | tf_op jit(solution)/shard_map/ppermute | solution.py:154
  169.1 11.1 %collective-permute-start.14 = (bf16[4,40,1024]{2,1,0:T(8,128)(2,1)S(1)}, bf16[4,40,1024]{2,1,0:T(8,128)(2,1)S(1)}, u32[]{:S(2)}, u32[]{:S(2)}) collective-permute-start(bf16[4,40,1024]{2,1,0:T(8,128)(2,1)S(1)} %pad_maximum_fusion.1), channel_id=1, source_target_pairs={{0,16},{16,32},{32,48},{48,0},{64,80},{80,96},{96,112},{112,64},{1... | collective-permute-start | bytes 983048 | tf_op jit(solution)/shard_map/ppermute | solution.py:153
  175.1 14.5 %all-to-all-start.5 = ((bf16[4,40,1152]{2,1,0:T(8,128)(2,1)}), bf16[4,40,1152]{2,1,0:T(8,128)(2,1)S(1)}, u32[]{:S(2)}, u32[]{:S(2)}) async-start(bf16[4,40,1152]{2,1,0:T(8,128)(2,1)} %reduce_sum.208), calls=%async_computation.5 | async-start | bytes 737280 | tf_op jit(solution)/shard_map/all_to_all | solution.py:132
  182.2 6.6 %collective-permute-start.17 = (bf16[40,1024]{1,0:T(8,128)(2,1)S(1)}, bf16[40,1024]{1,0:T(8,128)(2,1)S(1)}, u32[]{:S(2)}, u32[]{:S(2)}) collective-permute-start(bf16[40,1024]{1,0:T(8,128)(2,1)S(1)} %get-tuple-element.136), channel_id=1, source_target_pairs={{0,64},{16,80},{32,96},{48,112},{64,128},{80,144},{96,160},{112,17... | collective-permute-start | bytes 245768 | tf_op jit(solution)/shard_map/ppermute | solution.py:162
  182.7 6.0 %collective-permute-start.18 = (bf16[40,1024]{1,0:T(8,128)(2,1)S(1)}, bf16[40,1024]{1,0:T(8,128)(2,1)S(1)}, u32[]{:S(2)}, u32[]{:S(2)}) collective-permute-start(bf16[40,1024]{1,0:T(8,128)(2,1)S(1)} %get-tuple-element.135), channel_id=1, source_target_pairs={{0,128},{16,144},{32,160},{48,176},{64,192},{80,208},{96,224},{112... | collective-permute-start | bytes 245768 | tf_op jit(solution)/shard_map/ppermute | solution.py:162
  192.3 27.5 %all-to-all-start.6 = ((bf16[8,40,384]{2,1,0:T(8,128)(2,1)}), bf16[8,40,384]{2,1,0:T(8,128)(2,1)S(1)}, u32[]{:S(2)}, u32[]{:S(2)}) async-start(bf16[8,40,384]{2,1,0:T(8,128)(2,1)} %sums.1), calls=%async_computation.6 | async-start | bytes 491520 | tf_op jit(solution)/shard_map/all_to_all | solution.py:76
  223.4 16.4 %all-to-all-start.7 = ((bf16[16,72,256]{2,1,0:T(8,128)(2,1)}), bf16[16,72,256]{2,1,0:T(8,128)(2,1)S(1)}, u32[]{:S(2)}, u32[]{:S(2)}) async-start(bf16[16,72,256]{2,1,0:T(8,128)(2,1)} %broadcast_in_dim.189), calls=%async_computation.7 | async-start | bytes 1179648 | tf_op jit(solution)/shard_map/all_to_all | solution.py:76
  242.4 19.7 %all-to-all-start.8 = ((bf16[8,128,128]{1,2,0:T(8,128)(2,1)}), bf16[8,128,128]{1,2,0:T(8,128)(2,1)S(1)}, u32[]{:S(2)}, u32[]{:S(2)}) async-start(bf16[8,128,128]{1,2,0:T(8,128)(2,1)} %broadcast_in_dim.190), calls=%async_computation.8 | async-start | bytes 524288 | tf_op jit(solution)/shard_map/all_to_all | solution.py:76
  (49 other events, 492.2 us)
